TPU v7x, 32 devices: a whole 2x2x4 slice. The times are simulated.
32 devices in a mesh: tm: 8 (over z, y), rows: 4 (over x, core).
Axes of the slice: x: 2, y: 2, z: 4, core: 2. Of those that a mesh axis runs over, the one named last changes fastest.
Arguments:
- phases: bfloat16 [16, 512, 512], P('tm', 'rows'), may hold values from -6 to 6
- focal_data: bfloat16 [16, 2, 256, 256], P('tm', None, 'rows'), may hold values from -6 to 6
- shifts: int32 [16, 2], P('tm'), may hold values from 0 to 2, as said below
- pupil_mask: int32 [512, 512], P('rows'), may hold values 0 or 1
Outputs:
- adjoint_field: float32 [16, 512, 512], P('tm', 'rows')
- wind_grad: float32 [2], replicated
Inputs may be any that keep to these rules, and one draw needn't show every extreme that they name: `shifts`: column 0 is a frame's shift along pupil rows, 0 or 1, and sums over all frames to exactly 8; column 1 is its shift along pupil columns, 0 to 2.
All inputs are finite; a program needn't handle non-finite values. No bound on the sum of `pupil_mask` on one device may be relied on, other than what follows from the above.
Results may differ from a plain program's by a relative error of at most 0.0054.
Values may be sent and summed in bfloat16 or wider, within the bound.
No kernel may reach another device: no remote copies, remote signals or barrier semaphores. Data moves between devices by JAX's collectives and lax.ppermute only.
A program may use at most 128 MiB of HBM per device.

v0:
```python
import math

import jax
import jax.numpy as jnp
from jax import lax
from jax.sharding import PartitionSpec as P

PUPIL = 512
FOCAL = 256


decay_rate = 0.999


def from_behind(value, axis, steps):
    count = lax.axis_size(axis)
    first, last = (max(0, -steps), min(count, count - steps))
    return lax.ppermute(value, axis, [(source, source + steps) for source in range(first, last)])


def carried_in(part, axis, combine, identity):
    count = lax.axis_size(axis)
    place = lax.axis_index(axis)
    ahead = count - 1 - place
    gathered = jax.tree.map(lambda a: lax.all_gather(a, axis), part)
    state = jax.tree.map(lambda a, e: jnp.zeros_like(a) + jnp.asarray(e, a.dtype), part, identity)

    def one(step, state):
        source = count - 1 - step
        return combine(
            state, jax.tree.map(lambda a: lax.dynamic_index_in_dim(a, source, 0, False), gathered)
        )

    return lax.fori_loop(0, ahead, one, state)


def tables(row_total):
    focal_pos = jnp.arange(FOCAL, dtype=jnp.int32) - FOCAL // 2
    pupil_pos = jnp.arange(row_total, dtype=jnp.int32) - PUPIL // 2
    turns = jnp.mod(focal_pos[:, None] * pupil_pos[None, :], 2 * PUPIL)
    angle = turns.astype(jnp.float32) * (math.pi / PUPIL)
    factor = 1.0 / math.sqrt(PUPIL)
    return (
        (jnp.cos(angle) * factor).astype(jnp.bfloat16),
        (-jnp.sin(angle) * factor).astype(jnp.bfloat16),
    )


def shift_back(field_in, shift_rows, shift_cols, pad_rows):
    cols_total = field_in.shape[1]
    padded = jnp.pad(field_in, ((0, pad_rows), (0, 0)))
    start_row = jnp.minimum(shift_rows, pad_rows).astype(jnp.int32)
    moved = lax.dynamic_slice(padded, (start_row, jnp.zeros((), jnp.int32)), field_in.shape)
    start_col = jnp.minimum(shift_cols, cols_total).astype(jnp.int32)
    rolled = jnp.roll(moved, -start_col, axis=1)
    keep = jnp.arange(cols_total, dtype=jnp.int32) < cols_total - start_col
    return jnp.where(keep[None, :], rolled, jnp.zeros_like(rolled))


def adjoint_rows(cos_part, sin_part, resid, cos_full, sin_full, live):
    real_part = resid[:, 0]
    imag_part = resid[:, 1]
    w_real = (
        jnp.einsum("qn,kqs->kns", cos_part, real_part, preferred_element_type=jnp.float32)
        + jnp.einsum("qn,kqs->kns", sin_part, imag_part, preferred_element_type=jnp.float32)
    ).astype(jnp.bfloat16)
    w_imag = (
        jnp.einsum("qn,kqs->kns", cos_part, imag_part, preferred_element_type=jnp.float32)
        - jnp.einsum("qn,kqs->kns", sin_part, real_part, preferred_element_type=jnp.float32)
    ).astype(jnp.bfloat16)
    summed = jnp.einsum(
        "kns,sp->knp", w_real, cos_full, preferred_element_type=jnp.float32
    ) + jnp.einsum("kns,sp->knp", w_imag, sin_full, preferred_element_type=jnp.float32)
    return jnp.where(live[None], summed, jnp.zeros_like(summed))


def on_device(phases, focal_data, shifts, pupil_mask):
    frame_count = phases.shape[0]
    block = phases.shape[1]
    width = phases.shape[2]
    halo_rows = width // (4 * lax.axis_size("rows"))
    window = block + halo_rows
    frames_all = frame_count * lax.axis_size("tm")
    row_start = lax.axis_index("rows") * block
    cos_t, sin_t = tables(width)
    cos_rows = lax.dynamic_slice_in_dim(cos_t, row_start, block, 1)
    sin_rows = lax.dynamic_slice_in_dim(sin_t, row_start, block, 1)
    live = pupil_mask == 1
    masked = jnp.where(live[None], phases, jnp.zeros_like(phases))
    y_real = jnp.einsum("kbp,qp->kbq", masked, cos_t, preferred_element_type=jnp.float32).astype(
        jnp.bfloat16
    )
    y_imag = jnp.einsum("kbp,qp->kbq", masked, sin_t, preferred_element_type=jnp.float32).astype(
        jnp.bfloat16
    )
    e_real = jnp.einsum(
        "qb,kbs->kqs", cos_rows, y_real, preferred_element_type=jnp.float32
    ) - jnp.einsum("qb,kbs->kqs", sin_rows, y_imag, preferred_element_type=jnp.float32)
    e_imag = jnp.einsum(
        "qb,kbs->kqs", cos_rows, y_imag, preferred_element_type=jnp.float32
    ) + jnp.einsum("qb,kbs->kqs", sin_rows, y_real, preferred_element_type=jnp.float32)
    partial_field = jnp.stack([e_real, e_imag], axis=1)
    placed = lax.dynamic_update_slice_in_dim(
        jnp.zeros_like(partial_field),
        focal_data.astype(jnp.float32),
        lax.axis_index("rows") * focal_data.shape[2],
        2,
    )
    total = lax.psum(partial_field - placed, "rows")
    resid = (-total).astype(jnp.bfloat16)
    grad = adjoint_rows(cos_rows, sin_rows, resid, cos_t, sin_t, live)
    outgoing = jnp.concatenate([grad[:, :halo_rows], phases[:, :1].astype(jnp.float32)], axis=1)
    incoming = from_behind(outgoing, "rows", -1)
    grad_window = jnp.concatenate([grad, incoming[:, :halo_rows]], axis=1)
    next_phase = incoming[:, halo_rows]
    lam_next = jnp.zeros((window, width), jnp.float32)
    local_lams = [lam_next] * frame_count
    for frame in reversed(range(frame_count)):
        lam_next = grad_window[frame] + decay_rate * shift_back(
            lam_next, shifts[frame, 0], shifts[frame, 1], halo_rows
        )
        local_lams[frame] = lam_next

    def compose(earlier, later):
        field_late, rows_late, cols_late = earlier
        field_early, rows_early, cols_early = later
        moved = shift_back(field_late, rows_early, cols_early, halo_rows)
        return (field_early + moved, rows_early + rows_late, cols_early + cols_late)

    time_index = lax.axis_index("tm").astype(jnp.float32)
    frames_float = jnp.float32(frame_count)
    start_weight = jnp.power(jnp.float32(decay_rate), time_index * frames_float)
    after_weight = jnp.power(jnp.float32(decay_rate), (time_index + 1.0) * frames_float)
    segment = (start_weight * local_lams[0], jnp.sum(shifts[:, 0]), jnp.sum(shifts[:, 1]))
    identity = (
        jnp.zeros((window, width), jnp.float32),
        jnp.zeros((), jnp.int32),
        jnp.zeros((), jnp.int32),
    )
    carried = carried_in(segment, "tm", compose, identity)
    carry_field = carried[0] / after_weight
    cum_rows = jnp.zeros((), jnp.int32)
    cum_cols = jnp.zeros((), jnp.int32)
    factor_now = 1.0
    results = [None] * frame_count
    wind_terms = jnp.zeros((2,), jnp.float32)
    for frame in reversed(range(frame_count)):
        cum_rows = cum_rows + shifts[frame, 0]
        cum_cols = cum_cols + shifts[frame, 1]
        factor_now = factor_now * decay_rate
        lam_now = (
            local_lams[frame][:block]
            + factor_now * shift_back(carry_field, cum_rows, cum_cols, halo_rows)[:block]
        )
        results[frame] = lam_now
        prior = lam_now - grad[frame]
        phase_wide = phases[frame].astype(jnp.float32)
        down_diff = jnp.concatenate([phase_wide[1:], next_phase[frame][None]], axis=0) - phase_wide
        side_diff = (
            jnp.concatenate([phase_wide[:, 1:], jnp.zeros((block, 1), jnp.float32)], axis=1)
            - phase_wide
        )
        wind_terms = wind_terms + jnp.stack(
            [jnp.sum(prior * down_diff), jnp.sum(prior * side_diff)]
        )
    wind_total = lax.psum(wind_terms, ("tm", "rows"))
    wind_grad = -wind_total / (width * frames_all)
    return (jnp.stack(results), wind_grad)


def solution(mesh):
    in_specs = (P("tm", "rows", None), P("tm", None, "rows", None), P("tm", None), P("rows", None))
    out_specs = (P("tm", "rows", None), P())
    return jax.shard_map(
        on_device, mesh=mesh, in_specs=in_specs, out_specs=out_specs, check_vma=False
    )
```

profile of v0, /device:TPU:0, one launch (start us, length us, event | category | flops | bytes accessed | tf_op | source)
XLA Modules:
  0.0 204.4 jit_solution(5280239042535664271)
XLA Ops:
  7.2 0.0 all-reduce.11.cloned.1.call-start
  7.2 1.0 broadcast_compare_fusion
  8.2 2.5 %multiply_convert_fusion = (bf16[256,512]{1,0:T(8,128)(2,1)S(1)}, bf16[256,512]{1,0:T(8,128)(2,1)S(1)}) fusion(s32[512]{0:T(512)S(1)} %iota_add_fusion, s32[256]{0:T(256)S(1)} %iota_add_fusion.1), kind=kLoop, calls=%fused_computation.43 | loop fusion | flops 2490368 | bytes 527360 | tf_op jit(solution)/shard_map/convert_element_type | solution.py:45
  10.7 3.3 %convolution_convert_fusion = bf16[2,128,256]{2,1,0:T(8,128)(2,1)S(1)} fusion(bf16[2,128,512]{2,1,0:T(8,128)(2,1)} %param.8, pred[128,512]{1,0:T(8,128)(4,1)S(1)} %broadcast_compare_fusion, s32[512]{0:T(512)S(1)} %iota_add_fusion, s32[256]{0:T(256)S(1)} %iota_add_fusion.1), kind=kOutput, calls=%fused_computation.17 | convolution fusion | flops 69533696 | bytes 461824 | tf_op jit(solution)/shard_map/kbp,qp->kbq/dot_general | solution.py:93
  14.0 2.2 %convolution_convert_fusion.1 = bf16[2,128,256]{2,1,0:T(8,128)(2,1)S(1)} fusion(bf16[2,128,512]{2,1,0:T(8,128)(2,1)S(1)} %copy-done, pred[128,512]{1,0:T(8,128)(4,1)S(1)} %broadcast_compare_fusion, s32[512]{0:T(512)S(1)} %iota_add_fusion, s32[256]{0:T(256)S(1)} %iota_add_fusion.1), kind=kOutput, calls=%fused_computation.18 | convolution fusion | flops 69402624 | bytes 461824 | tf_op jit(solution)/shard_map/kbp,qp->kbq/dot_general | solution.py:90
  16.2 0.2 fusion.55
  16.5 0.3 fusion.57
  16.7 0.3 fusion.3
  17.0 0.3 fusion.4
  17.3 0.1 copy.15
  17.4 0.1 broadcast_in_dim.73
  17.5 2.3 %dynamic_update_slice.3 = f32[2,2,256,256]{2,3,0,1:T(8,128)S(1)} dynamic-update-slice(f32[2,2,256,256]{2,3,0,1:T(8,128)S(1)} %broadcast_in_dim.73, f32[2,2,64,256]{2,3,0,1:T(8,128)S(1)} %copy.15, s32[]{:T(128)} %copy.49, s32[]{:T(128)} %copy.49, s32[]{:T(128)S(6)} %select_n.123, s32[]{:T(128)} %copy.49) | dynamic-update-slice | bytes 524292 | tf_op jit(solution)/shard_map/dynamic_update_slice | solution.py:103
  19.8 1.2 maximum_subtract_fusion
  20.9 0.0 all-reduce.11.cloned.1.call-update
  21.0 0.0 all-gather.3.cloned.1.call-start
  21.0 0.6 fusion.104
  24.1 35.6 %all-reduce.11.cloned.1.call-done = f32[2,2,256,256]{2,3,0,1:T(8,128)} async-done(((f32[2,2,256,256]{2,3,0,1:T(8,128)}), f32[2,2,256,256]{2,3,0,1:T(8,128)}) %all-reduce.11.cloned.1.call-update) | async-done | bytes 1048592 | tf_op jit(solution)/shard_map/psum | solution.py:109
  59.7 1.3 negate_convert_fusion
  61.1 0.2 fusion.43
  61.3 0.2 fusion.44
  61.5 2.2 %fusion.10 = f32[2,128,512]{2,1,0:T(8,128)S(1)} fusion(f32[2,256,128]{1,2,0:T(8,128)S(1)} %fusion.43, bf16[2,2,256,256]{2,3,0,1:T(8,128)(2,1)S(1)} %negate_convert_fusion, s32[512]{0:T(512)S(1)} %iota_add_fusion, s32[256]{0:T(256)S(1)} %iota_add_fusion.1, bf16[256,512]{1,0:T(8,128)(2,1)S(1)} %get-tuple-element.162, s32[]{:T(128)S(6)} %select_n.122), kind=kOutput, calls=%fused_computation.21 | convolution fusion | flops 102891520 | bytes 1117188 | tf_op jit(solution)/shard_map/kns,sp->knp/dot_general | solution.py:71
  63.7 3.1 %fusion.5 = f32[2,128,512]{2,1,0:T(8,128)S(1)} fusion(f32[2,128,512]{2,1,0:T(8,128)S(1)} %fusion.10, f32[2,256,128]{1,2,0:T(8,128)S(1)} %fusion.44, pred[128,512]{1,0:T(8,128)(4,1)S(1)} %broadcast_compare_fusion, bf16[2,2,256,256]{2,3,0,1:T(8,128)(2,1)S(1)} %negate_convert_fusion, s32[512]{0:T(512)S(1)} %iota_add_fusion, s32[256]{0:T(256)S(1)} %iota_add_fusion.1, ...), kind=kOutput, calls=%fused_computation.12 | convolution fusion | flops 103284736 | bytes 1707012 | tf_op jit(solution)/shard_map/kns,sp->knp/dot_general | solution.py:73
  66.8 1.5 collective-permute-start
  69.8 0.3 collective-permute-done
  70.1 0.2 fusion.21
  70.5 1.0 broadcast_multiply_fusion
  71.5 0.6 dynamic-slice
  72.1 0.8 slice_reduce_fusion
  72.8 1.4 dynamic-update-slice
  74.2 1.3 dynamic-update-slice.1
  75.5 11.8 %all-reduce.8 = (s32[8]{0:T(128)S(1)}, s32[8]{0:T(128)S(1)}) all-reduce(s32[8]{0:T(128)S(1)} %dynamic-update-slice, s32[8]{0:T(128)S(1)} %dynamic-update-slice.1), channel_id=1, replica_groups=mesh['tm'=8,'rows'=4] {'tm'}, use_global_device_ids=true, to_apply=%add.6 | all-reduce | flops 16 | bytes 128
  88.7 0.1 slice_convert_fusion.1
  88.8 0.1 slice.142
  88.9 0.1 slice.146
  89.1 0.1 slice_bitcast_fusion
  89.1 39.3 %all-gather.3.cloned.1.call-done = f32[1280,512]{1,0:T(8,128)} async-done(((f32[160,512]{1,0:T(8,128)}), f32[1280,512]{1,0:T(8,128)}) %all-gather.3.cloned.1.call-update) | async-done | bytes 2621456 | tf_op jit(solution)/shard_map/all_gather | solution.py:25
  128.5 27.1 %while.16 = (s32[]{:T(128)}, f32[160,512]{1,0:T(8,128)S(1)}, s32[]{:T(128)}, f32[8,160,512]{2,1,0:T(8,128)}, s32[8]{0:T(128)S(1)}, /*index=5*/s32[8]{0:T(128)S(1...) while((s32[]{:T(128)}, f32[160,512]{1,0:T(8,128)S(1)}, ...), condition=%wide.region_4.6_spmd, body=%wide.region_3.5_spmd.sunk | while | flops 246299 | bytes 1639884 | solution.py:34
  128.5 0.6 dynamic_slice.173
  129.7 0.7 dynamic_slice.174
  131.1 1.2 fusion.110
  132.3 0.6 dynamic_slice.173
  133.6 0.7 dynamic_slice.174
  135.0 1.2 fusion.110
  136.2 0.6 dynamic_slice.173
  137.5 0.7 dynamic_slice.174
  138.8 1.2 fusion.110
  140.1 0.6 dynamic_slice.173
  141.4 0.7 dynamic_slice.174
  142.7 1.2 fusion.110
  144.0 0.6 dynamic_slice.173
  145.2 0.7 dynamic_slice.174
  146.6 1.2 fusion.110
  147.9 0.6 dynamic_slice.173
  149.1 0.7 dynamic_slice.174
  150.5 1.2 fusion.110
  151.7 0.6 dynamic_slice.173
  153.0 0.7 dynamic_slice.174
  154.4 1.2 fusion.110
  155.6 0.1 pad_dynamic-slice_fusion.11
  155.7 1.1 fusion.38
  156.9 2.6 %maximum_add_fusion = f32[2]{0:T(128)S(1)} fusion(f32[1]{0:T(128)} %bitcast.37, f32[1]{0:T(128)} %bitcast.36, f32[1]{0:T(128)} %bitcast.43, f32[1]{0:T(128)} %bitcast.42), kind=kLoop, calls=%fused_computation.140 | loop fusion | flops 6 | bytes 24 | tf_op jit(solution)/shard_map/add | solution.py:163
  159.5 36.8 %psum.15 = f32[2]{0:T(128)S(1)} all-reduce(f32[2]{0:T(128)S(1)} %maximum_add_fusion), channel_id=1, replica_groups=mesh['tm'=8,'rows'=4] {'tm','rows'}, use_global_device_ids=true, to_apply=%region_9.11 | all-reduce | flops 2 | bytes 16 | tf_op jit(solution)/shard_map/psum | solution.py:166
  196.3 0.5 negate_multiply_fusion
  196.8 0.8 pad_maximum_fusion
  (40 shorter events, 0.6 us)
Async XLA Ops:
  7.2 6.8 %copy-start = (bf16[2,128,512]{2,1,0:T(8,128)(2,1)S(1)}, bf16[2,128,512]{2,1,0:T(8,128)(2,1)}, u32[]{:S(2)}) copy-start(bf16[2,128,512]{2,1,0:T(8,128)(2,1)} %param.8) | copy-start | bytes 786436
  7.2 52.6 %all-reduce.11.cloned.1.call-start = ((), (), s32[]{:S(2)}) async-start(), calls=%async_computation | async-start | bytes 2097152 | tf_op jit(solution)/shard_map/psum | solution.py:109
  10.7 50.8 %copy-start.1 = (bf16[256,512]{1,0:T(8,128)(2,1)}, bf16[256,512]{1,0:T(8,128)(2,1)S(1)}, u32[]{:S(2)}) copy-start(bf16[256,512]{1,0:T(8,128)(2,1)S(1)} %get-tuple-element.162) | copy-start | bytes 786436
  16.2 1.1 copy-start.2
  17.5 3.5 %copy-start.3 = (s32[2,2]{1,0:T(2,128)S(1)}, s32[2,2]{1,0:T(2,128)}, u32[]{:S(2)}) copy-start(s32[2,2]{1,0:T(2,128)} %param.10) | copy-start | bytes 52
  21.0 107.5 %all-gather.3.cloned.1.call-start = ((), (), s32[]{:S(2)}) async-start(), calls=%async_computation.1 | async-start | bytes 2949120 | tf_op jit(solution)/shard_map/all_gather | solution.py:25
  66.8 3.3 %collective-permute-start = (f32[2,33,512]{2,1,0:T(8,128)S(1)}, f32[2,33,512]{2,1,0:T(8,128)S(1)}, u32[]{:S(2)}, u32[]{:S(2)}) collective-permute-start(f32[2,33,512]{2,1,0:T(8,128)S(1)} %pad_maximum_fusion.2), channel_id=1, source_target_pairs={{1,0},{2,1},{3,2},{5,4},{6,5},{7,6},{9,8},{10,9},{11,10},{13,12},{... | collective-permute-start | bytes 405512 | tf_op jit(solution)/shard_map/ppermute | solution.py:18
  68.4 3.1 %copy-start.4 = (u32[32]{0:T(128)S(1)}, u32[32]{0:T(128)}, u32[]{:S(2)}) copy-start(u32[32]{0:T(128)} %constant.215) | copy-start | bytes 388
Sparse Core Ops, SparseCore 0:
  21.1 38.6 all-reduce.10
  71.6 56.8 all-gather.2
where the time goes:
time: 206 us; the launch traced here: 204 us
  waiting for transfers between devices  75.3 us (37%)
  blocking collectives  48.6 us (24%)
  other arithmetic  21.8 us (11%)
  between operations  19.6 us (10%)
  local copies, waits for them, and re-layouts  15.9 us (8%)
  matrix products  12.2 us (6%)
  loops' own time  9.56 us (5%)
    all_gather x1, waiting for transfers between devices, carried_in(): gathered = jax.tree.map(lambda a: lax.all_gather(a, axis), part)  39.3 us
    psum x1, blocking collectives, on_device(): wind_total = lax.psum(wind_terms, ('tm', 'rows'))  36.8 us
    psum x1, waiting for transfers between devices, on_device(): total = lax.psum(partial_field - placed, 'rows')  35.6 us
    unnamed x1, blocking collectives  11.8 us
    another operation x1, loops' own time, carried_in(): return lax.fori_loop(0, ahead, one, state)  9.56 us
    dynamic_slice x14, local copies, waits for them, and re-layouts, one(): lax.dynamic_index_in_dim(a, source, 0, False)  8.69 us
    add x7, other arithmetic, compose(): return (field_early + moved, rows_early + rows_late, cols_early + cols_late)  8.56 us
  transfers between devices with their start and end apart: 3, of which 3 were waited for; matrix products, arithmetic and copies ran while one was open for 3% of the time, Pallas kernels for 0%

commit v1 on v0

v1 whole, which is shorter than its diff:
```python
import functools
import math

import jax
import jax.numpy as jnp
import numpy as np
from jax import lax
from jax.experimental import pallas as pl
from jax.experimental.pallas import tpu as pltpu
from jax.sharding import PartitionSpec as P

decay_rate = 0.999
LANES = 128


def tables(pupil, focal):
    focal_pos = np.arange(focal) - focal // 2
    pupil_pos = np.arange(pupil) - pupil // 2
    turns = np.mod(focal_pos[:, None] * pupil_pos[None, :], 2 * pupil)
    angle = turns.astype(np.float32) * np.float32(math.pi / pupil)
    factor = np.float32(1.0 / math.sqrt(pupil))
    cos_t = (np.cos(angle) * factor).astype(jnp.bfloat16)
    sin_t = (-np.sin(angle) * factor).astype(jnp.bfloat16)
    return np.concatenate([cos_t, sin_t], axis=0)


def cum_shifts(sh_ref, stop):
    def add(t, sums):
        return (sums[0] + sh_ref[2 * t], sums[1] + sh_ref[2 * t + 1])

    return lax.fori_loop(0, stop, add, (jnp.int32(0), jnp.int32(0)))


def dot(a, b):
    return jnp.dot(a, b, preferred_element_type=jnp.float32)


def turned(value, down, right):
    value = pltpu.roll(value, lax.rem(down, value.shape[0]), 0)
    return pltpu.roll(value, lax.rem(right, value.shape[1]), 1)


def columns(shape):
    return lax.broadcasted_iota(jnp.int32, shape, 1)


def grad_kernel(
    n_rows, halo, slot, sh_ref, *refs
):
    m_refs, d_refs = refs[:n_rows], refs[n_rows : 2 * n_rows]
    phases_ref, mask_ref, halo_ref, tt_ref, cs_ref = refs[2 * n_rows : 2 * n_rows + 5]
    loc_ref, msg_ref, wind_ref = refs[2 * n_rows + 5 : 2 * n_rows + 8]
    y_ref, d_ref, r_ref, w_ref, lam_ref = refs[2 * n_rows + 8 :]
    frames, block, width = phases_ref.shape
    focal = cs_ref.shape[0] // 2
    part = focal // n_rows
    rows = block + halo
    me = lax.axis_index("rows")
    tm = lax.axis_index("tm")
    for d in range(n_rows):
        at = pl.multiple_of((me ^ d) * block, block)
        y = dot(m_refs[d][...].reshape(frames * block, width), tt_ref[:width])
        y = y.astype(jnp.bfloat16)
        at_q = pl.multiple_of((me ^ d) * part, part)
        for k in range(frames):
            y_ref[k, pl.ds(at, block), :] = y[k * block : (k + 1) * block]
            d_ref[k, :, pl.ds(at_q, part), :] = d_refs[d][k]
    for k in range(frames):
        pq = dot(cs_ref[...], y_ref[k])
        e_real = pq[:focal, :focal] - pq[focal:, focal:]
        e_imag = pq[:focal, focal:] + pq[focal:, :focal]
        real = (d_ref[k, 0].astype(jnp.float32) - e_real).astype(jnp.bfloat16)
        imag = (d_ref[k, 1].astype(jnp.float32) - e_imag).astype(jnp.bfloat16)
        r_ref[:focal, :focal] = real
        r_ref[:focal, focal:] = imag
        r_ref[focal:, :focal] = imag
        r_ref[focal:, focal:] = -real
        rows_t = tt_ref[pl.ds(pl.multiple_of(me * block, block), rows), :]
        w_ref[k] = dot(rows_t, r_ref[...]).astype(jnp.bfloat16)
    live = mask_ref[...] == 1
    live_halo = halo_ref[:halo].astype(jnp.float32) == 1.0
    col = columns((rows, width))
    row = lax.broadcasted_iota(jnp.int32, (rows, width), 0)
    down_sum = jnp.float32(0.0)
    side_sum = jnp.float32(0.0)
    for k in reversed(range(frames)):
        g = dot(w_ref[k], cs_ref[...])
        own = jnp.where(live, g[:block], 0.0)
        over = jnp.where(live_halo, g[block:], 0.0)
        if k == frames - 1:
            loc_ref[k] = own
            lam_ref[:block] = own
            lam_ref[block:] = over
        else:
            t = tm * frames + k
            a = sh_ref[2 * t]
            b = sh_ref[2 * t + 1]
            moved = turned(lam_ref[...], rows - a, width - b)
            inside = (col < width - b) & (row < rows - a)
            prior = jnp.where(inside, decay_rate * moved, 0.0)
            down, side = diffs(phases_ref, halo_ref, halo, k)
            down_sum = down_sum + jnp.sum(prior[:block] * down)
            side_sum = side_sum + jnp.sum(prior[:block] * side)
            own = own + prior[:block]
            loc_ref[k] = own
            lam_ref[:block] = own
            lam_ref[block:] = over + prior[block:]
    wind_ref[0] = down_sum
    wind_ref[1] = side_sum
    a_cum, b_cum = cum_shifts(sh_ref, tm * frames)
    canvas = turned(lam_ref[...], halo - a_cum, width - lax.rem(b_cum, width))
    canvas = jnp.where(row >= halo - a_cum, canvas, 0.0)
    per = rows // slot
    for j in range(msg_ref.shape[0]):
        if j < per * (width // LANES):
            c = j // per
            r = j % per
            msg_ref[j] = canvas[r * slot : (r + 1) * slot, c * LANES : (c + 1) * LANES]
        else:
            msg_ref[j] = jnp.zeros((slot, LANES), jnp.float32)


def diffs(phases_ref, halo_ref, halo, k):
    frames, block, width = phases_ref.shape
    here = phases_ref[k].astype(jnp.float32)
    last = halo_ref[halo + 8 * k : halo + 8 * k + 8].astype(jnp.float32)[:1]
    row = lax.broadcasted_iota(jnp.int32, (block, width), 0)
    below = jnp.where(row == block - 1, last, pltpu.roll(here, block - 1, 0))
    right = jnp.where(columns((block, width)) == width - 1, 0.0, pltpu.roll(here, width - 1, 1))
    return below - here, right - here


def scan_kernel(frames, rows, width, sh_ref, got_ref, out_ref):
    n, slot, _ = got_ref.shape
    me = lax.axis_index("tm")
    flat = me * slot + lax.broadcasted_iota(jnp.int32, (slot, LANES), 0)
    pos = lax.broadcasted_iota(jnp.int32, (slot, LANES), 1)
    for c in range(1, width // LANES):
        pos = pos + jnp.where(flat >= c * rows, LANES, 0)
    weight = decay_rate**frames

    def one(step, carry):
        field, b_cum = carry
        j = n - 1 - step
        out_ref[j] = field
        b_here = jnp.int32(0)
        for k in range(frames):
            b_here = b_here + sh_ref[2 * (j * frames + k) + 1]
        c = pos + lax.rem(b_cum, width)
        c = jnp.where(c >= width, c - width, c)
        field = got_ref[j] + jnp.where(c >= b_here, weight * field, 0.0)
        return field, b_cum - b_here

    _, b_all = cum_shifts(sh_ref, n * frames)
    lax.fori_loop(0, n, one, (jnp.zeros((slot, LANES), jnp.float32), b_all))


def final_kernel(halo, sh_ref, wind_in, got_ref, loc_ref, phases_ref, halo_ref, adj_ref, wind_ref, c_ref):
    frames, block, width = phases_ref.shape
    n, slot, _ = got_ref.shape
    rows = block + halo
    per = rows // slot
    for j in range(min(n, per * (width // LANES))):
        c = j // per
        r = j % per
        c_ref[r * slot : (r + 1) * slot, c * LANES : (c + 1) * LANES] = got_ref[j]
    tm = lax.axis_index("tm")
    a_cum, b_cum = cum_shifts(sh_ref, (tm + 1) * frames)
    down_sum = wind_in[0]
    side_sum = wind_in[1]
    col = columns((block, width))
    b_own = jnp.int32(0)
    for k in reversed(range(frames)):
        t = tm * frames + k
        a_cum = a_cum - sh_ref[2 * t]
        b_cum = b_cum - sh_ref[2 * t + 1]
        b_own = b_own + sh_ref[2 * t + 1]
        moved = turned(c_ref[...], rows - halo + a_cum, b_cum)[:block]
        moved = jnp.where(col < width - b_own, decay_rate ** (frames - k) * moved, 0.0)
        adj_ref[k] = loc_ref[k] + moved
        down, side = diffs(phases_ref, halo_ref, halo, k)
        down_sum = down_sum + jnp.sum(moved * down)
        side_sum = side_sum + jnp.sum(moved * side)
    wind_ref[0] = down_sum
    wind_ref[1] = side_sum


def swap(value, axis, bit):
    count = lax.axis_size(axis)
    return lax.ppermute(value, axis, [(s, s ^ bit) for s in range(count)])


def gather_rows(value):
    count = lax.axis_size("rows")
    held = {0: value}
    bit = count // 2
    while bit:
        held.update({d ^ bit: swap(v, "rows", bit) for d, v in list(held.items())})
        bit //= 2
    return [held[d] for d in range(count)]


def on_device(phases, focal_data, shifts, pupil_mask):
    frames, block, width = phases.shape
    n_rows = lax.axis_size("rows")
    n_tm = lax.axis_size("tm")
    frames_all = frames * n_tm
    focal = focal_data.shape[3]
    halo = min(frames_all // 2, width // (4 * n_rows))
    halo = -(-halo // 16) * 16
    rows = block + halo
    slot = max(1, rows * (width // LANES) // n_tm)
    cs = tables(width, focal)
    tt = np.concatenate([cs.T, np.zeros((halo, 2 * focal), cs.dtype)], axis=0)
    sh_all = lax.all_to_all(
        jnp.broadcast_to(shifts.reshape(1, 2 * frames), (n_tm, 2 * frames)), "tm", 0, 0
    ).reshape(2 * frames_all)
    masked = jnp.where((pupil_mask == 1)[None], phases, jnp.zeros_like(phases))
    m_parts = gather_rows(masked)
    d_parts = gather_rows(focal_data)
    outgoing = jnp.concatenate(
        [pupil_mask[:halo].astype(jnp.bfloat16)] + [phases[k, :8] for k in range(frames)], axis=0
    )
    incoming = lax.ppermute(outgoing, "rows", [(s, s - 1) for s in range(1, n_rows)])
    vmem = pl.BlockSpec(memory_space=pltpu.VMEM)
    smem = pl.BlockSpec(memory_space=pltpu.SMEM)
    field = jax.ShapeDtypeStruct((frames, block, width), jnp.float32)
    message = jax.ShapeDtypeStruct((n_tm, slot, LANES), jnp.float32)
    pair = jax.ShapeDtypeStruct((2,), jnp.float32)
    loc, msg, wind_local = pl.pallas_call(
        functools.partial(grad_kernel, n_rows, halo, slot),
        out_shape=(field, message, pair),
        in_specs=[smem] + [vmem] * (2 * n_rows + 5),
        out_specs=(vmem, vmem, smem),
        scratch_shapes=[
            pltpu.VMEM((frames, width, 2 * focal), jnp.bfloat16),
            pltpu.VMEM((frames, 2, focal, focal), jnp.bfloat16),
            pltpu.VMEM((2 * focal, 2 * focal), jnp.bfloat16),
            pltpu.VMEM((frames, rows, 2 * focal), jnp.bfloat16),
            pltpu.VMEM((rows, width), jnp.float32),
        ],
        name="grad",
    )(sh_all, *m_parts, *d_parts, phases, pupil_mask, incoming, tt, cs)
    got = lax.all_to_all(msg, "tm", 0, 0)
    fields = pl.pallas_call(
        functools.partial(scan_kernel, frames, rows, width),
        out_shape=message,
        in_specs=[smem, vmem],
        out_specs=vmem,
        name="scan",
    )(sh_all, got)
    back = lax.all_to_all(fields, "tm", 0, 0)
    adjoint, wind = pl.pallas_call(
        functools.partial(final_kernel, halo),
        out_shape=(field, pair),
        in_specs=[smem, smem, vmem, vmem, vmem, vmem],
        out_specs=(vmem, smem),
        scratch_shapes=[pltpu.VMEM((rows, width), jnp.float32)],
        name="final",
    )(sh_all, wind_local, back, loc, phases, incoming)
    wind = lax.psum(wind, "rows")
    wind = lax.all_to_all(jnp.broadcast_to(wind[None], (n_tm, 2)), "tm", 0, 0)
    wind_grad = -jnp.sum(wind, axis=0) / (width * frames_all)
    return adjoint, wind_grad


def solution(mesh):
    in_specs = (P("tm", "rows", None), P("tm", None, "rows", None), P("tm", None), P("rows", None))
    out_specs = (P("tm", "rows", None), P())
    return jax.shard_map(
        on_device, mesh=mesh, in_specs=in_specs, out_specs=out_specs, check_vma=False
    )
```

time: 206 us -> 85.9 us (0.42)
  waiting for transfers between devices: 75.3 us -> 7.34 us
  between operations: 19.6 us -> 0.82 us
  other arithmetic: 21.8 us -> 3.03 us
  local copies, waits for them, and re-layouts: 15.9 us -> 3.32 us
  matrix products: 12.2 us -> 0 us
  Pallas kernels: 0 us -> 10.3 us
  loops' own time: 9.56 us -> 0 us
  blocking collectives: 48.6 us -> 55.1 us
  starting transfers between devices: 1.55 us -> 5.34 us
    all_to_all x0 -> x4, blocking collectives: none -> 49.5 us  [the longest x1 14.7 us: on_device(): got = lax.all_to_all(msg, 'tm', 0, 0)]
    all_gather x1 -> x0, waiting for transfers between devices: 39.3 us -> none  [carried_in(): gathered = jax.tree.map(lambda a: lax.all_gather(a, axis), part)]
    psum x1 -> x0, waiting for transfers between devices: 35.6 us -> none  [on_device(): total = lax.psum(partial_field - placed, 'rows')]
    psum x1, blocking collectives: 36.8 us -> 5.63 us  [on_device(): wind = lax.psum(wind, 'rows')]
    dot_general x10 -> x0, matrix products: 12.2 us -> none  [the longest x1 3.25 us: on_device(): jnp.einsum('kbp,qp->kbq', masked, sin_t, preferred_element_type=jnp.float32)]
    unnamed x1 -> x0, blocking collectives: 11.8 us -> none
    add x9 -> x0, other arithmetic: 11.4 us -> none  [the longest x7 8.56 us: compose(): return (field_early + moved, rows_early + rows_late, cols_early + cols_late)]
    pallas_call x0 -> x3, Pallas kernels: none -> 10.3 us  [the longest x1 5.83 us: on_device(): pl.pallas_call(functools.partial(grad_kernel, n_rows, halo, slot), out_sh...]
  transfers between devices with their start and end apart: 3 -> 7, of which waited for: 3 -> 2; matrix products, arithmetic and copies ran while one was open for 3% -> 3% of each run, Pallas kernels for 0% -> 0%
where the time goes in v1:
time: 85.9 us; the launch traced here: 85.3 us
  blocking collectives  55.1 us (64%)
  Pallas kernels  10.3 us (12%)
  waiting for transfers between devices  7.34 us (9%)
  starting transfers between devices  5.34 us (6%)
  local copies, waits for them, and re-layouts  3.32 us (4%)
  other arithmetic  3.03 us (4%)
    all_to_all x1, blocking collectives, on_device(): got = lax.all_to_all(msg, 'tm', 0, 0)  14.7 us
    all_to_all x1, blocking collectives, on_device(): back = lax.all_to_all(fields, 'tm', 0, 0)  13.2 us
    all_to_all x1, blocking collectives, on_device(): lax.all_to_all(jnp.broadcast_to(shifts.reshape(1, 2 * frames), (n_tm, 2 *...  12.4 us
    all_to_all x1, blocking collectives, on_device(): wind = lax.all_to_all(jnp.broadcast_to(wind[None], (n_tm, 2)), 'tm', 0, 0)  9.21 us
    ppermute x6, waiting for transfers between devices, swap(): return lax.ppermute(value, axis, [(s, s ^ bit) for s in range(count)])  7.34 us
    pallas_call x1, Pallas kernels, on_device(): pl.pallas_call(functools.partial(grad_kernel, n_rows, halo, slot), out_sh...  5.83 us
    psum x1, blocking collectives, on_device(): wind = lax.psum(wind, 'rows')  5.63 us
    ppermute x6, starting transfers between devices, swap(): return lax.ppermute(value, axis, [(s, s ^ bit) for s in range(count)])  4.05 us
  transfers between devices with their start and end apart: 7, of which 2 were waited for; matrix products, arithmetic and copies ran while one was open for 3% of the time, Pallas kernels for 0%

profile of v1, /device:TPU:0, one launch (start us, length us, event | category | flops | bytes accessed | tf_op | source)
XLA Modules:
  0.0 85.3 jit_solution(14011045702696760786)
XLA Ops:
  0.6 0.0 copy-start
  0.6 1.0 %broadcast_compare_fusion = pred[128,512]{1,0:T(8,128)(4,1)S(1)} fusion(s32[128,512]{1,0:T(8,128)} %refs_9_.1), kind=kLoop, calls=%fused_computation.1 | loop fusion | flops 65536 | bytes 327680 | tf_op jit(solution)/shard_map/eq | solution.py:218
  1.7 0.0 copy-done
  1.7 0.0 copy-start.6
  1.7 0.0 copy-start.1
  1.7 3.0 %collective-permute-start.1 = (bf16[2,128,512]{2,1,0:T(8,128)(2,1)S(1)}, bf16[2,128,512]{2,1,0:T(8,128)(2,1)S(1)}, u32[]{:S(2)}, u32[]{:S(2)}) collective-permute-start(bf16[2,128,512]{2,1,0:T(8,128)(2,1)S(1)} %broadcast_select_fusion.refs_0_), channel_id=1, source_target_pairs={{0,2},{1,3},{2,0},{3,1},{4,6},{5,7},{6,4},{7,5},{8,10},{9,11},{10,... | collective-permute-start | bytes 786440 | tf_op jit(solution)/shard_map/ppermute | solution.py:190
  4.8 0.0 copy-done.6
  4.8 0.0 collective-permute-start.3
  4.8 0.8 collective-permute-start.4
  5.6 0.2 collective-permute-start
  5.8 0.8 slice_convert_fusion
  6.6 5.4 %collective-permute-done.1.refs_2_ = bf16[2,128,512]{2,1,0:T(8,128)(2,1)S(1)} collective-permute-done((bf16[2,128,512]{2,1,0:T(8,128)(2,1)S(1)}, bf16[2,128,512]{2,1,0:T(8,128)(2,1)S(1)}, u32[]{:S(2)}, u32[]{:S(2)}) %collective-permute-start.1) | collective-permute-done | bytes 262176 | tf_op jit(solution)/shard_map/ppermute | solution.py:190
  11.9 0.0 copy-start.2
  11.9 0.0 collective-permute-start.2
  11.9 1.9 %collective-permute-done.4.refs_6_ = bf16[2,2,64,256]{3,2,1,0:T(8,128)(2,1)S(1)} collective-permute-done((bf16[2,2,64,256]{3,2,1,0:T(8,128)(2,1)S(1)}, bf16[2,2,64,256]{3,2,1,0:T(8,128)(2,1)S(1)}, u32[]{:S(2)}, u32[]{:S(2)}) %collective-permute-start.4) | collective-permute-done | bytes 131104 | tf_op jit(solution)/shard_map/ppermute | solution.py:190
  13.9 0.0 copy-start.8
  13.9 0.0 collective-permute-start.5
  13.9 0.0 copy-start.10
  13.9 1.3 %collective-permute-start.6 = (bf16[32,512]{1,0:T(8,128)(2,1)S(1)}, bf16[32,512]{1,0:T(8,128)(2,1)S(1)}, u32[]{:S(2)}, u32[]{:S(2)}) collective-permute-start(bf16[32,512]{1,0:T(8,128)(2,1)S(1)} %pad_maximum_fusion), channel_id=1, source_target_pairs={{1,0},{2,1},{3,2},{5,4},{6,5},{7,6},{9,8},{10,9},{11,10},{13,12},{... | collective-permute-start | bytes 98312 | tf_op jit(solution)/shard_map/ppermute | solution.py:224
  15.2 0.0 copy-done.10
  15.2 0.1 broadcast_in_dim.25
  15.3 12.4 %all_to_all.22 = s32[8,1,4]{2,1,0:T(1,128)S(1)} all-to-all(s32[8,1,4]{2,1,0:T(1,128)S(1)} %broadcast_in_dim.26), channel_id=1, replica_groups=mesh['tm'=8,'rows'=4] {'tm'}, dimensions={0} | all-to-all | bytes 256 | tf_op jit(solution)/shard_map/all_to_all | solution.py:215
  27.7 0.5 broadcast.16
  28.2 0.7 reduce.4
  28.9 0.6 reshape.24.sh_ref
  29.5 0.0 collective-permute-done.6.refs_10_.halo_ref
  29.5 0.0 copy-start.5
  29.5 0.0 collective-permute-done.3.refs_5_
  29.5 0.0 copy-start.7
  29.5 0.0 collective-permute-done.5.refs_7_
  29.5 0.0 copy-start.9
  29.5 0.0 collective-permute-done.refs_1_
  29.5 0.0 copy-start.3
  29.5 0.0 collective-permute-done.2.refs_3_
  29.5 0.0 copy-done.1
  29.5 0.0 copy-done.2
  29.6 0.0 copy-done.8
  29.6 0.5 copy-done.5
  30.1 0.1 copy-done.7
  30.1 0.0 copy-done.9
  30.2 0.1 copy-done.3
  30.3 0.0 copy-start.4
  30.3 0.7 copy-done.4
  31.0 5.8 %grad.1 = (f32[2,128,512]{2,1,0:T(8,128)}, f32[8,72,128]{2,1,0:T(8,128)}, f32[2]{0:T(128)}) custom-call(s32[32]{0:T(128)} %reshape.24.sh_ref, bf16[2,128,512]{2,1,0:T(8,128)(2,1)} %copy-done.1, bf16[2,128,512]{2,1,0:T(8,128)(2,1)} %copy-done.3, bf16[2,128,512]{2,1,0:T(8,128)(2,1)} %copy-done.2, bf16[2,128,512]{2,1,0:T(8,128)(2,1)} %copy-done.4, ...), custom_call_target="tpu_custom_call" | custom-call | tf_op jit(solution)/shard_map/grad/pallas_call | solution.py:230
  36.8 14.7 %all_to_all.23.got_ref = f32[8,72,128]{2,1,0:T(8,128)} all-to-all(f32[8,72,128]{2,1,0:T(8,128)} %get-tuple-element.8), channel_id=1, replica_groups=mesh['tm'=8,'rows'=4] {'tm'}, dimensions={0} | all-to-all | bytes 589824 | tf_op jit(solution)/shard_map/all_to_all | solution.py:244
  51.5 1.9 %scan.1 = f32[8,72,128]{2,1,0:T(8,128)} custom-call(s32[32]{0:T(128)} %reshape.24.sh_ref, f32[8,72,128]{2,1,0:T(8,128)} %all_to_all.23.got_ref), custom_call_target="tpu_custom_call" | custom-call | tf_op jit(solution)/shard_map/scan/pallas_call | solution.py:245
  53.4 13.2 %all_to_all.24.got_ref = f32[8,72,128]{2,1,0:T(8,128)} all-to-all(f32[8,72,128]{2,1,0:T(8,128)} %scan.1), channel_id=1, replica_groups=mesh['tm'=8,'rows'=4] {'tm'}, dimensions={0} | all-to-all | bytes 589824 | tf_op jit(solution)/shard_map/all_to_all | solution.py:252
  66.7 2.6 %final.1 = (f32[2,128,512]{2,1,0:T(8,128)}, f32[2]{0:T(128)}) custom-call(s32[32]{0:T(128)} %reshape.24.sh_ref, f32[2]{0:T(128)} %get-tuple-element.7.wind_in, f32[8,72,128]{2,1,0:T(8,128)} %all_to_all.24.got_ref, f32[2,128,512]{2,1,0:T(8,128)} %get-tuple-element.9.loc_ref, bf16[2,128,512]{2,1,0:T(8,128)(2,1)} %phases_ref.1, bf16[32,512]{1,0:T(8,128)(2,1)} %copy-done.5), custom_call_target="tpu_custom_call" | custom-call | tf_op jit(solution)/shard_map/final/pallas_call | solution.py:253
  69.2 0.0 copy-start.11
  69.2 0.7 copy-done.11
  69.9 5.6 %psum.7 = f32[2]{0:T(128)S(1)} all-reduce(f32[2]{0:T(128)S(1)} %copy-done.11), channel_id=1, replica_groups=mesh['tm'=8,'rows'=4] {'rows'}, use_global_device_ids=true, to_apply=%region_0.1 | all-reduce | flops 2 | bytes 16 | tf_op jit(solution)/shard_map/psum | solution.py:261
  75.5 9.2 %all_to_all.25 = f32[8,1,2]{2,1,0:T(1,128)S(1)} all-to-all(f32[8,1,2]{2,1,0:T(1,128)S(1)} %broadcast_in_dim.29), channel_id=1, replica_groups=mesh['tm'=8,'rows'=4] {'tm'}, dimensions={0} | all-to-all | bytes 128 | tf_op jit(solution)/shard_map/all_to_all | solution.py:262
  84.8 0.5 negate_multiply_fusion
  (6 shorter events, 0.1 us)
Async XLA Ops:
  0.6 1.0 %copy-start = (bf16[2,128,512]{2,1,0:T(8,128)(2,1)S(1)}, bf16[2,128,512]{2,1,0:T(8,128)(2,1)}, u32[]{:S(2)}) copy-start(bf16[2,128,512]{2,1,0:T(8,128)(2,1)} %phases_ref.1) | copy-start | bytes 786436
  1.7 3.1 %copy-start.6 = (bf16[2,2,64,256]{3,2,1,0:T(8,128)(2,1)S(1)}, bf16[2,2,64,256]{3,2,1,0:T(8,128)(2,1)}, u32[]{:S(2)}) copy-start(bf16[2,2,64,256]{3,2,1,0:T(8,128)(2,1)} %refs_4_.1) | copy-start | bytes 393220
  1.7 27.8 %copy-start.1 = (bf16[2,128,512]{2,1,0:T(8,128)(2,1)}, bf16[2,128,512]{2,1,0:T(8,128)(2,1)S(1)}, u32[]{:S(2)}) copy-start(bf16[2,128,512]{2,1,0:T(8,128)(2,1)S(1)} %broadcast_select_fusion.refs_0_) | copy-start | bytes 786436
  1.7 10.2 %collective-permute-start.1 = (bf16[2,128,512]{2,1,0:T(8,128)(2,1)S(1)}, bf16[2,128,512]{2,1,0:T(8,128)(2,1)S(1)}, u32[]{:S(2)}, u32[]{:S(2)}) collective-permute-start(bf16[2,128,512]{2,1,0:T(8,128)(2,1)S(1)} %broadcast_select_fusion.refs_0_), channel_id=1, source_target_pairs={{0,2},{1,3},{2,0},{3,1},{4,6},{5,7},{6,4},{7,5},{8,10},{9,11},{10,... | collective-permute-start | bytes 786440 | tf_op jit(solution)/shard_map/ppermute | solution.py:190
  4.8 24.7 %collective-permute-start.3 = (bf16[2,2,64,256]{3,2,1,0:T(8,128)(2,1)S(1)}, bf16[2,2,64,256]{3,2,1,0:T(8,128)(2,1)S(1)}, u32[]{:S(2)}, u32[]{:S(2)}) collective-permute-start(bf16[2,2,64,256]{3,2,1,0:T(8,128)(2,1)S(1)} %copy-done.6), channel_id=1, source_target_pairs={{0,1},{1,0},{2,3},{3,2},{4,5},{5,4},{6,7},{7,6},{8,9},{9,8},{10,11... | collective-permute-start | bytes 393224 | tf_op jit(solution)/shard_map/ppermute | solution.py:190
  4.8 9.1 %collective-permute-start.4 = (bf16[2,2,64,256]{3,2,1,0:T(8,128)(2,1)S(1)}, bf16[2,2,64,256]{3,2,1,0:T(8,128)(2,1)S(1)}, u32[]{:S(2)}, u32[]{:S(2)}) collective-permute-start(bf16[2,2,64,256]{3,2,1,0:T(8,128)(2,1)S(1)} %copy-done.6), channel_id=1, source_target_pairs={{0,2},{1,3},{2,0},{3,1},{4,6},{5,7},{6,4},{7,5},{8,10},{9,11},{10,... | collective-permute-start | bytes 393224 | tf_op jit(solution)/shard_map/ppermute | solution.py:190
  5.6 23.9 %collective-permute-start = (bf16[2,128,512]{2,1,0:T(8,128)(2,1)S(1)}, bf16[2,128,512]{2,1,0:T(8,128)(2,1)S(1)}, u32[]{:S(2)}, u32[]{:S(2)}) collective-permute-start(bf16[2,128,512]{2,1,0:T(8,128)(2,1)S(1)} %broadcast_select_fusion.refs_0_), channel_id=1, source_target_pairs={{0,1},{1,0},{2,3},{3,2},{4,5},{5,4},{6,7},{7,6},{8,9},{9,8},{10,11... | collective-permute-start | bytes 786440 | tf_op jit(solution)/shard_map/ppermute | solution.py:190
  11.9 17.6 %copy-start.2 = (bf16[2,128,512]{2,1,0:T(8,128)(2,1)}, bf16[2,128,512]{2,1,0:T(8,128)(2,1)S(1)}, u32[]{:S(2)}) copy-start(bf16[2,128,512]{2,1,0:T(8,128)(2,1)S(1)} %collective-permute-done.1.refs_2_) | copy-start | bytes 786436
  11.9 17.6 %collective-permute-start.2 = (bf16[2,128,512]{2,1,0:T(8,128)(2,1)S(1)}, bf16[2,128,512]{2,1,0:T(8,128)(2,1)S(1)}, u32[]{:S(2)}, u32[]{:S(2)}) collective-permute-start(bf16[2,128,512]{2,1,0:T(8,128)(2,1)S(1)} %collective-permute-done.1.refs_2_), channel_id=1, source_target_pairs={{0,1},{1,0},{2,3},{3,2},{4,5},{5,4},{6,7},{7,6},{8,9},{9,8},{10,11... | collective-permute-start | bytes 786440 | tf_op jit(solution)/shard_map/ppermute | solution.py:190
  13.9 15.7 %copy-start.8 = (bf16[2,2,64,256]{3,2,1,0:T(8,128)(2,1)}, bf16[2,2,64,256]{3,2,1,0:T(8,128)(2,1)S(1)}, u32[]{:S(2)}) copy-start(bf16[2,2,64,256]{3,2,1,0:T(8,128)(2,1)S(1)} %collective-permute-done.4.refs_6_) | copy-start | bytes 393220
  13.9 15.6 %collective-permute-start.5 = (bf16[2,2,64,256]{3,2,1,0:T(8,128)(2,1)S(1)}, bf16[2,2,64,256]{3,2,1,0:T(8,128)(2,1)S(1)}, u32[]{:S(2)}, u32[]{:S(2)}) collective-permute-start(bf16[2,2,64,256]{3,2,1,0:T(8,128)(2,1)S(1)} %collective-permute-done.4.refs_6_), channel_id=1, source_target_pairs={{0,1},{1,0},{2,3},{3,2},{4,5},{5,4},{6,7},{7,6},{8,9},{9,8},{10,11... | collective-permute-start | bytes 393224 | tf_op jit(solution)/shard_map/ppermute | solution.py:190
  13.9 1.3 %copy-start.10 = (s32[2,2]{1,0:T(2,128)S(1)}, s32[2,2]{1,0:T(2,128)}, u32[]{:S(2)}) copy-start(s32[2,2]{1,0:T(2,128)} %param.8) | copy-start | bytes 52
  13.9 15.6 %collective-permute-start.6 = (bf16[32,512]{1,0:T(8,128)(2,1)S(1)}, bf16[32,512]{1,0:T(8,128)(2,1)S(1)}, u32[]{:S(2)}, u32[]{:S(2)}) collective-permute-start(bf16[32,512]{1,0:T(8,128)(2,1)S(1)} %pad_maximum_fusion), channel_id=1, source_target_pairs={{1,0},{2,1},{3,2},{5,4},{6,5},{7,6},{9,8},{10,9},{11,10},{13,12},{... | collective-permute-start | bytes 98312 | tf_op jit(solution)/shard_map/ppermute | solution.py:224
  29.5 0.6 copy-start.5
  29.5 0.7 copy-start.7
  29.5 0.7 copy-start.9
  29.5 0.8 copy-start.3
  30.3 0.7 copy-start.4
  69.2 0.7 copy-start.11

commit v2 on v1

--- a/solution.py
+++ b/solution.py
@@ -24,9 +24,17 @@
     return np.concatenate([cos_t, sin_t], axis=0)
 
 
-def cum_shifts(sh_ref, stop):
-    def add(t, sums):
-        return (sums[0] + sh_ref[2 * t], sums[1] + sh_ref[2 * t + 1])
+def own_shift(sh_ref, frames, j, k):
+    at = 2 * ((j ^ lax.axis_index("tm")) * frames + k)
+    return sh_ref[at], sh_ref[at + 1]
+
+
+def cum_shifts(sh_ref, frames, stop):
+    def add(j, sums):
+        for k in range(frames):
+            a, b = own_shift(sh_ref, frames, j, k)
+            sums = (sums[0] + a, sums[1] + b)
+        return sums
 
     return lax.fori_loop(0, stop, add, (jnp.int32(0), jnp.int32(0)))
 
@@ -92,9 +100,7 @@
             lam_ref[:block] = own
             lam_ref[block:] = over
         else:
-            t = tm * frames + k
-            a = sh_ref[2 * t]
-            b = sh_ref[2 * t + 1]
+            a, b = sh_ref[2 * k], sh_ref[2 * k + 1]
             moved = turned(lam_ref[...], rows - a, width - b)
             inside = (col < width - b) & (row < rows - a)
             prior = jnp.where(inside, decay_rate * moved, 0.0)
@@ -107,7 +113,7 @@
             lam_ref[block:] = over + prior[block:]
     wind_ref[0] = down_sum
     wind_ref[1] = side_sum
-    a_cum, b_cum = cum_shifts(sh_ref, tm * frames)
+    a_cum, b_cum = cum_shifts(sh_ref, frames, tm)
     canvas = turned(lam_ref[...], halo - a_cum, width - lax.rem(b_cum, width))
     canvas = jnp.where(row >= halo - a_cum, canvas, 0.0)
     per = rows // slot
@@ -145,18 +151,17 @@
         out_ref[j] = field
         b_here = jnp.int32(0)
         for k in range(frames):
-            b_here = b_here + sh_ref[2 * (j * frames + k) + 1]
+            b_here = b_here + own_shift(sh_ref, frames, j, k)[1]
         c = pos + lax.rem(b_cum, width)
         c = jnp.where(c >= width, c - width, c)
         field = got_ref[j] + jnp.where(c >= b_here, weight * field, 0.0)
         return field, b_cum - b_here
 
-    _, b_all = cum_shifts(sh_ref, n * frames)
+    _, b_all = cum_shifts(sh_ref, frames, n)
     lax.fori_loop(0, n, one, (jnp.zeros((slot, LANES), jnp.float32), b_all))
 
 
-def final_kernel(halo, sh_ref, wind_in, got_ref, loc_ref, phases_ref, halo_ref, adj_ref, wind_ref, c_ref):
-    frames, block, width = phases_ref.shape
+def carried(halo, frames, block, width, sh_ref, got_ref, c_ref):
     n, slot, _ = got_ref.shape
     rows = block + halo
     per = rows // slot
@@ -164,25 +169,34 @@
         c = j // per
         r = j % per
         c_ref[r * slot : (r + 1) * slot, c * LANES : (c + 1) * LANES] = got_ref[j]
-    tm = lax.axis_index("tm")
-    a_cum, b_cum = cum_shifts(sh_ref, (tm + 1) * frames)
-    down_sum = wind_in[0]
-    side_sum = wind_in[1]
+    a_cum, b_cum = cum_shifts(sh_ref, frames, lax.axis_index("tm") + 1)
     col = columns((block, width))
     b_own = jnp.int32(0)
     for k in reversed(range(frames)):
-        t = tm * frames + k
-        a_cum = a_cum - sh_ref[2 * t]
-        b_cum = b_cum - sh_ref[2 * t + 1]
-        b_own = b_own + sh_ref[2 * t + 1]
+        a, b = sh_ref[2 * k], sh_ref[2 * k + 1]
+        a_cum = a_cum - a
+        b_cum = b_cum - b
+        b_own = b_own + b
         moved = turned(c_ref[...], rows - halo + a_cum, b_cum)[:block]
-        moved = jnp.where(col < width - b_own, decay_rate ** (frames - k) * moved, 0.0)
-        adj_ref[k] = loc_ref[k] + moved
+        yield k, jnp.where(col < width - b_own, decay_rate ** (frames - k) * moved, 0.0)
+
+
+def wind_kernel(halo, sh_ref, wind_in, got_ref, phases_ref, halo_ref, wind_ref, c_ref):
+    frames, block, width = phases_ref.shape
+    down_sum = wind_in[0]
+    side_sum = wind_in[1]
+    for k, moved in carried(halo, frames, block, width, sh_ref, got_ref, c_ref):
         down, side = diffs(phases_ref, halo_ref, halo, k)
         down_sum = down_sum + jnp.sum(moved * down)
         side_sum = side_sum + jnp.sum(moved * side)
-    wind_ref[0] = down_sum
-    wind_ref[1] = side_sum
+    lane = lax.broadcasted_iota(jnp.int32, wind_ref.shape, 2)
+    wind_ref[...] = jnp.where(lane == 0, down_sum, jnp.where(lane == 1, side_sum, 0.0))
+
+
+def final_kernel(halo, sh_ref, got_ref, loc_ref, adj_ref, c_ref):
+    frames, block, width = loc_ref.shape
+    for k, moved in carried(halo, frames, block, width, sh_ref, got_ref, c_ref):
+        adj_ref[k] = loc_ref[k] + moved
 
 
 def swap(value, axis, bit):
@@ -212,9 +226,11 @@
     slot = max(1, rows * (width // LANES) // n_tm)
     cs = tables(width, focal)
     tt = np.concatenate([cs.T, np.zeros((halo, 2 * focal), cs.dtype)], axis=0)
-    sh_all = lax.all_to_all(
-        jnp.broadcast_to(shifts.reshape(1, 2 * frames), (n_tm, 2 * frames)), "tm", 0, 0
-    ).reshape(2 * frames_all)
+    sh_all = shifts.reshape(2 * frames)
+    bit = 1
+    while bit < n_tm:
+        sh_all = jnp.concatenate([sh_all, swap(sh_all, "tm", bit)])
+        bit *= 2
     masked = jnp.where((pupil_mask == 1)[None], phases, jnp.zeros_like(phases))
     m_parts = gather_rows(masked)
     d_parts = gather_rows(focal_data)
@@ -239,6 +255,7 @@
             pltpu.VMEM((frames, rows, 2 * focal), jnp.bfloat16),
             pltpu.VMEM((rows, width), jnp.float32),
         ],
+        compiler_params=pltpu.CompilerParams(vmem_limit_bytes=28 << 20),
         name="grad",
     )(sh_all, *m_parts, *d_parts, phases, pupil_mask, incoming, tt, cs)
     got = lax.all_to_all(msg, "tm", 0, 0)
@@ -247,20 +264,35 @@
         out_shape=message,
         in_specs=[smem, vmem],
         out_specs=vmem,
+        compiler_params=pltpu.CompilerParams(vmem_limit_bytes=6 << 20),
         name="scan",
     )(sh_all, got)
     back = lax.all_to_all(fields, "tm", 0, 0)
-    adjoint, wind = pl.pallas_call(
+    n_all = n_tm * n_rows
+    canvas = pltpu.VMEM((rows, width), jnp.float32)
+    wind = pl.pallas_call(
+        functools.partial(wind_kernel, halo),
+        out_shape=jax.ShapeDtypeStruct((n_all, 1, LANES), jnp.float32),
+        in_specs=[smem, smem, vmem, vmem, vmem],
+        out_specs=vmem,
+        scratch_shapes=[canvas],
+        compiler_params=pltpu.CompilerParams(vmem_limit_bytes=8 << 20),
+        name="wind",
+    )(sh_all, wind_local, back, phases, incoming)
+    winds = lax.all_to_all(wind, ("tm", "rows"), 0, 0)
+    adjoint = pl.pallas_call(
         functools.partial(final_kernel, halo),
-        out_shape=(field, pair),
-        in_specs=[smem, smem, vmem, vmem, vmem, vmem],
-        out_specs=(vmem, smem),
-        scratch_shapes=[pltpu.VMEM((rows, width), jnp.float32)],
+        out_shape=field,
+        in_specs=[smem, vmem, vmem],
+        out_specs=vmem,
+        scratch_shapes=[canvas],
+        cost_estimate=pl.CostEstimate(
+            flops=10 * rows * width, bytes_accessed=12 * frames * block * width, transcendentals=0
+        ),
+        compiler_params=pltpu.CompilerParams(vmem_limit_bytes=8 << 20),
         name="final",
-    )(sh_all, wind_local, back, loc, phases, incoming)
-    wind = lax.psum(wind, "rows")
-    wind = lax.all_to_all(jnp.broadcast_to(wind[None], (n_tm, 2)), "tm", 0, 0)
-    wind_grad = -jnp.sum(wind, axis=0) / (width * frames_all)
+    )(sh_all, back, loc)
+    wind_grad = -jnp.sum(winds[:, 0, :2], axis=0) / (width * frames_all)
     return adjoint, wind_grad
 
 

time: 85.9 us -> 71.7 us (0.83)
  blocking collectives: 55.1 us -> 30.9 us
  starting transfers between devices: 5.34 us -> 13.3 us
  waiting for transfers between devices: 7.34 us -> 13.6 us
  Pallas kernels: 10.3 us -> 8.41 us
  other arithmetic: 3.03 us -> 1.82 us
    all_to_all x2 -> x0, blocking collectives: 21.6 us -> none  [the longest x1 12.4 us: on_device(): lax.all_to_all(jnp.broadcast_to(shifts.reshape(1, 2 * frames), (n_tm, 2 *...]
    psum x1 -> x0, blocking collectives: 5.63 us -> none  [on_device(): wind = lax.psum(wind, 'rows')]
    all_to_all x0 -> x1, waiting for transfers between devices: none -> 5.53 us  [on_device(): winds = lax.all_to_all(wind, ('tm', 'rows'), 0, 0)]
    ppermute x6 -> x9, starting transfers between devices: 4.05 us -> 9.58 us  [swap(): return lax.ppermute(value, axis, [(s, s ^ bit) for s in range(count)])]
    all_to_all x0 -> x1, starting transfers between devices: none -> 2.46 us  [on_device(): winds = lax.all_to_all(wind, ('tm', 'rows'), 0, 0)]
    ppermute x1, waiting for transfers between devices: 0.01 us -> 1.72 us  [on_device(): lax.ppermute(outgoing, 'rows', [(s, s - 1) for s in range(1, n_rows)])]
    all_to_all x1, blocking collectives: 14.7 us -> 16.3 us  [on_device(): got = lax.all_to_all(msg, 'tm', 0, 0)]
    pallas_call x1, Pallas kernels: 5.83 us -> 4.22 us  [on_device(): pl.pallas_call(functools.partial(grad_kernel, n_rows, halo, slot), out_sh...]
  transfers between devices with their start and end apart: 7 -> 11, of which waited for: 2 -> 5; matrix products, arithmetic and copies ran while one was open for 3% -> 2% of each run, Pallas kernels for 0% -> 2%
where the time goes in v2:
time: 71.7 us; the launch traced here: 71.3 us
  blocking collectives  30.9 us (43%)
  waiting for transfers between devices  13.6 us (19%)
  starting transfers between devices  13.3 us (19%)
  Pallas kernels  8.41 us (12%)
  local copies, waits for them, and re-layouts  2.51 us (4%)
  other arithmetic  1.82 us (3%)
  between operations  0.77 us (1%)
    all_to_all x1, blocking collectives, on_device(): got = lax.all_to_all(msg, 'tm', 0, 0)  16.3 us
    all_to_all x1, blocking collectives, on_device(): back = lax.all_to_all(fields, 'tm', 0, 0)  14.6 us
    ppermute x9, starting transfers between devices, swap(): return lax.ppermute(value, axis, [(s, s ^ bit) for s in range(count)])  9.58 us
    ppermute x9, waiting for transfers between devices, swap(): return lax.ppermute(value, axis, [(s, s ^ bit) for s in range(count)])  6.36 us
    all_to_all x1, waiting for transfers between devices, on_device(): winds = lax.all_to_all(wind, ('tm', 'rows'), 0, 0)  5.53 us
    pallas_call x1, Pallas kernels, on_device(): pl.pallas_call(functools.partial(grad_kernel, n_rows, halo, slot), out_sh...  4.22 us
    all_to_all x1, starting transfers between devices, on_device(): winds = lax.all_to_all(wind, ('tm', 'rows'), 0, 0)  2.46 us
    unnamed x12, local copies, waits for them, and re-layouts  2.42 us
  transfers between devices with their start and end apart: 11, of which 5 were waited for; matrix products, arithmetic and copies ran while one was open for 2% of the time, Pallas kernels for 2%

profile of v2, /device:TPU:0, one launch (start us, length us, event | category | flops | bytes accessed | tf_op | source)
XLA Modules:
  0.0 71.3 jit_solution(5554294317477447216)
XLA Ops:
  0.6 0.0 copy-start
  0.6 0.6 collective-permute-start.6
  1.2 2.6 %collective-permute-start.7 = (bf16[2,2,64,256]{3,2,1,0:T(8,128)(2,1)}, bf16[2,2,64,256]{3,2,1,0:T(8,128)(2,1)S(1)}, u32[]{:S(2)}, u32[]{:S(2)}) collective-permute-start(bf16[2,2,64,256]{3,2,1,0:T(8,128)(2,1)} %refs_4_.1), channel_id=1, source_target_pairs={{0,2},{1,3},{2,0},{3,1},{4,6},{5,7},{6,4},{7,5},{8,10},{9,11},{10,... | collective-permute-start | bytes 393224 | tf_op jit(solution)/shard_map/ppermute | solution.py:204
  3.8 1.0 %broadcast_compare_fusion = pred[128,512]{1,0:T(8,128)(4,1)S(1)} fusion(s32[128,512]{1,0:T(8,128)} %refs_9_.1), kind=kLoop, calls=%fused_computation.1 | loop fusion | flops 65536 | bytes 327680 | tf_op jit(solution)/shard_map/eq | solution.py:234
  4.7 0.0 copy-done
  4.8 0.0 copy-start.5
  4.8 0.0 copy-start.1
  4.8 0.0 copy-start.4
  4.8 0.1 collective-permute-start.4
  4.9 0.2 collective-permute-start.3
  5.1 0.3 copy-done.5
  5.4 0.1 reshape.8
  5.5 1.5 %collective-permute-start = (s32[4]{0:T(128)S(1)}, s32[4]{0:T(128)S(1)}, u32[]{:S(2)}, u32[]{:S(2)}) collective-permute-start(s32[4]{0:T(128)S(1)} %reshape.8), channel_id=1, source_target_pairs={{0,4},{4,0},{8,12},{12,8},{16,20},{20,16},{24,28},{28,24},{1,5},{5... | collective-permute-start | bytes 56 | tf_op jit(solution)/shard_map/ppermute | solution.py:204
  7.0 0.0 copy-done.1
  7.1 2.0 %collective-permute-done = s32[4]{0:T(128)S(1)} collective-permute-done((s32[4]{0:T(128)S(1)}, s32[4]{0:T(128)S(1)}, u32[]{:S(2)}, u32[]{:S(2)}) %collective-permute-start) | collective-permute-done | bytes 48 | tf_op jit(solution)/shard_map/ppermute | solution.py:204
  9.1 0.1 pad_add_fusion
  9.2 1.6 %collective-permute-start.1 = (s32[8]{0:T(128)S(1)}, s32[8]{0:T(128)S(1)}, u32[]{:S(2)}, u32[]{:S(2)}) collective-permute-start(s32[8]{0:T(128)S(1)} %pad_add_fusion), channel_id=1, source_target_pairs={{0,8},{4,12},{8,0},{12,4},{16,24},{20,28},{24,16},{28,20},{1,9},{5... | collective-permute-start | bytes 104 | tf_op jit(solution)/shard_map/ppermute | solution.py:204
  10.7 2.9 %collective-permute-done.4.refs_2_ = bf16[2,128,512]{2,1,0:T(8,128)(2,1)S(1)} collective-permute-done((bf16[2,128,512]{2,1,0:T(8,128)(2,1)S(1)}, bf16[2,128,512]{2,1,0:T(8,128)(2,1)S(1)}, u32[]{:S(2)}, u32[]{:S(2)}) %collective-permute-start.4) | collective-permute-done | bytes 262176 | tf_op jit(solution)/shard_map/ppermute | solution.py:204
  13.7 0.0 collective-permute-start.5
  13.7 0.0 collective-permute-done.1
  13.7 0.1 pad_add_fusion.1
  13.8 2.8 %collective-permute-start.2 = (s32[16]{0:T(128)S(1)}, s32[16]{0:T(128)S(1)}, u32[]{:S(2)}, u32[]{:S(2)}) collective-permute-start(s32[16]{0:T(128)S(1)} %pad_add_fusion.1), channel_id=1, source_target_pairs={{0,16},{4,20},{8,24},{12,28},{16,0},{20,4},{24,8},{28,12},{1,17},{... | collective-permute-start | bytes 200 | tf_op jit(solution)/shard_map/ppermute | solution.py:204
  16.6 0.0 collective-permute-done.7.refs_6_
  16.6 0.2 collective-permute-start.8
  16.8 1.4 %collective-permute-done.2 = s32[16]{0:T(128)S(1)} collective-permute-done((s32[16]{0:T(128)S(1)}, s32[16]{0:T(128)S(1)}, u32[]{:S(2)}, u32[]{:S(2)}) %collective-permute-start.2) | collective-permute-done | bytes 96 | tf_op jit(solution)/shard_map/ppermute | solution.py:204
  18.2 1.3 %collective-permute-start.9 = (bf16[32,512]{1,0:T(8,128)(2,1)S(1)}, bf16[32,512]{1,0:T(8,128)(2,1)S(1)}, u32[]{:S(2)}, u32[]{:S(2)}) collective-permute-start(bf16[32,512]{1,0:T(8,128)(2,1)S(1)} %pad_maximum_fusion), channel_id=1, source_target_pairs={{1,0},{2,1},{3,2},{5,4},{6,5},{7,6},{9,8},{10,9},{11,10},{13,12},{... | collective-permute-start | bytes 98312 | tf_op jit(solution)/shard_map/ppermute | solution.py:240
  19.5 0.1 pad_add_fusion.2.sh_ref
  19.6 1.7 %collective-permute-done.9.refs_10_.halo_ref = bf16[32,512]{1,0:T(8,128)(2,1)S(1)} collective-permute-done((bf16[32,512]{1,0:T(8,128)(2,1)S(1)}, bf16[32,512]{1,0:T(8,128)(2,1)S(1)}, u32[]{:S(2)}, u32[]{:S(2)}) %collective-permute-start.9) | collective-permute-done | bytes 32800 | tf_op jit(solution)/shard_map/ppermute | solution.py:240
  21.3 0.0 collective-permute-done.6.refs_5_
  21.3 0.0 collective-permute-done.8.refs_7_
  21.3 0.0 collective-permute-done.3.refs_1_
  21.3 0.0 collective-permute-done.5.refs_3_
  21.3 0.0 copy-done.4
  21.3 0.0 copy-start.2
  21.4 1.0 %copy-done.2 = bf16[528,512]{1,0:T(8,128)(2,1)S(1)} copy-done((bf16[528,512]{1,0:T(8,128)(2,1)S(1)}, bf16[528,512]{1,0:T(8,128)(2,1)}, u32[]{:S(2)}) %copy-start.2) | copy-done | bytes 540696
  22.4 0.0 copy-start.3
  22.4 1.0 %copy-done.3 = bf16[512,512]{1,0:T(8,128)(2,1)S(1)} copy-done((bf16[512,512]{1,0:T(8,128)(2,1)S(1)}, bf16[512,512]{1,0:T(8,128)(2,1)}, u32[]{:S(2)}) %copy-start.3) | copy-done | bytes 524312
  23.4 4.2 %grad.1 = (f32[2,128,512]{2,1,0:T(8,128)S(1)}, f32[8,72,128]{2,1,0:T(8,128)S(1)}, f32[2]{0:T(128)S(1)}) custom-call(s32[32]{0:T(128)S(1)} %pad_add_fusion.2.sh_ref, bf16[2,128,512]{2,1,0:T(8,128)(2,1)S(1)} %broadcast_select_fusion.refs_0_, bf16[2,128,512]{2,1,0:T(8,128)(2,1)S(1)} %collective-permute-done.3.refs_1_, ...), custom_call_target="tpu_custom_call" | custom-call | tf_op jit(solution)/shard_map/grad/pallas_call | solution.py:246
  27.7 16.3 %all_to_all.15.got_ref = f32[8,72,128]{2,1,0:T(8,128)S(1)} all-to-all(f32[8,72,128]{2,1,0:T(8,128)S(1)} %get-tuple-element.5), channel_id=1, replica_groups=mesh['tm'=8,'rows'=4] {'tm'}, dimensions={0} | all-to-all | bytes 589824 | tf_op jit(solution)/shard_map/all_to_all | solution.py:261
  44.0 0.7 %scan.1 = f32[8,72,128]{2,1,0:T(8,128)S(1)} custom-call(s32[32]{0:T(128)S(1)} %pad_add_fusion.2.sh_ref, f32[8,72,128]{2,1,0:T(8,128)S(1)} %all_to_all.15.got_ref), custom_call_target="tpu_custom_call" | custom-call | tf_op jit(solution)/shard_map/scan/pallas_call | solution.py:262
  44.7 14.6 %all_to_all.16.got_ref = f32[8,72,128]{2,1,0:T(8,128)S(1)} all-to-all(f32[8,72,128]{2,1,0:T(8,128)S(1)} %scan.1), channel_id=1, replica_groups=mesh['tm'=8,'rows'=4] {'tm'}, dimensions={0} | all-to-all | bytes 589824 | tf_op jit(solution)/shard_map/all_to_all | solution.py:270
  59.3 1.8 %wind.1 = f32[32,1,128]{2,1,0:T(1,128)} custom-call(s32[32]{0:T(128)S(1)} %pad_add_fusion.2.sh_ref, f32[2]{0:T(128)S(1)} %get-tuple-element.7.wind_in, f32[8,72,128]{2,1,0:T(8,128)S(1)} %all_to_all.16.got_ref, bf16[2,128,512]{2,1,0:T(8,128)(2,1)S(1)} %copy-done, bf16[32,512]{1,0:T(8,128)(2,1)S(1)} %collective-permute-done.9.refs_10_.halo_ref), custom_call_target="tpu_custom_call" | custom-call | tf_op jit(solution)/shard_map/wind/pallas_call | solution.py:273
  61.1 2.5 %all-to-all-start.2 = ((f32[32,1,128]{2,1,0:T(1,128)}), f32[32,1,128]{2,1,0:T(1,128)S(1)}, u32[]{:S(2)}, u32[]{:S(2)}) async-start(f32[32,1,128]{2,1,0:T(1,128)} %wind.1), calls=%async_computation.2 | async-start | bytes 32768 | tf_op jit(solution)/shard_map/all_to_all | solution.py:282
  63.6 1.6 %final.1 = f32[2,128,512]{2,1,0:T(8,128)} custom-call(s32[32]{0:T(128)S(1)} %pad_add_fusion.2.sh_ref, f32[8,72,128]{2,1,0:T(8,128)S(1)} %all_to_all.16.got_ref, f32[2,128,512]{2,1,0:T(8,128)S(1)} %get-tuple-element.6.loc_ref), custom_call_target="tpu_custom_call" | custom-call | flops 737280 | bytes 1572864 | tf_op jit(solution)/shard_map/final/pallas_call | solution.py:283
  65.2 5.5 %all-to-all-done.2 = f32[32,1,128]{2,1,0:T(1,128)S(1)} async-done(((f32[32,1,128]{2,1,0:T(1,128)}), f32[32,1,128]{2,1,0:T(1,128)S(1)}, u32[]{:S(2)}, u32[]{:S(2)}) %all-to-all-start.2) | async-done | bytes 16416 | tf_op jit(solution)/shard_map/all_to_all | solution.py:282
  70.8 0.1 slice_reduce_fusion
  70.8 0.5 negate_multiply_fusion
  (4 shorter events, 0.0 us)
Async XLA Ops:
  0.6 4.1 %copy-start = (bf16[2,128,512]{2,1,0:T(8,128)(2,1)S(1)}, bf16[2,128,512]{2,1,0:T(8,128)(2,1)}, u32[]{:S(2)}) copy-start(bf16[2,128,512]{2,1,0:T(8,128)(2,1)} %phases_ref.1) | copy-start | bytes 786436
  0.6 20.7 %collective-permute-start.6 = (bf16[2,2,64,256]{3,2,1,0:T(8,128)(2,1)}, bf16[2,2,64,256]{3,2,1,0:T(8,128)(2,1)S(1)}, u32[]{:S(2)}, u32[]{:S(2)}) collective-permute-start(bf16[2,2,64,256]{3,2,1,0:T(8,128)(2,1)} %refs_4_.1), channel_id=1, source_target_pairs={{0,1},{1,0},{2,3},{3,2},{4,5},{5,4},{6,7},{7,6},{8,9},{9,8},{10,11... | collective-permute-start | bytes 393224 | tf_op jit(solution)/shard_map/ppermute | solution.py:204
  1.2 15.4 %collective-permute-start.7 = (bf16[2,2,64,256]{3,2,1,0:T(8,128)(2,1)}, bf16[2,2,64,256]{3,2,1,0:T(8,128)(2,1)S(1)}, u32[]{:S(2)}, u32[]{:S(2)}) collective-permute-start(bf16[2,2,64,256]{3,2,1,0:T(8,128)(2,1)} %refs_4_.1), channel_id=1, source_target_pairs={{0,2},{1,3},{2,0},{3,1},{4,6},{5,7},{6,4},{7,5},{8,10},{9,11},{10,... | collective-permute-start | bytes 393224 | tf_op jit(solution)/shard_map/ppermute | solution.py:204
  4.8 0.7 copy-start.5
  4.8 2.3 %copy-start.1 = (s32[128,512]{1,0:T(8,128)S(1)}, s32[128,512]{1,0:T(8,128)}, u32[]{:S(2)}) copy-start(s32[128,512]{1,0:T(8,128)} %refs_9_.1) | copy-start | bytes 786436
  4.8 16.5 %copy-start.4 = (bf16[2,2,64,256]{3,2,1,0:T(8,128)(2,1)S(1)}, bf16[2,2,64,256]{3,2,1,0:T(8,128)(2,1)}, u32[]{:S(2)}) copy-start(bf16[2,2,64,256]{3,2,1,0:T(8,128)(2,1)} %refs_4_.1) | copy-start | bytes 393220
  4.8 8.8 %collective-permute-start.4 = (bf16[2,128,512]{2,1,0:T(8,128)(2,1)S(1)}, bf16[2,128,512]{2,1,0:T(8,128)(2,1)S(1)}, u32[]{:S(2)}, u32[]{:S(2)}) collective-permute-start(bf16[2,128,512]{2,1,0:T(8,128)(2,1)S(1)} %broadcast_select_fusion.refs_0_), channel_id=1, source_target_pairs={{0,2},{1,3},{2,0},{3,1},{4,6},{5,7},{6,4},{7,5},{8,10},{9,11},{10,... | collective-permute-start | bytes 786440 | tf_op jit(solution)/shard_map/ppermute | solution.py:204
  4.9 16.4 %collective-permute-start.3 = (bf16[2,128,512]{2,1,0:T(8,128)(2,1)S(1)}, bf16[2,128,512]{2,1,0:T(8,128)(2,1)S(1)}, u32[]{:S(2)}, u32[]{:S(2)}) collective-permute-start(bf16[2,128,512]{2,1,0:T(8,128)(2,1)S(1)} %broadcast_select_fusion.refs_0_), channel_id=1, source_target_pairs={{0,1},{1,0},{2,3},{3,2},{4,5},{5,4},{6,7},{7,6},{8,9},{9,8},{10,11... | collective-permute-start | bytes 786440 | tf_op jit(solution)/shard_map/ppermute | solution.py:204
  5.5 3.6 %collective-permute-start = (s32[4]{0:T(128)S(1)}, s32[4]{0:T(128)S(1)}, u32[]{:S(2)}, u32[]{:S(2)}) collective-permute-start(s32[4]{0:T(128)S(1)} %reshape.8), channel_id=1, source_target_pairs={{0,4},{4,0},{8,12},{12,8},{16,20},{20,16},{24,28},{28,24},{1,5},{5... | collective-permute-start | bytes 56 | tf_op jit(solution)/shard_map/ppermute | solution.py:204
  9.2 4.5 %collective-permute-start.1 = (s32[8]{0:T(128)S(1)}, s32[8]{0:T(128)S(1)}, u32[]{:S(2)}, u32[]{:S(2)}) collective-permute-start(s32[8]{0:T(128)S(1)} %pad_add_fusion), channel_id=1, source_target_pairs={{0,8},{4,12},{8,0},{12,4},{16,24},{20,28},{24,16},{28,20},{1,9},{5... | collective-permute-start | bytes 104 | tf_op jit(solution)/shard_map/ppermute | solution.py:204
  13.7 7.7 %collective-permute-start.5 = (bf16[2,128,512]{2,1,0:T(8,128)(2,1)S(1)}, bf16[2,128,512]{2,1,0:T(8,128)(2,1)S(1)}, u32[]{:S(2)}, u32[]{:S(2)}) collective-permute-start(bf16[2,128,512]{2,1,0:T(8,128)(2,1)S(1)} %collective-permute-done.4.refs_2_), channel_id=1, source_target_pairs={{0,1},{1,0},{2,3},{3,2},{4,5},{5,4},{6,7},{7,6},{8,9},{9,8},{10,11... | collective-permute-start | bytes 786440 | tf_op jit(solution)/shard_map/ppermute | solution.py:204
  13.8 4.5 %collective-permute-start.2 = (s32[16]{0:T(128)S(1)}, s32[16]{0:T(128)S(1)}, u32[]{:S(2)}, u32[]{:S(2)}) collective-permute-start(s32[16]{0:T(128)S(1)} %pad_add_fusion.1), channel_id=1, source_target_pairs={{0,16},{4,20},{8,24},{12,28},{16,0},{20,4},{24,8},{28,12},{1,17},{... | collective-permute-start | bytes 200 | tf_op jit(solution)/shard_map/ppermute | solution.py:204
  16.6 4.7 %collective-permute-start.8 = (bf16[2,2,64,256]{3,2,1,0:T(8,128)(2,1)S(1)}, bf16[2,2,64,256]{3,2,1,0:T(8,128)(2,1)S(1)}, u32[]{:S(2)}, u32[]{:S(2)}) collective-permute-start(bf16[2,2,64,256]{3,2,1,0:T(8,128)(2,1)S(1)} %collective-permute-done.7.refs_6_), channel_id=1, source_target_pairs={{0,1},{1,0},{2,3},{3,2},{4,5},{5,4},{6,7},{7,6},{8,9},{9,8},{10,11... | collective-permute-start | bytes 393224 | tf_op jit(solution)/shard_map/ppermute | solution.py:204
  18.2 3.1 %collective-permute-start.9 = (bf16[32,512]{1,0:T(8,128)(2,1)S(1)}, bf16[32,512]{1,0:T(8,128)(2,1)S(1)}, u32[]{:S(2)}, u32[]{:S(2)}) collective-permute-start(bf16[32,512]{1,0:T(8,128)(2,1)S(1)} %pad_maximum_fusion), channel_id=1, source_target_pairs={{1,0},{2,1},{3,2},{5,4},{6,5},{7,6},{9,8},{10,9},{11,10},{13,12},{... | collective-permute-start | bytes 98312 | tf_op jit(solution)/shard_map/ppermute | solution.py:240
  21.3 1.1 %copy-start.2 = (bf16[528,512]{1,0:T(8,128)(2,1)S(1)}, bf16[528,512]{1,0:T(8,128)(2,1)}, u32[]{:S(2)}) copy-start(bf16[528,512]{1,0:T(8,128)(2,1)} %constant.13.clone.refs_11_) | copy-start | bytes 1622020
  22.4 1.0 %copy-start.3 = (bf16[512,512]{1,0:T(8,128)(2,1)S(1)}, bf16[512,512]{1,0:T(8,128)(2,1)}, u32[]{:S(2)}) copy-start(bf16[512,512]{1,0:T(8,128)(2,1)} %constant.14.clone.refs_12_) | copy-start | bytes 1572868
  61.1 9.6 %all-to-all-start.2 = ((f32[32,1,128]{2,1,0:T(1,128)}), f32[32,1,128]{2,1,0:T(1,128)S(1)}, u32[]{:S(2)}, u32[]{:S(2)}) async-start(f32[32,1,128]{2,1,0:T(1,128)} %wind.1), calls=%async_computation.2 | async-start | bytes 32768 | tf_op jit(solution)/shard_map/all_to_all | solution.py:282

commit v3 on v2

--- a/solution.py
+++ b/solution.py
@@ -52,69 +52,140 @@
     return lax.broadcasted_iota(jnp.int32, shape, 1)
 
 
-def grad_kernel(
-    n_rows, halo, slot, sh_ref, *refs
-):
+def y_kernel(halo, phases_ref, mask_ref, half_ref, *refs):
+    count = (len(refs) - 2) // 2
+    y_ref = refs[count]
+    copies = [
+        pltpu.make_async_copy(refs[i], refs[count + 1 + i], refs[-1].at[i]) for i in range(count)
+    ]
+    for copy in copies:
+        copy.start()
+    frames, block, width = phases_ref.shape
+    focal = y_ref.shape[1]
+    parts = width // focal
+    live = mask_ref[...] == 1
+    zero_freq = jnp.full((16, width), zero_freq_value(width), jnp.bfloat16)
+    row = lax.broadcasted_iota(jnp.int32, (16, block), 0)
+    rows = lax.broadcasted_iota(jnp.int32, (16, focal), 0)
+    dc = jnp.zeros((16, block), jnp.float32)
+    edge = jnp.zeros((16, focal), jnp.float32)
+    for k in range(frames):
+        masked = jnp.where(live, phases_ref[k].astype(jnp.float32), 0.0).astype(jnp.bfloat16)
+        y_ref[k * block : (k + 1) * block] = dot(masked, half_ref[...]).astype(jnp.bfloat16)
+        dc = jnp.where(row == k, dot_t(zero_freq, masked), dc)
+        top = phases_ref[k, :8].astype(jnp.float32)[:1]
+        for i in range(parts):
+            here = jnp.broadcast_to(top[:, i * focal : (i + 1) * focal], edge.shape)
+            edge = jnp.where(rows == frames + k * parts + i, here, edge)
+    at = frames * block
+    y_ref[at : at + 16] = edge.astype(jnp.bfloat16)
+    y_ref[at : at + 16, :block] = (edge[:, :block] + dc).astype(jnp.bfloat16)
+    at = at + 16
+    mask = mask_ref[:halo].astype(jnp.float32).astype(jnp.bfloat16)
+    for i in range(parts):
+        y_ref[at + i * halo : at + (i + 1) * halo] = mask[:, i * focal : (i + 1) * focal]
+    for copy in copies:
+        copy.wait()
+
+
+def zero_freq_value(width):
+    return float(np.float32(np.float32(1.0 / math.sqrt(width)).astype(jnp.bfloat16)))
+
+
+def dot_t(a, b):
+    return lax.dot_general(a, b, (((1,), (1,)), ((), ())), preferred_element_type=jnp.float32)
+
+
+def grad_kernel(n_rows, halo, *refs):
     m_refs, d_refs = refs[:n_rows], refs[n_rows : 2 * n_rows]
-    phases_ref, mask_ref, halo_ref, tt_ref, cs_ref = refs[2 * n_rows : 2 * n_rows + 5]
-    loc_ref, msg_ref, wind_ref = refs[2 * n_rows + 5 : 2 * n_rows + 8]
-    y_ref, d_ref, r_ref, w_ref, lam_ref = refs[2 * n_rows + 8 :]
-    frames, block, width = phases_ref.shape
+    mask_ref, tt_ref, cs_ref, turned_ref, flip_ref = refs[2 * n_rows : 2 * n_rows + 5]
+    g_ref, next_ref = refs[2 * n_rows + 5 : 2 * n_rows + 7]
+    y_ref, dc_ref, d_ref, r_ref, w_ref, over_ref = refs[2 * n_rows + 7 :]
+    frames = w_ref.shape[0]
+    block, width = mask_ref.shape
     focal = cs_ref.shape[0] // 2
+    parts = width // focal
+    half = focal // 2
     part = focal // n_rows
     rows = block + halo
     me = lax.axis_index("rows")
-    tm = lax.axis_index("tm")
+    over_ref[...] = jnp.zeros_like(over_ref)
+    next_ref[...] = jnp.zeros_like(next_ref)
+    for d in range(1, n_rows):
+
+        @pl.when((me ^ d) == me + 1)
+        def _():
+            at = frames * block
+            edge = m_refs[d][at : at + 16].astype(jnp.float32)
+            for k in range(frames):
+                for i in range(parts):
+                    line = frames + k * parts + i
+                    next_ref[k : k + 1, i * focal : (i + 1) * focal] = edge[line : line + 1]
+            at = at + 16
+            for i in range(parts):
+                over_ref[:, i * focal : (i + 1) * focal] = m_refs[d][
+                    at + i * halo : at + (i + 1) * halo
+                ].astype(jnp.float32)
+
     for d in range(n_rows):
         at = pl.multiple_of((me ^ d) * block, block)
-        y = dot(m_refs[d][...].reshape(frames * block, width), tt_ref[:width])
-        y = y.astype(jnp.bfloat16)
         at_q = pl.multiple_of((me ^ d) * part, part)
         for k in range(frames):
-            y_ref[k, pl.ds(at, block), :] = y[k * block : (k + 1) * block]
+            y_ref[k, pl.ds(at, block), :] = m_refs[d][k * block : (k + 1) * block]
             d_ref[k, :, pl.ds(at_q, part), :] = d_refs[d][k]
+        dc_ref[:, pl.ds(at, block)] = m_refs[d][frames * block : frames * block + 16, :block]
+    dc = dot_t(cs_ref[...], dc_ref[...])
+    first = columns((focal, half)) == 0
     for k in range(frames):
         pq = dot(cs_ref[...], y_ref[k])
-        e_real = pq[:focal, :focal] - pq[focal:, focal:]
-        e_imag = pq[:focal, focal:] + pq[focal:, :focal]
-        real = (d_ref[k, 0].astype(jnp.float32) - e_real).astype(jnp.bfloat16)
-        imag = (d_ref[k, 1].astype(jnp.float32) - e_imag).astype(jnp.bfloat16)
-        r_ref[:focal, :focal] = real
-        r_ref[:focal, focal:] = imag
-        r_ref[focal:, :focal] = imag
-        r_ref[focal:, focal:] = -real
+        c_real, c_imag = pq[:focal, :half], pq[:focal, half:]
+        s_real, s_imag = pq[focal:, :half], pq[focal:, half:]
+        e_real = (c_real - s_imag, jnp.where(first, dc[:focal, k : k + 1], c_real + s_imag))
+        e_imag = (c_imag + s_real, jnp.where(first, dc[focal:, k : k + 1], s_real - c_imag))
+        for i in range(2):
+            at = slice(i * half, (i + 1) * half)
+            real, imag = d_ref[k, 0, :, at], d_ref[k, 1, :, at]
+            if i:
+                real, imag = dot(real, flip_ref[...]), dot(imag, flip_ref[...])
+            real = (real.astype(jnp.float32) - e_real[i]).astype(jnp.bfloat16)
+            imag = (imag.astype(jnp.float32) - e_imag[i]).astype(jnp.bfloat16)
+            r_ref[:focal, i * half : (i + 1) * half] = real
+            r_ref[:focal, focal + i * half : focal + (i + 1) * half] = imag
+            r_ref[focal:, i * half : (i + 1) * half] = imag
+            r_ref[focal:, focal + i * half : focal + (i + 1) * half] = -real
         rows_t = tt_ref[pl.ds(pl.multiple_of(me * block, block), rows), :]
         w_ref[k] = dot(rows_t, r_ref[...]).astype(jnp.bfloat16)
     live = mask_ref[...] == 1
-    live_halo = halo_ref[:halo].astype(jnp.float32) == 1.0
+    live_over = over_ref[...] == 1.0
+    for k in range(frames):
+        g = dot(w_ref[k], turned_ref[...])
+        g_ref[k, :block] = jnp.where(live, g[:block], 0.0)
+        g_ref[k, block:] = jnp.where(live_over, g[block:], 0.0)
+
+
+def segment_kernel(slot, sh_ref, g_ref, phases_ref, next_ref, loc_ref, msg_ref, wind_ref):
+    frames, rows, width = g_ref.shape
+    block = phases_ref.shape[1]
+    halo = rows - block
     col = columns((rows, width))
     row = lax.broadcasted_iota(jnp.int32, (rows, width), 0)
     down_sum = jnp.float32(0.0)
     side_sum = jnp.float32(0.0)
-    for k in reversed(range(frames)):
-        g = dot(w_ref[k], cs_ref[...])
-        own = jnp.where(live, g[:block], 0.0)
-        over = jnp.where(live_halo, g[block:], 0.0)
-        if k == frames - 1:
-            loc_ref[k] = own
-            lam_ref[:block] = own
-            lam_ref[block:] = over
-        else:
-            a, b = sh_ref[2 * k], sh_ref[2 * k + 1]
-            moved = turned(lam_ref[...], rows - a, width - b)
-            inside = (col < width - b) & (row < rows - a)
-            prior = jnp.where(inside, decay_rate * moved, 0.0)
-            down, side = diffs(phases_ref, halo_ref, halo, k)
-            down_sum = down_sum + jnp.sum(prior[:block] * down)
-            side_sum = side_sum + jnp.sum(prior[:block] * side)
-            own = own + prior[:block]
-            loc_ref[k] = own
-            lam_ref[:block] = own
-            lam_ref[block:] = over + prior[block:]
+    lam = g_ref[frames - 1]
+    loc_ref[frames - 1] = lam[:block]
+    for k in reversed(range(frames - 1)):
+        a, b = sh_ref[2 * k], sh_ref[2 * k + 1]
+        inside = (col < width - b) & (row < rows - a)
+        prior = jnp.where(inside, decay_rate * turned(lam, rows - a, width - b), 0.0)
+        down, side = diffs(phases_ref, next_ref, k)
+        down_sum = down_sum + jnp.sum(prior[:block] * down)
+        side_sum = side_sum + jnp.sum(prior[:block] * side)
+        lam = g_ref[k] + prior
+        loc_ref[k] = lam[:block]
     wind_ref[0] = down_sum
     wind_ref[1] = side_sum
-    a_cum, b_cum = cum_shifts(sh_ref, frames, tm)
-    canvas = turned(lam_ref[...], halo - a_cum, width - lax.rem(b_cum, width))
+    a_cum, b_cum = cum_shifts(sh_ref, frames, lax.axis_index("tm"))
+    canvas = turned(lam, halo - a_cum, width - lax.rem(b_cum, width))
     canvas = jnp.where(row >= halo - a_cum, canvas, 0.0)
     per = rows // slot
     for j in range(msg_ref.shape[0]):
@@ -126,10 +197,10 @@
             msg_ref[j] = jnp.zeros((slot, LANES), jnp.float32)
 
 
-def diffs(phases_ref, halo_ref, halo, k):
+def diffs(phases_ref, next_ref, k):
     frames, block, width = phases_ref.shape
     here = phases_ref[k].astype(jnp.float32)
-    last = halo_ref[halo + 8 * k : halo + 8 * k + 8].astype(jnp.float32)[:1]
+    last = next_ref[k : k + 1]
     row = lax.broadcasted_iota(jnp.int32, (block, width), 0)
     below = jnp.where(row == block - 1, last, pltpu.roll(here, block - 1, 0))
     right = jnp.where(columns((block, width)) == width - 1, 0.0, pltpu.roll(here, width - 1, 1))
@@ -181,12 +252,12 @@
         yield k, jnp.where(col < width - b_own, decay_rate ** (frames - k) * moved, 0.0)
 
 
-def wind_kernel(halo, sh_ref, wind_in, got_ref, phases_ref, halo_ref, wind_ref, c_ref):
+def wind_kernel(halo, sh_ref, wind_in, got_ref, phases_ref, next_ref, wind_ref, c_ref):
     frames, block, width = phases_ref.shape
     down_sum = wind_in[0]
     side_sum = wind_in[1]
     for k, moved in carried(halo, frames, block, width, sh_ref, got_ref, c_ref):
-        down, side = diffs(phases_ref, halo_ref, halo, k)
+        down, side = diffs(phases_ref, next_ref, k)
         down_sum = down_sum + jnp.sum(moved * down)
         side_sum = side_sum + jnp.sum(moved * side)
     lane = lax.broadcasted_iota(jnp.int32, wind_ref.shape, 2)
@@ -224,40 +295,67 @@
     halo = -(-halo // 16) * 16
     rows = block + halo
     slot = max(1, rows * (width // LANES) // n_tm)
+    half = focal // 2
     cs = tables(width, focal)
     tt = np.concatenate([cs.T, np.zeros((halo, 2 * focal), cs.dtype)], axis=0)
+    order = np.concatenate([np.arange(half), half + (half - np.arange(half)) % half])
+    cs_turned = np.concatenate([cs[order], cs[focal + order]], axis=0)
+    y_table = np.concatenate([cs[:half], cs[focal : focal + half]], axis=0).T
+    flip = np.zeros((half, half), cs.dtype)
+    flip[(half - np.arange(half)) % half, np.arange(half)] = 1
     sh_all = shifts.reshape(2 * frames)
     bit = 1
     while bit < n_tm:
         sh_all = jnp.concatenate([sh_all, swap(sh_all, "tm", bit)])
         bit *= 2
-    masked = jnp.where((pupil_mask == 1)[None], phases, jnp.zeros_like(phases))
-    m_parts = gather_rows(masked)
-    d_parts = gather_rows(focal_data)
-    outgoing = jnp.concatenate(
-        [pupil_mask[:halo].astype(jnp.bfloat16)] + [phases[k, :8] for k in range(frames)], axis=0
-    )
-    incoming = lax.ppermute(outgoing, "rows", [(s, s - 1) for s in range(1, n_rows)])
     vmem = pl.BlockSpec(memory_space=pltpu.VMEM)
     smem = pl.BlockSpec(memory_space=pltpu.SMEM)
+    hbm = pl.BlockSpec(memory_space=pltpu.HBM)
+    kept = [tt, cs, cs_turned, flip]
+    y, *kept = pl.pallas_call(
+        functools.partial(y_kernel, halo),
+        out_shape=[
+            jax.ShapeDtypeStruct((frames * block + 16 + halo * width // focal, focal), jnp.bfloat16)
+        ]
+        + [jax.ShapeDtypeStruct(t.shape, jnp.bfloat16) for t in kept],
+        in_specs=[vmem] * 3 + [hbm] * len(kept),
+        out_specs=[vmem] * (1 + len(kept)),
+        scratch_shapes=[pltpu.SemaphoreType.DMA((len(kept),))],
+        compiler_params=pltpu.CompilerParams(vmem_limit_bytes=8 << 20),
+        name="transform",
+    )(*[pltpu.with_memory_space_constraint(t, pltpu.HBM) for t in (phases, pupil_mask, y_table, *kept)])
+    d_parts = gather_rows(focal_data)
+    m_parts = gather_rows(y)
     field = jax.ShapeDtypeStruct((frames, block, width), jnp.float32)
     message = jax.ShapeDtypeStruct((n_tm, slot, LANES), jnp.float32)
     pair = jax.ShapeDtypeStruct((2,), jnp.float32)
-    loc, msg, wind_local = pl.pallas_call(
-        functools.partial(grad_kernel, n_rows, halo, slot),
-        out_shape=(field, message, pair),
-        in_specs=[smem] + [vmem] * (2 * n_rows + 5),
-        out_specs=(vmem, vmem, smem),
+    grads, next_rows = pl.pallas_call(
+        functools.partial(grad_kernel, n_rows, halo),
+        out_shape=(
+            jax.ShapeDtypeStruct((frames, rows, width), jnp.float32),
+            jax.ShapeDtypeStruct((-(-frames // 8) * 8, width), jnp.float32),
+        ),
+        in_specs=[vmem] * (2 * n_rows + 5),
+        out_specs=(vmem, vmem),
         scratch_shapes=[
-            pltpu.VMEM((frames, width, 2 * focal), jnp.bfloat16),
+            pltpu.VMEM((frames, width, focal), jnp.bfloat16),
+            pltpu.VMEM((16, width), jnp.bfloat16),
             pltpu.VMEM((frames, 2, focal, focal), jnp.bfloat16),
             pltpu.VMEM((2 * focal, 2 * focal), jnp.bfloat16),
             pltpu.VMEM((frames, rows, 2 * focal), jnp.bfloat16),
-            pltpu.VMEM((rows, width), jnp.float32),
+            pltpu.VMEM((halo, width), jnp.float32),
         ],
-        compiler_params=pltpu.CompilerParams(vmem_limit_bytes=28 << 20),
+        compiler_params=pltpu.CompilerParams(vmem_limit_bytes=24 << 20),
         name="grad",
-    )(sh_all, *m_parts, *d_parts, phases, pupil_mask, incoming, tt, cs)
+    )(*m_parts, *d_parts, pupil_mask, *kept)
+    loc, msg, wind_local = pl.pallas_call(
+        functools.partial(segment_kernel, slot),
+        out_shape=(field, message, pair),
+        in_specs=[smem, vmem, vmem, vmem],
+        out_specs=(vmem, vmem, smem),
+        compiler_params=pltpu.CompilerParams(vmem_limit_bytes=12 << 20),
+        name="segment",
+    )(sh_all, grads, phases, next_rows)
     got = lax.all_to_all(msg, "tm", 0, 0)
     fields = pl.pallas_call(
         functools.partial(scan_kernel, frames, rows, width),
@@ -278,7 +376,7 @@
         scratch_shapes=[canvas],
         compiler_params=pltpu.CompilerParams(vmem_limit_bytes=8 << 20),
         name="wind",
-    )(sh_all, wind_local, back, phases, incoming)
+    )(sh_all, wind_local, back, phases, next_rows)
     winds = lax.all_to_all(wind, ("tm", "rows"), 0, 0)
     adjoint = pl.pallas_call(
         functools.partial(final_kernel, halo),

time: 71.7 us -> 61.4 us (0.86)
  blocking collectives: 30.9 us -> 26.1 us
  waiting for transfers between devices: 13.6 us -> 9.72 us
  local copies, waits for them, and re-layouts: 2.51 us -> 0.1 us
  Pallas kernels: 8.41 us -> 9.83 us
  other arithmetic: 1.82 us -> 0.79 us
    all_to_all x1, blocking collectives: 14.6 us -> 11.3 us  [on_device(): back = lax.all_to_all(fields, 'tm', 0, 0)]
    unnamed x12 -> x8, local copies, waits for them, and re-layouts: 2.42 us -> 0.02 us
    ppermute x9, waiting for transfers between devices: 6.36 us -> 4.19 us  [swap(): return lax.ppermute(value, axis, [(s, s ^ bit) for s in range(count)])]
    ppermute x1 -> x0, waiting for transfers between devices: 1.72 us -> none  [on_device(): lax.ppermute(outgoing, 'rows', [(s, s - 1) for s in range(1, n_rows)])]
    ppermute x9, starting transfers between devices: 9.58 us -> 11.2 us  [swap(): return lax.ppermute(value, axis, [(s, s ^ bit) for s in range(count)])]
    all_to_all x1, blocking collectives: 16.3 us -> 14.8 us  [on_device(): got = lax.all_to_all(msg, 'tm', 0, 0)]
    pallas_call x1 -> x3, Pallas kernels: 4.22 us -> 5.66 us  [the longest x1 2.59 us: on_device(): pl.pallas_call(functools.partial(y_kernel, halo), out_shape=[jax.ShapeDty...]
    ppermute x1 -> x0, starting transfers between devices: 1.28 us -> none  [on_device(): lax.ppermute(outgoing, 'rows', [(s, s - 1) for s in range(1, n_rows)])]
  transfers between devices with their start and end apart: 11 -> 10, of which waited for: 5 -> 5; matrix products, arithmetic and copies ran while one was open for 2% -> 1% of each run, Pallas kernels for 2% -> 3%
where the time goes in v3:
time: 61.4 us; the launch traced here: 61.2 us
  blocking collectives  26.1 us (43%)
  starting transfers between devices  13.9 us (23%)
  Pallas kernels  9.83 us (16%)
  waiting for transfers between devices  9.72 us (16%)
  other arithmetic  0.79 us (1%)
  between operations  0.74 us (1%)
    all_to_all x1, blocking collectives, on_device(): got = lax.all_to_all(msg, 'tm', 0, 0)  14.8 us
    all_to_all x1, blocking collectives, on_device(): back = lax.all_to_all(fields, 'tm', 0, 0)  11.3 us
    ppermute x9, starting transfers between devices, swap(): return lax.ppermute(value, axis, [(s, s ^ bit) for s in range(count)])  11.2 us
    all_to_all x1, waiting for transfers between devices, on_device(): winds = lax.all_to_all(wind, ('tm', 'rows'), 0, 0)  5.52 us
    ppermute x9, waiting for transfers between devices, swap(): return lax.ppermute(value, axis, [(s, s ^ bit) for s in range(count)])  4.19 us
    all_to_all x1, starting transfers between devices, on_device(): winds = lax.all_to_all(wind, ('tm', 'rows'), 0, 0)  2.73 us
    pallas_call x1, Pallas kernels, on_device(): pl.pallas_call(functools.partial(y_kernel, halo), out_shape=[jax.ShapeDty...  2.59 us
    pallas_call x1, Pallas kernels, on_device(): pl.pallas_call(functools.partial(wind_kernel, halo), out_shape=jax.ShapeD...  1.79 us
  transfers between devices with their start and end apart: 10, of which 5 were waited for; matrix products, arithmetic and copies ran while one was open for 1% of the time, Pallas kernels for 3%

profile of v3, /device:TPU:0, one launch (start us, length us, event | category | flops | bytes accessed | tf_op | source)
XLA Modules:
  0.0 61.2 jit_solution(3081389150672111387)
XLA Ops:
  0.6 0.0 copy-start.1
  0.6 0.0 copy-start.2
  0.6 2.6 %transform.1 = (bf16[304,256]{1,0:T(8,128)(2,1)S(1)}, bf16[528,512]{1,0:T(8,128)(2,1)S(1)}, bf16[512,512]{1,0:T(8,128)(2,1)S(1)}, bf16[512,512]{1,0:T(8,128)(2,1)S(1)}, bf16[128,128]{1,0:T(8,128)(2,1)S(1)}) custom-call(bf16[2,128,512]{2,1,0:T(8,128)(2,1)} %phases_ref.5, s32[128,512]{1,0:T(8,128)} %refs_8_.1, bf16[512,256]{1,0:T(8,128)(2,1)} %constant.15.clone.half_ref, ...), custom_call_target="tpu_custom_call" | custom-call | tf_op jit(solution)/shard_map/transform/pallas_call | solution.py:315
  3.2 0.0 copy-start.3
  3.3 3.0 %collective-permute-start.4 = (bf16[304,256]{1,0:T(8,128)(2,1)S(1)}, bf16[304,256]{1,0:T(8,128)(2,1)S(1)}, u32[]{:S(2)}, u32[]{:S(2)}) collective-permute-start(bf16[304,256]{1,0:T(8,128)(2,1)S(1)} %get-tuple-element.12.refs_0_), channel_id=1, source_target_pairs={{0,2},{1,3},{2,0},{3,1},{4,6},{5,7},{6,4},{7,5},{8,10},{9,11},{10,... | collective-permute-start | bytes 466952 | tf_op jit(solution)/shard_map/ppermute | solution.py:275
  6.3 0.0 copy-done.2
  6.3 0.1 collective-permute-start.7
  6.4 0.0 collective-permute-start.3
  6.4 0.5 collective-permute-start.6
  6.9 0.0 copy-done.3
  6.9 0.1 reshape.7
  7.0 2.0 %collective-permute-start = (s32[4]{0:T(128)S(1)}, s32[4]{0:T(128)S(1)}, u32[]{:S(2)}, u32[]{:S(2)}) collective-permute-start(s32[4]{0:T(128)S(1)} %reshape.7), channel_id=1, source_target_pairs={{0,4},{4,0},{8,12},{12,8},{16,20},{20,16},{24,28},{28,24},{1,5},{5... | collective-permute-start | bytes 56 | tf_op jit(solution)/shard_map/ppermute | solution.py:275
  8.9 1.6 %collective-permute-done = s32[4]{0:T(128)S(1)} collective-permute-done((s32[4]{0:T(128)S(1)}, s32[4]{0:T(128)S(1)}, u32[]{:S(2)}, u32[]{:S(2)}) %collective-permute-start) | collective-permute-done | bytes 48 | tf_op jit(solution)/shard_map/ppermute | solution.py:275
  10.5 0.1 pad_add_fusion
  10.6 2.0 %collective-permute-start.1 = (s32[8]{0:T(128)S(1)}, s32[8]{0:T(128)S(1)}, u32[]{:S(2)}, u32[]{:S(2)}) collective-permute-start(s32[8]{0:T(128)S(1)} %pad_add_fusion), channel_id=1, source_target_pairs={{0,8},{4,12},{8,0},{12,4},{16,24},{20,28},{24,16},{28,20},{1,9},{5... | collective-permute-start | bytes 104 | tf_op jit(solution)/shard_map/ppermute | solution.py:275
  12.6 0.5 collective-permute-done.7.refs_6_
  13.1 0.0 collective-permute-start.8
  13.1 0.0 collective-permute-done.4.refs_2_
  13.1 0.5 collective-permute-start.5
  13.6 0.6 collective-permute-done.1
  14.2 0.1 pad_add_fusion.1
  14.3 3.0 %collective-permute-start.2 = (s32[16]{0:T(128)S(1)}, s32[16]{0:T(128)S(1)}, u32[]{:S(2)}, u32[]{:S(2)}) collective-permute-start(s32[16]{0:T(128)S(1)} %pad_add_fusion.1), channel_id=1, source_target_pairs={{0,16},{4,20},{8,24},{12,28},{16,0},{20,4},{24,8},{28,12},{1,17},{... | collective-permute-start | bytes 200 | tf_op jit(solution)/shard_map/ppermute | solution.py:275
  17.3 1.5 %collective-permute-done.2 = s32[16]{0:T(128)S(1)} collective-permute-done((s32[16]{0:T(128)S(1)}, s32[16]{0:T(128)S(1)}, u32[]{:S(2)}, u32[]{:S(2)}) %collective-permute-start.2) | collective-permute-done | bytes 96 | tf_op jit(solution)/shard_map/ppermute | solution.py:275
  18.9 0.1 pad_add_fusion.2.sh_ref
  18.9 0.0 collective-permute-done.6.refs_5_
  18.9 0.0 collective-permute-done.3.refs_1_
  18.9 0.0 collective-permute-done.8.refs_7_
  18.9 0.0 collective-permute-done.5.refs_3_
  19.0 0.0 copy-done.1
  19.0 0.0 copy-start
  19.0 1.5 %grad.1 = (f32[2,144,512]{2,1,0:T(8,128)S(1)}, f32[8,512]{1,0:T(8,128)S(1)}) custom-call(bf16[304,256]{1,0:T(8,128)(2,1)S(1)} %get-tuple-element.12.refs_0_, bf16[304,256]{1,0:T(8,128)(2,1)S(1)} %collective-permute-done.3.refs_1_, bf16[304,256]{1,0:T(8,128)(2,1)S(1)} %collective-permute-done.4.refs_2_, bf16[304,256]{1,0:T(8,128)(2,1)S(1)} %collective-permute-done.5.refs_3_, ...), custom_call_target="tpu_custom_call" | custom-call | tf_op jit(solution)/shard_map/grad/pallas_call | solution.py:332
  20.5 0.0 copy-done
  20.5 1.6 %segment.1 = (f32[2,128,512]{2,1,0:T(8,128)S(1)}, f32[8,72,128]{2,1,0:T(8,128)S(1)}, f32[2]{0:T(128)S(1)}) custom-call(s32[32]{0:T(128)S(1)} %pad_add_fusion.2.sh_ref, f32[2,144,512]{2,1,0:T(8,128)S(1)} %get-tuple-element.17.g_ref, bf16[2,128,512]{2,1,0:T(8,128)(2,1)S(1)} %copy-done, f32[8,512]{1,0:T(8,128)S(1)} %get-tuple-element.18.next_ref), custom_call_target="tpu_custom_call" | custom-call | tf_op jit(solution)/shard_map/segment/pallas_call | solution.py:351
  22.1 14.8 %all_to_all.15.got_ref = f32[8,72,128]{2,1,0:T(8,128)S(1)} all-to-all(f32[8,72,128]{2,1,0:T(8,128)S(1)} %get-tuple-element.19), channel_id=1, replica_groups=mesh['tm'=8,'rows'=4] {'tm'}, dimensions={0} | all-to-all | bytes 589824 | tf_op jit(solution)/shard_map/all_to_all | solution.py:359
  36.9 0.7 %scan.1 = f32[8,72,128]{2,1,0:T(8,128)S(1)} custom-call(s32[32]{0:T(128)S(1)} %pad_add_fusion.2.sh_ref, f32[8,72,128]{2,1,0:T(8,128)S(1)} %all_to_all.15.got_ref), custom_call_target="tpu_custom_call" | custom-call | tf_op jit(solution)/shard_map/scan/pallas_call | solution.py:360
  37.6 11.3 %all_to_all.16.got_ref = f32[8,72,128]{2,1,0:T(8,128)S(1)} all-to-all(f32[8,72,128]{2,1,0:T(8,128)S(1)} %scan.1), channel_id=1, replica_groups=mesh['tm'=8,'rows'=4] {'tm'}, dimensions={0} | all-to-all | bytes 589824 | tf_op jit(solution)/shard_map/all_to_all | solution.py:368
  48.9 1.8 %wind.1 = f32[32,1,128]{2,1,0:T(1,128)} custom-call(s32[32]{0:T(128)S(1)} %pad_add_fusion.2.sh_ref, f32[2]{0:T(128)S(1)} %get-tuple-element.21.wind_in, f32[8,72,128]{2,1,0:T(8,128)S(1)} %all_to_all.16.got_ref, bf16[2,128,512]{2,1,0:T(8,128)(2,1)S(1)} %copy-done, f32[8,512]{1,0:T(8,128)S(1)} %get-tuple-element.18.next_ref), custom_call_target="tpu_custom_call" | custom-call | tf_op jit(solution)/shard_map/wind/pallas_call | solution.py:371
  50.7 2.7 %all-to-all-start.2 = ((f32[32,1,128]{2,1,0:T(1,128)}), f32[32,1,128]{2,1,0:T(1,128)S(1)}, u32[]{:S(2)}, u32[]{:S(2)}) async-start(f32[32,1,128]{2,1,0:T(1,128)} %wind.1), calls=%async_computation.2 | async-start | bytes 32768 | tf_op jit(solution)/shard_map/all_to_all | solution.py:380
  53.4 1.6 %final.1 = f32[2,128,512]{2,1,0:T(8,128)} custom-call(s32[32]{0:T(128)S(1)} %pad_add_fusion.2.sh_ref, f32[8,72,128]{2,1,0:T(8,128)S(1)} %all_to_all.16.got_ref, f32[2,128,512]{2,1,0:T(8,128)S(1)} %get-tuple-element.20.loc_ref), custom_call_target="tpu_custom_call" | custom-call | flops 737280 | bytes 1572864 | tf_op jit(solution)/shard_map/final/pallas_call | solution.py:381
  55.1 5.5 %all-to-all-done.2 = f32[32,1,128]{2,1,0:T(1,128)S(1)} async-done(((f32[32,1,128]{2,1,0:T(1,128)}), f32[32,1,128]{2,1,0:T(1,128)S(1)}, u32[]{:S(2)}, u32[]{:S(2)}) %all-to-all-start.2) | async-done | bytes 16416 | tf_op jit(solution)/shard_map/all_to_all | solution.py:380
  60.6 0.1 slice_reduce_fusion
  60.7 0.5 negate_multiply_fusion
Async XLA Ops:
  0.6 18.3 %copy-start.1 = (s32[128,512]{1,0:T(8,128)S(1)}, s32[128,512]{1,0:T(8,128)}, u32[]{:S(2)}) copy-start(s32[128,512]{1,0:T(8,128)} %refs_8_.1) | copy-start | bytes 786436
  0.6 5.7 %copy-start.2 = (bf16[2,2,64,256]{3,2,1,0:T(8,128)(2,1)S(1)}, bf16[2,2,64,256]{3,2,1,0:T(8,128)(2,1)}, u32[]{:S(2)}) copy-start(bf16[2,2,64,256]{3,2,1,0:T(8,128)(2,1)} %refs_4_.1) | copy-start | bytes 393220
  3.2 3.6 %copy-start.3 = (s32[2,2]{1,0:T(2,128)S(1)}, s32[2,2]{1,0:T(2,128)}, u32[]{:S(2)}) copy-start(s32[2,2]{1,0:T(2,128)} %param.11) | copy-start | bytes 52
  3.3 9.9 %collective-permute-start.4 = (bf16[304,256]{1,0:T(8,128)(2,1)S(1)}, bf16[304,256]{1,0:T(8,128)(2,1)S(1)}, u32[]{:S(2)}, u32[]{:S(2)}) collective-permute-start(bf16[304,256]{1,0:T(8,128)(2,1)S(1)} %get-tuple-element.12.refs_0_), channel_id=1, source_target_pairs={{0,2},{1,3},{2,0},{3,1},{4,6},{5,7},{6,4},{7,5},{8,10},{9,11},{10,... | collective-permute-start | bytes 466952 | tf_op jit(solution)/shard_map/ppermute | solution.py:275
  6.3 6.8 %collective-permute-start.7 = (bf16[2,2,64,256]{3,2,1,0:T(8,128)(2,1)S(1)}, bf16[2,2,64,256]{3,2,1,0:T(8,128)(2,1)S(1)}, u32[]{:S(2)}, u32[]{:S(2)}) collective-permute-start(bf16[2,2,64,256]{3,2,1,0:T(8,128)(2,1)S(1)} %copy-done.2), channel_id=1, source_target_pairs={{0,2},{1,3},{2,0},{3,1},{4,6},{5,7},{6,4},{7,5},{8,10},{9,11},{10,... | collective-permute-start | bytes 393224 | tf_op jit(solution)/shard_map/ppermute | solution.py:275
  6.4 12.6 %collective-permute-start.3 = (bf16[304,256]{1,0:T(8,128)(2,1)S(1)}, bf16[304,256]{1,0:T(8,128)(2,1)S(1)}, u32[]{:S(2)}, u32[]{:S(2)}) collective-permute-start(bf16[304,256]{1,0:T(8,128)(2,1)S(1)} %get-tuple-element.12.refs_0_), channel_id=1, source_target_pairs={{0,1},{1,0},{2,3},{3,2},{4,5},{5,4},{6,7},{7,6},{8,9},{9,8},{10,11... | collective-permute-start | bytes 466952 | tf_op jit(solution)/shard_map/ppermute | solution.py:275
  6.4 12.6 %collective-permute-start.6 = (bf16[2,2,64,256]{3,2,1,0:T(8,128)(2,1)S(1)}, bf16[2,2,64,256]{3,2,1,0:T(8,128)(2,1)S(1)}, u32[]{:S(2)}, u32[]{:S(2)}) collective-permute-start(bf16[2,2,64,256]{3,2,1,0:T(8,128)(2,1)S(1)} %copy-done.2), channel_id=1, source_target_pairs={{0,1},{1,0},{2,3},{3,2},{4,5},{5,4},{6,7},{7,6},{8,9},{9,8},{10,11... | collective-permute-start | bytes 393224 | tf_op jit(solution)/shard_map/ppermute | solution.py:275
  7.0 3.6 %collective-permute-start = (s32[4]{0:T(128)S(1)}, s32[4]{0:T(128)S(1)}, u32[]{:S(2)}, u32[]{:S(2)}) collective-permute-start(s32[4]{0:T(128)S(1)} %reshape.7), channel_id=1, source_target_pairs={{0,4},{4,0},{8,12},{12,8},{16,20},{20,16},{24,28},{28,24},{1,5},{5... | collective-permute-start | bytes 56 | tf_op jit(solution)/shard_map/ppermute | solution.py:275
  10.6 3.6 %collective-permute-start.1 = (s32[8]{0:T(128)S(1)}, s32[8]{0:T(128)S(1)}, u32[]{:S(2)}, u32[]{:S(2)}) collective-permute-start(s32[8]{0:T(128)S(1)} %pad_add_fusion), channel_id=1, source_target_pairs={{0,8},{4,12},{8,0},{12,4},{16,24},{20,28},{24,16},{28,20},{1,9},{5... | collective-permute-start | bytes 104 | tf_op jit(solution)/shard_map/ppermute | solution.py:275
  13.1 5.8 %collective-permute-start.8 = (bf16[2,2,64,256]{3,2,1,0:T(8,128)(2,1)S(1)}, bf16[2,2,64,256]{3,2,1,0:T(8,128)(2,1)S(1)}, u32[]{:S(2)}, u32[]{:S(2)}) collective-permute-start(bf16[2,2,64,256]{3,2,1,0:T(8,128)(2,1)S(1)} %collective-permute-done.7.refs_6_), channel_id=1, source_target_pairs={{0,1},{1,0},{2,3},{3,2},{4,5},{5,4},{6,7},{7,6},{8,9},{9,8},{10,11... | collective-permute-start | bytes 393224 | tf_op jit(solution)/shard_map/ppermute | solution.py:275
  13.1 5.8 %collective-permute-start.5 = (bf16[304,256]{1,0:T(8,128)(2,1)S(1)}, bf16[304,256]{1,0:T(8,128)(2,1)S(1)}, u32[]{:S(2)}, u32[]{:S(2)}) collective-permute-start(bf16[304,256]{1,0:T(8,128)(2,1)S(1)} %collective-permute-done.4.refs_2_), channel_id=1, source_target_pairs={{0,1},{1,0},{2,3},{3,2},{4,5},{5,4},{6,7},{7,6},{8,9},{9,8},{10,11... | collective-permute-start | bytes 466952 | tf_op jit(solution)/shard_map/ppermute | solution.py:275
  14.3 4.6 %collective-permute-start.2 = (s32[16]{0:T(128)S(1)}, s32[16]{0:T(128)S(1)}, u32[]{:S(2)}, u32[]{:S(2)}) collective-permute-start(s32[16]{0:T(128)S(1)} %pad_add_fusion.1), channel_id=1, source_target_pairs={{0,16},{4,20},{8,24},{12,28},{16,0},{20,4},{24,8},{28,12},{1,17},{... | collective-permute-start | bytes 200 | tf_op jit(solution)/shard_map/ppermute | solution.py:275
  19.0 1.5 %copy-start = (bf16[2,128,512]{2,1,0:T(8,128)(2,1)S(1)}, bf16[2,128,512]{2,1,0:T(8,128)(2,1)}, u32[]{:S(2)}) copy-start(bf16[2,128,512]{2,1,0:T(8,128)(2,1)} %phases_ref.5) | copy-start | bytes 786436
  50.7 9.9 %all-to-all-start.2 = ((f32[32,1,128]{2,1,0:T(1,128)}), f32[32,1,128]{2,1,0:T(1,128)S(1)}, u32[]{:S(2)}, u32[]{:S(2)}) async-start(f32[32,1,128]{2,1,0:T(1,128)} %wind.1), calls=%async_computation.2 | async-start | bytes 32768 | tf_op jit(solution)/shard_map/all_to_all | solution.py:380

commit v4 on v3

--- a/solution.py
+++ b/solution.py
@@ -29,16 +29,6 @@
     return sh_ref[at], sh_ref[at + 1]
 
 
-def cum_shifts(sh_ref, frames, stop):
-    def add(j, sums):
-        for k in range(frames):
-            a, b = own_shift(sh_ref, frames, j, k)
-            sums = (sums[0] + a, sums[1] + b)
-        return sums
-
-    return lax.fori_loop(0, stop, add, (jnp.int32(0), jnp.int32(0)))
-
-
 def dot(a, b):
     return jnp.dot(a, b, preferred_element_type=jnp.float32)
 
@@ -52,14 +42,19 @@
     return lax.broadcasted_iota(jnp.int32, shape, 1)
 
 
-def y_kernel(halo, phases_ref, mask_ref, half_ref, *refs):
-    count = (len(refs) - 2) // 2
+def y_kernel(halo, phases_hbm, mask_hbm, half_hbm, *refs):
+    count = (len(refs) - 5) // 2
     y_ref = refs[count]
+    phases_ref, mask_ref, half_ref, sem = refs[-4:]
+    ins = [(phases_hbm, phases_ref), (mask_hbm, mask_ref), (half_hbm, half_ref)]
+    copies = [(refs[i], refs[count + 1 + i]) for i in range(count)]
     copies = [
-        pltpu.make_async_copy(refs[i], refs[count + 1 + i], refs[-1].at[i]) for i in range(count)
+        pltpu.make_async_copy(src, dst, sem.at[i]) for i, (src, dst) in enumerate(ins + copies)
     ]
     for copy in copies:
         copy.start()
+    for copy in copies[:3]:
+        copy.wait()
     frames, block, width = phases_ref.shape
     focal = y_ref.shape[1]
     parts = width // focal
@@ -84,7 +79,7 @@
     mask = mask_ref[:halo].astype(jnp.float32).astype(jnp.bfloat16)
     for i in range(parts):
         y_ref[at + i * halo : at + (i + 1) * halo] = mask[:, i * focal : (i + 1) * focal]
-    for copy in copies:
+    for copy in copies[3:]:
         copy.wait()
 
 
@@ -163,10 +158,53 @@
         g_ref[k, block:] = jnp.where(live_over, g[block:], 0.0)
 
 
-def segment_kernel(slot, sh_ref, g_ref, phases_ref, next_ref, loc_ref, msg_ref, wind_ref):
+def halves(value, y):
+    width = value.shape[1]
+    low, high = value[:, : width // 2], value[:, width // 2 :]
+    return jnp.where(y == 0, low, high), jnp.where(y == 0, high, low)
+
+
+def pack(ref, value):
+    rows, width = value.shape
+    top = jnp.full((8, width), jnp.maximum(jnp.max(jnp.abs(value)), 1e-30))
+    power = jnp.ceil(jnp.log2(top))
+    ref[:rows] = value * jnp.exp2(-power[:1])
+    ref[rows:] = power
+
+
+def unpack(ref):
+    rows = ref.shape[0] - 8
+    return ref[:rows] * jnp.exp2(ref[rows : rows + 1])
+
+
+def dropped(value, pos, width, b_cum, b_here):
+    c = pos + lax.rem(b_cum, width)
+    c = jnp.where(c >= width, c - width, c)
+    return jnp.where(c >= b_here, value, 0.0)
+
+
+def fill_sums(sh_ref, frames, sums_ref):
+    def add(j, sums):
+        sums_ref[2 * j] = sums[0]
+        sums_ref[2 * j + 1] = sums[1]
+        for k in range(frames):
+            a, b = own_shift(sh_ref, frames, j, k)
+            sums = (sums[0] + a, sums[1] + b)
+        return sums
+
+    count = lax.axis_size("tm")
+    last = lax.fori_loop(0, count, add, (jnp.int32(0), jnp.int32(0)))
+    sums_ref[2 * count] = last[0]
+    sums_ref[2 * count + 1] = last[1]
+
+
+def segment_kernel(
+    sh_ref, g_ref, phases_ref, next_ref, loc_ref, keep_ref, send_ref, wind_ref, sums_ref
+):
     frames, rows, width = g_ref.shape
     block = phases_ref.shape[1]
     halo = rows - block
+    tm = lax.axis_index("tm")
     col = columns((rows, width))
     row = lax.broadcasted_iota(jnp.int32, (rows, width), 0)
     down_sum = jnp.float32(0.0)
@@ -184,63 +222,116 @@
         loc_ref[k] = lam[:block]
     wind_ref[0] = down_sum
     wind_ref[1] = side_sum
-    a_cum, b_cum = cum_shifts(sh_ref, frames, lax.axis_index("tm"))
+    fill_sums(sh_ref, frames, sums_ref)
+    a_cum, b_cum = sums_ref[2 * tm], sums_ref[2 * tm + 1]
     canvas = turned(lam, halo - a_cum, width - lax.rem(b_cum, width))
     canvas = jnp.where(row >= halo - a_cum, canvas, 0.0)
-    per = rows // slot
-    for j in range(msg_ref.shape[0]):
-        if j < per * (width // LANES):
-            c = j // per
-            r = j % per
-            msg_ref[j] = canvas[r * slot : (r + 1) * slot, c * LANES : (c + 1) * LANES]
-        else:
-            msg_ref[j] = jnp.zeros((slot, LANES), jnp.float32)
-
-
-def diffs(phases_ref, next_ref, k):
+    keep, send = halves(canvas, tm % 2)
+    keep_ref[...] = keep
+    pack(send_ref, send)
+
+
+def z_kernel(halo, sh_ref, sums_ref, phases_ref, next_ref, after_ref, keep_ref, send_ref):
     frames, block, width = phases_ref.shape
-    here = phases_ref[k].astype(jnp.float32)
-    last = next_ref[k : k + 1]
-    row = lax.broadcasted_iota(jnp.int32, (block, width), 0)
-    below = jnp.where(row == block - 1, last, pltpu.roll(here, block - 1, 0))
-    right = jnp.where(columns((block, width)) == width - 1, 0.0, pltpu.roll(here, width - 1, 1))
-    return below - here, right - here
-
-
-def scan_kernel(frames, rows, width, sh_ref, got_ref, out_ref):
-    n, slot, _ = got_ref.shape
-    me = lax.axis_index("tm")
-    flat = me * slot + lax.broadcasted_iota(jnp.int32, (slot, LANES), 0)
-    pos = lax.broadcasted_iota(jnp.int32, (slot, LANES), 1)
-    for c in range(1, width // LANES):
-        pos = pos + jnp.where(flat >= c * rows, LANES, 0)
-    weight = decay_rate**frames
-
-    def one(step, carry):
-        field, b_cum = carry
-        j = n - 1 - step
-        out_ref[j] = field
-        b_here = jnp.int32(0)
-        for k in range(frames):
-            b_here = b_here + own_shift(sh_ref, frames, j, k)[1]
-        c = pos + lax.rem(b_cum, width)
-        c = jnp.where(c >= width, c - width, c)
-        field = got_ref[j] + jnp.where(c >= b_here, weight * field, 0.0)
-        return field, b_cum - b_here
-
-    _, b_all = cum_shifts(sh_ref, frames, n)
-    lax.fori_loop(0, n, one, (jnp.zeros((slot, LANES), jnp.float32), b_all))
-
-
-def carried(halo, frames, block, width, sh_ref, got_ref, c_ref):
-    n, slot, _ = got_ref.shape
-    rows = block + halo
-    per = rows // slot
-    for j in range(min(n, per * (width // LANES))):
-        c = j // per
-        r = j % per
-        c_ref[r * slot : (r + 1) * slot, c * LANES : (c + 1) * LANES] = got_ref[j]
-    a_cum, b_cum = cum_shifts(sh_ref, frames, lax.axis_index("tm") + 1)
+    tm = lax.axis_index("tm")
+    a_cum, b_cum = sums_ref[2 * tm + 2], sums_ref[2 * tm + 3]
+    b_own = jnp.int32(0)
+    col = columns((block, width))
+    pad = jnp.zeros((halo, width), jnp.float32)
+    sums = [jnp.zeros((block + halo, width), jnp.float32) for _ in range(2)]
+    for k in reversed(range(frames)):
+        a, b = sh_ref[2 * k], sh_ref[2 * k + 1]
+        a_cum = a_cum - a
+        b_cum = b_cum - b
+        b_own = b_own + b
+        for i, diff in enumerate(diffs(phases_ref, next_ref, k)):
+            diff = jnp.where(col < width - b_own, decay_rate ** (frames - k) * diff, 0.0)
+            diff = jnp.concatenate([diff, pad], axis=0)
+            sums[i] = sums[i] + turned(diff, halo - a_cum, width - lax.rem(b_cum, width))
+    for i in range(2):
+        keep, send = halves(sums[i], tm % 2)
+        keep_ref[i] = keep
+        pack(send_ref.at[i], send)
+
+
+def combine_kernel(frames, width, sums_ref, keep_ref, got_ref, late_ref, both_ref, send_ref):
+    rows, part = keep_ref.shape
+    tm = lax.axis_index("tm")
+    pair, y = tm // 2, tm % 2
+    keep, got = keep_ref[...], unpack(got_ref)
+    early = jnp.where(y == 0, keep, got)
+    late = jnp.where(y == 0, got, keep)
+    late_ref[...] = late
+    b_from, b_cum = sums_ref[4 * pair + 1], sums_ref[4 * pair + 3]
+    pos = columns((rows, part)) + y * part
+    both = early + dropped(decay_rate**frames * late, pos, width, b_cum, b_cum - b_from)
+    both_ref[...] = both
+    pack(send_ref, both)
+
+
+def later_pairs(frames, width, reach, sums_ref, got_ref):
+    rows = got_ref.shape[0] - 8
+    part = got_ref.shape[1]
+    tm = lax.axis_index("tm")
+    pair, y = tm // 2, tm % 2
+    pos = columns((rows, part)) + y * part
+    pairs = lax.axis_size("tm") // 2
+    got = jnp.where(pair + reach < pairs, unpack(got_ref), 0.0)
+    b_cum = sums_ref[4 * jnp.minimum(pair + reach, pairs) + 1]
+    b_from, b_next = sums_ref[4 * pair + 1], sums_ref[4 * pair + 5]
+    weight = decay_rate ** (2 * frames * reach)
+    weight_next = decay_rate ** (2 * frames * (reach - 1))
+    incl = dropped(weight * got, pos, width, b_cum, b_cum - b_from)
+    return incl, dropped(weight_next * got, pos, width, b_cum, b_cum - b_next)
+
+
+def step_kernel(frames, width, reach, sums_ref, both_ref, got_ref, *refs):
+    incl, excl = later_pairs(frames, width, reach, sums_ref, got_ref)
+    incl_ref, excl_ref, send_ref = refs[-3:]
+    both = both_ref[...] + incl
+    incl_ref[...] = both
+    excl_ref[...] = excl + refs[0][...] if len(refs) == 4 else excl
+    pack(send_ref, both)
+
+
+def carry_kernel(frames, width, reach, sums_ref, late_ref, got_ref, *refs):
+    keep_ref, send_ref, raw_ref = refs[-3:]
+    rows, part = late_ref.shape
+    tm = lax.axis_index("tm")
+    pair, y = tm // 2, tm % 2
+    _, late = later_pairs(frames, width, reach, sums_ref, got_ref)
+    if len(refs) == 4:
+        late = late + refs[0][...]
+    b_from, b_cum = sums_ref[4 * pair + 3], sums_ref[4 * pair + 5]
+    pos = columns((rows, part)) + y * part
+    moved = dropped(decay_rate**frames * late, pos, width, b_cum, b_cum - b_from)
+    early = late_ref[...] + moved
+    keep_ref[...] = jnp.where(y == 0, early, late)
+    send = jnp.where(y == 0, late, early)
+    raw_ref[...] = send
+    pack(send_ref, send)
+
+
+def wind_kernel(wind_in, keep_ref, send_ref, z_ref, zgot_ref, wind_ref):
+    sums = [
+        wind_in[i]
+        + jnp.sum(keep_ref[...] * z_ref[i] + send_ref[...] * unpack(zgot_ref.at[i]))
+        for i in range(2)
+    ]
+    lane = lax.broadcasted_iota(jnp.int32, wind_ref.shape, 2)
+    wind_ref[...] = jnp.where(lane == 0, sums[0], jnp.where(lane == 1, sums[1], 0.0))
+
+
+def final_kernel(sh_ref, sums_ref, keep_ref, got_ref, loc_ref, adj_ref):
+    frames, block, width = loc_ref.shape
+    rows = keep_ref.shape[0]
+    halo = rows - block
+    tm = lax.axis_index("tm")
+    keep, got = keep_ref[...], unpack(got_ref)
+    low = jnp.where(tm % 2 == 0, keep, got)
+    high = jnp.where(tm % 2 == 0, got, keep)
+    canvas = jnp.concatenate([low, high], axis=1)
+    a_cum, b_cum = sums_ref[2 * tm + 2], sums_ref[2 * tm + 3]
     col = columns((block, width))
     b_own = jnp.int32(0)
     for k in reversed(range(frames)):
@@ -248,26 +339,19 @@
         a_cum = a_cum - a
         b_cum = b_cum - b
         b_own = b_own + b
-        moved = turned(c_ref[...], rows - halo + a_cum, b_cum)[:block]
-        yield k, jnp.where(col < width - b_own, decay_rate ** (frames - k) * moved, 0.0)
-
-
-def wind_kernel(halo, sh_ref, wind_in, got_ref, phases_ref, next_ref, wind_ref, c_ref):
-    frames, block, width = phases_ref.shape
-    down_sum = wind_in[0]
-    side_sum = wind_in[1]
-    for k, moved in carried(halo, frames, block, width, sh_ref, got_ref, c_ref):
-        down, side = diffs(phases_ref, next_ref, k)
-        down_sum = down_sum + jnp.sum(moved * down)
-        side_sum = side_sum + jnp.sum(moved * side)
-    lane = lax.broadcasted_iota(jnp.int32, wind_ref.shape, 2)
-    wind_ref[...] = jnp.where(lane == 0, down_sum, jnp.where(lane == 1, side_sum, 0.0))
-
-
-def final_kernel(halo, sh_ref, got_ref, loc_ref, adj_ref, c_ref):
-    frames, block, width = loc_ref.shape
-    for k, moved in carried(halo, frames, block, width, sh_ref, got_ref, c_ref):
+        moved = turned(canvas, rows - halo + a_cum, b_cum)[:block]
+        moved = jnp.where(col < width - b_own, decay_rate ** (frames - k) * moved, 0.0)
         adj_ref[k] = loc_ref[k] + moved
+
+
+def diffs(phases_ref, next_ref, k):
+    _, block, width = phases_ref.shape
+    here = phases_ref[k].astype(jnp.float32)
+    last = next_ref[k : k + 1]
+    row = lax.broadcasted_iota(jnp.int32, (block, width), 0)
+    below = jnp.where(row == block - 1, last, pltpu.roll(here, block - 1, 0))
+    right = jnp.where(columns((block, width)) == width - 1, 0.0, pltpu.roll(here, width - 1, 1))
+    return below - here, right - here
 
 
 def swap(value, axis, bit):
@@ -283,6 +367,28 @@
         held.update({d ^ bit: swap(v, "rows", bit) for d, v in list(held.items())})
         bit //= 2
     return [held[d] for d in range(count)]
+
+
+def from_later(value, pairs_away):
+    count = lax.axis_size("tm")
+    route = [(s, s - 2 * pairs_away) for s in range(2 * pairs_away, count)]
+    return lax.ppermute(value.astype(jnp.float16), "tm", route).astype(jnp.float32)
+
+
+def swap_half(value):
+    return swap(value.astype(jnp.float16), "tm", 1).astype(jnp.float32)
+
+
+def kernel_call(body, vmem_mib, out_shape, in_specs, out_specs, cost=0):
+    estimate = pl.CostEstimate(flops=0, bytes_accessed=cost, transcendentals=0) if cost else None
+    return pl.pallas_call(
+        body,
+        out_shape=out_shape,
+        in_specs=in_specs,
+        out_specs=out_specs,
+        cost_estimate=estimate,
+        compiler_params=pltpu.CompilerParams(vmem_limit_bytes=vmem_mib << 20),
+    )
 
 
 def on_device(phases, focal_data, shifts, pupil_mask):
@@ -294,7 +400,8 @@
     halo = min(frames_all // 2, width // (4 * n_rows))
     halo = -(-halo // 16) * 16
     rows = block + halo
-    slot = max(1, rows * (width // LANES) // n_tm)
+    part = width // 2
+    pairs = n_tm // 2
     half = focal // 2
     cs = tables(width, focal)
     tt = np.concatenate([cs.T, np.zeros((halo, 2 * focal), cs.dtype)], axis=0)
@@ -318,16 +425,20 @@
             jax.ShapeDtypeStruct((frames * block + 16 + halo * width // focal, focal), jnp.bfloat16)
         ]
         + [jax.ShapeDtypeStruct(t.shape, jnp.bfloat16) for t in kept],
-        in_specs=[vmem] * 3 + [hbm] * len(kept),
+        in_specs=[hbm] * (3 + len(kept)),
         out_specs=[vmem] * (1 + len(kept)),
-        scratch_shapes=[pltpu.SemaphoreType.DMA((len(kept),))],
+        scratch_shapes=[
+            pltpu.VMEM(phases.shape, phases.dtype),
+            pltpu.VMEM(pupil_mask.shape, pupil_mask.dtype),
+            pltpu.VMEM(y_table.shape, y_table.dtype),
+            pltpu.SemaphoreType.DMA((3 + len(kept),)),
+        ],
         compiler_params=pltpu.CompilerParams(vmem_limit_bytes=8 << 20),
         name="transform",
     )(*[pltpu.with_memory_space_constraint(t, pltpu.HBM) for t in (phases, pupil_mask, y_table, *kept)])
     d_parts = gather_rows(focal_data)
     m_parts = gather_rows(y)
     field = jax.ShapeDtypeStruct((frames, block, width), jnp.float32)
-    message = jax.ShapeDtypeStruct((n_tm, slot, LANES), jnp.float32)
     pair = jax.ShapeDtypeStruct((2,), jnp.float32)
     grads, next_rows = pl.pallas_call(
         functools.partial(grad_kernel, n_rows, halo),
@@ -348,48 +459,53 @@
         compiler_params=pltpu.CompilerParams(vmem_limit_bytes=24 << 20),
         name="grad",
     )(*m_parts, *d_parts, pupil_mask, *kept)
-    loc, msg, wind_local = pl.pallas_call(
-        functools.partial(segment_kernel, slot),
-        out_shape=(field, message, pair),
-        in_specs=[smem, vmem, vmem, vmem],
-        out_specs=(vmem, vmem, smem),
-        compiler_params=pltpu.CompilerParams(vmem_limit_bytes=12 << 20),
-        name="segment",
+    half_field = jax.ShapeDtypeStruct((rows, part), jnp.float32)
+    message = jax.ShapeDtypeStruct((rows + 8, part), jnp.float32)
+    loc, keep, send, wind_local, sums_all = kernel_call(
+        segment_kernel, 12,
+        (field, half_field, message, pair, jax.ShapeDtypeStruct((2 * n_tm + 2,), jnp.int32)),
+        [smem, vmem, vmem, vmem], (vmem, vmem, vmem, smem, smem),
     )(sh_all, grads, phases, next_rows)
-    got = lax.all_to_all(msg, "tm", 0, 0)
-    fields = pl.pallas_call(
-        functools.partial(scan_kernel, frames, rows, width),
-        out_shape=message,
-        in_specs=[smem, vmem],
-        out_specs=vmem,
-        compiler_params=pltpu.CompilerParams(vmem_limit_bytes=6 << 20),
-        name="scan",
-    )(sh_all, got)
-    back = lax.all_to_all(fields, "tm", 0, 0)
+    late, both, send = kernel_call(
+        functools.partial(combine_kernel, frames, width), 6,
+        (half_field, half_field, message), [smem, vmem, vmem], (vmem, vmem, vmem),
+    )(sums_all, keep, swap_half(send))
+    z_keep, z_send = kernel_call(
+        functools.partial(z_kernel, halo), 12,
+        (
+            jax.ShapeDtypeStruct((2, rows, part), jnp.float32),
+            jax.ShapeDtypeStruct((2, rows + 8, part), jnp.float32),
+        ),
+        [smem, smem, vmem, vmem, pl.BlockSpec(memory_space=pl.ANY)], (vmem, vmem),
+    )(sh_all, sums_all, phases, next_rows, late)
+    z_got = swap_half(z_send)
+    sums = []
+    reach = 1
+    while 2 * reach < pairs:
+        both, excl, send = kernel_call(
+            functools.partial(step_kernel, frames, width, reach), 6,
+            (half_field, half_field, message),
+            [smem] + [vmem] * (2 + len(sums)), (vmem, vmem, vmem),
+        )(sums_all, both, from_later(send, reach), *sums)
+        sums = [excl]
+        reach *= 2
+    keep, send, raw = kernel_call(
+        functools.partial(carry_kernel, frames, width, reach), 6,
+        (half_field, message, half_field),
+        [smem] + [vmem] * (2 + len(sums)), (vmem, vmem, vmem),
+    )(sums_all, late, from_later(send, reach), *sums)
+    got = swap_half(send)
     n_all = n_tm * n_rows
-    canvas = pltpu.VMEM((rows, width), jnp.float32)
-    wind = pl.pallas_call(
-        functools.partial(wind_kernel, halo),
-        out_shape=jax.ShapeDtypeStruct((n_all, 1, LANES), jnp.float32),
-        in_specs=[smem, smem, vmem, vmem, vmem],
-        out_specs=vmem,
-        scratch_shapes=[canvas],
-        compiler_params=pltpu.CompilerParams(vmem_limit_bytes=8 << 20),
-        name="wind",
-    )(sh_all, wind_local, back, phases, next_rows)
+    wind = kernel_call(
+        wind_kernel, 6,
+        jax.ShapeDtypeStruct((n_all, 1, LANES), jnp.float32),
+        [smem] + [vmem] * 4, vmem,
+    )(wind_local, keep, raw, z_keep, z_got)
     winds = lax.all_to_all(wind, ("tm", "rows"), 0, 0)
-    adjoint = pl.pallas_call(
-        functools.partial(final_kernel, halo),
-        out_shape=field,
-        in_specs=[smem, vmem, vmem],
-        out_specs=vmem,
-        scratch_shapes=[canvas],
-        cost_estimate=pl.CostEstimate(
-            flops=10 * rows * width, bytes_accessed=12 * frames * block * width, transcendentals=0
-        ),
-        compiler_params=pltpu.CompilerParams(vmem_limit_bytes=8 << 20),
-        name="final",
-    )(sh_all, back, loc)
+    adjoint = kernel_call(
+        final_kernel, 8, field, [smem, smem, vmem, vmem, vmem], vmem,
+        cost=12 * frames * block * width,
+    )(sh_all, sums_all, keep, got, loc)
     wind_grad = -jnp.sum(winds[:, 0, :2], axis=0) / (width * frames_all)
     return adjoint, wind_grad
 
@@ -397,6 +513,7 @@
 def solution(mesh):
     in_specs = (P("tm", "rows", None), P("tm", None, "rows", None), P("tm", None), P("rows", None))
     out_specs = (P("tm", "rows", None), P())
+
     return jax.shard_map(
         on_device, mesh=mesh, in_specs=in_specs, out_specs=out_specs, check_vma=False
     )

time: 61.4 us -> 57.3 us (0.933)
  blocking collectives: 26.1 us -> 0 us
  starting transfers between devices: 13.9 us -> 23.6 us
  waiting for transfers between devices: 9.72 us -> 19.3 us
  Pallas kernels: 9.83 us -> 12.4 us
    all_to_all x2 -> x0, blocking collectives: 26.1 us -> none  [the longest x1 14.8 us: on_device(): got = lax.all_to_all(msg, 'tm', 0, 0)]
    ppermute x0 -> x2, waiting for transfers between devices: none -> 7.26 us  [from_later(): lax.ppermute(value.astype(jnp.float16), 'tm', route).astype(jnp.float32)]
    ppermute x9 -> x12, starting transfers between devices: 11.2 us -> 16.8 us  [swap(): return lax.ppermute(value, axis, [(s, s ^ bit) for s in range(count)])]
    pallas_call x4 -> x7, Pallas kernels: 5.73 us -> 9.15 us  [the longest x1 1.74 us: on_device(): kernel_call(segment_kernel, 12, (field, half_field, message, pair, jax.Sh...]
    ppermute x0 -> x2, starting transfers between devices: none -> 2.58 us  [from_later(): lax.ppermute(value.astype(jnp.float16), 'tm', route).astype(jnp.float32)]
    ppermute x9 -> x12, waiting for transfers between devices: 4.19 us -> 6.75 us  [swap(): return lax.ppermute(value, axis, [(s, s ^ bit) for s in range(count)])]
    all_to_all x1, starting transfers between devices: 2.73 us -> 4.16 us  [on_device(): winds = lax.all_to_all(wind, ('tm', 'rows'), 0, 0)]
    pallas_call x1, Pallas kernels: 2.59 us -> 1.74 us  [on_device(): pl.pallas_call(functools.partial(y_kernel, halo), out_shape=[jax.ShapeDty...]
  transfers between devices with their start and end apart: 10 -> 15, of which waited for: 5 -> 8; matrix products, arithmetic and copies ran while one was open for 1% -> 2% of each run, Pallas kernels for 3% -> 6%
where the time goes in v4:
time: 57.3 us; the launch traced here: 57.1 us
  starting transfers between devices  23.6 us (41%)
  waiting for transfers between devices  19.3 us (34%)
  Pallas kernels  12.4 us (22%)
  other arithmetic  0.93 us (2%)
  between operations  0.84 us (1%)
    ppermute x12, starting transfers between devices, swap(): return lax.ppermute(value, axis, [(s, s ^ bit) for s in range(count)])  16.8 us
    ppermute x2, waiting for transfers between devices, from_later(): lax.ppermute(value.astype(jnp.float16), 'tm', route).astype(jnp.float32)  7.26 us
    ppermute x12, waiting for transfers between devices, swap(): return lax.ppermute(value, axis, [(s, s ^ bit) for s in range(count)])  6.75 us
    all_to_all x1, waiting for transfers between devices, on_device(): winds = lax.all_to_all(wind, ('tm', 'rows'), 0, 0)  5.25 us
    all_to_all x1, starting transfers between devices, on_device(): winds = lax.all_to_all(wind, ('tm', 'rows'), 0, 0)  4.16 us
    ppermute x2, starting transfers between devices, from_later(): lax.ppermute(value.astype(jnp.float16), 'tm', route).astype(jnp.float32)  2.58 us
    pallas_call x1, Pallas kernels, on_device(): kernel_call(segment_kernel, 12, (field, half_field, message, pair, jax.Sh...  1.74 us
    pallas_call x1, Pallas kernels, on_device(): pl.pallas_call(functools.partial(y_kernel, halo), out_shape=[jax.ShapeDty...  1.74 us
  transfers between devices with their start and end apart: 15, of which 8 were waited for; matrix products, arithmetic and copies ran while one was open for 2% of the time, Pallas kernels for 6%

profile of v4, /device:TPU:0, one launch (start us, length us, event | category | flops | bytes accessed | tf_op | source)
XLA Modules:
  0.0 57.1 jit_solution(17165928653127225003)
XLA Ops:
  0.6 0.0 copy-start.1
  0.6 0.0 copy-start.2
  0.6 1.7 %transform.1 = (bf16[304,256]{1,0:T(8,128)(2,1)S(1)}, bf16[528,512]{1,0:T(8,128)(2,1)S(1)}, bf16[512,512]{1,0:T(8,128)(2,1)S(1)}, bf16[512,512]{1,0:T(8,128)(2,1)S(1)}, bf16[128,128]{1,0:T(8,128)(2,1)S(1)}) custom-call(bf16[2,128,512]{2,1,0:T(8,128)(2,1)} %phases_ref.3, s32[128,512]{1,0:T(8,128)} %refs_8_.1, bf16[512,256]{1,0:T(8,128)(2,1)} %constant.15.clone.half_hbm, ...), custom_call_target="tpu_custom_call" | custom-call | tf_op jit(solution)/shard_map/transform/pallas_call | solution.py:422
  2.4 0.0 copy-start.3
  2.4 3.0 %collective-permute-start.4 = (bf16[304,256]{1,0:T(8,128)(2,1)S(1)}, bf16[304,256]{1,0:T(8,128)(2,1)S(1)}, u32[]{:S(2)}, u32[]{:S(2)}) collective-permute-start(bf16[304,256]{1,0:T(8,128)(2,1)S(1)} %get-tuple-element.24.refs_0_), channel_id=1, source_target_pairs={{0,2},{1,3},{2,0},{3,1},{4,6},{5,7},{6,4},{7,5},{8,10},{9,11},{10,... | collective-permute-start | bytes 466952 | tf_op jit(solution)/shard_map/ppermute | solution.py:359
  5.4 0.0 copy-done.2
  5.4 0.1 collective-permute-start.7
  5.5 0.0 collective-permute-start.3
  5.5 0.5 collective-permute-start.6
  6.0 0.0 copy-done.3
  6.0 0.1 reshape.7
  6.1 2.0 %collective-permute-start = (s32[4]{0:T(128)S(1)}, s32[4]{0:T(128)S(1)}, u32[]{:S(2)}, u32[]{:S(2)}) collective-permute-start(s32[4]{0:T(128)S(1)} %reshape.7), channel_id=1, source_target_pairs={{0,4},{4,0},{8,12},{12,8},{16,20},{20,16},{24,28},{28,24},{1,5},{5... | collective-permute-start | bytes 56 | tf_op jit(solution)/shard_map/ppermute | solution.py:359
  8.1 1.6 %collective-permute-done = s32[4]{0:T(128)S(1)} collective-permute-done((s32[4]{0:T(128)S(1)}, s32[4]{0:T(128)S(1)}, u32[]{:S(2)}, u32[]{:S(2)}) %collective-permute-start) | collective-permute-done | bytes 48 | tf_op jit(solution)/shard_map/ppermute | solution.py:359
  9.7 0.1 pad_add_fusion
  9.8 2.0 %collective-permute-start.1 = (s32[8]{0:T(128)S(1)}, s32[8]{0:T(128)S(1)}, u32[]{:S(2)}, u32[]{:S(2)}) collective-permute-start(s32[8]{0:T(128)S(1)} %pad_add_fusion), channel_id=1, source_target_pairs={{0,8},{4,12},{8,0},{12,4},{16,24},{20,28},{24,16},{28,20},{1,9},{5... | collective-permute-start | bytes 104 | tf_op jit(solution)/shard_map/ppermute | solution.py:359
  11.8 0.5 collective-permute-done.7.refs_6_
  12.3 0.0 collective-permute-start.8
  12.3 0.0 collective-permute-done.4.refs_2_
  12.3 0.5 collective-permute-start.5
  12.8 0.6 collective-permute-done.1
  13.3 0.1 pad_add_fusion.1
  13.4 3.0 %collective-permute-start.2 = (s32[16]{0:T(128)S(1)}, s32[16]{0:T(128)S(1)}, u32[]{:S(2)}, u32[]{:S(2)}) collective-permute-start(s32[16]{0:T(128)S(1)} %pad_add_fusion.1), channel_id=1, source_target_pairs={{0,16},{4,20},{8,24},{12,28},{16,0},{20,4},{24,8},{28,12},{1,17},{... | collective-permute-start | bytes 200 | tf_op jit(solution)/shard_map/ppermute | solution.py:359
  16.5 1.5 %collective-permute-done.2 = s32[16]{0:T(128)S(1)} collective-permute-done((s32[16]{0:T(128)S(1)}, s32[16]{0:T(128)S(1)}, u32[]{:S(2)}, u32[]{:S(2)}) %collective-permute-start.2) | collective-permute-done | bytes 96 | tf_op jit(solution)/shard_map/ppermute | solution.py:359
  18.0 0.1 pad_add_fusion.2.sh_ref
  18.1 0.0 collective-permute-done.6.refs_5_
  18.1 0.0 collective-permute-done.3.refs_1_
  18.1 0.0 collective-permute-done.8.refs_7_
  18.1 0.0 collective-permute-done.5.refs_3_
  18.1 0.0 copy-done.1
  18.1 0.0 copy-start
  18.1 1.5 %grad.1 = (f32[2,144,512]{2,1,0:T(8,128)S(1)}, f32[8,512]{1,0:T(8,128)S(1)}) custom-call(bf16[304,256]{1,0:T(8,128)(2,1)S(1)} %get-tuple-element.24.refs_0_, bf16[304,256]{1,0:T(8,128)(2,1)S(1)} %collective-permute-done.3.refs_1_, bf16[304,256]{1,0:T(8,128)(2,1)S(1)} %collective-permute-done.4.refs_2_, bf16[304,256]{1,0:T(8,128)(2,1)S(1)} %collective-permute-done.5.refs_3_, ...), custom_call_target="tpu_custom_call" | custom-call | tf_op jit(solution)/shard_map/grad/pallas_call | solution.py:443
  19.6 0.0 copy-done
  19.7 1.7 %shard_map.104 = (f32[2,128,512]{2,1,0:T(8,128)S(1)}, f32[144,256]{1,0:T(8,128)S(1)}, f32[152,256]{1,0:T(8,128)S(1)}, f32[2]{0:T(128)S(1)}, s32[18]{0:T(128)S(1)}) custom-call(s32[32]{0:T(128)S(1)} %pad_add_fusion.2.sh_ref, f32[2,144,512]{2,1,0:T(8,128)S(1)} %get-tuple-element.29.g_ref, bf16[2,128,512]{2,1,0:T(8,128)(2,1)S(1)} %copy-done, ...), custom_call_target="tpu_custom_call" | custom-call | tf_op jit(solution)/shard_map/pallas_call | solution.py:464
  21.4 1.9 %collective-permute-start.9 = (f16[152,256]{1,0:T(8,128)(2,1)S(1)}, f16[152,256]{1,0:T(8,128)(2,1)S(1)}, u32[]{:S(2)}, u32[]{:S(2)}) collective-permute-start(f16[152,256]{1,0:T(8,128)(2,1)S(1)} %convert_element_type.30), channel_id=1, source_target_pairs={{0,4},{4,0},{8,12},{12,8},{16,20},{20,16},{24,28},{28,24},{1,5},{5... | collective-permute-start | bytes 233480 | tf_op jit(solution)/shard_map/ppermute | solution.py:359
  23.3 2.5 %collective-permute-done.9 = f16[152,256]{1,0:T(8,128)(2,1)S(1)} collective-permute-done((f16[152,256]{1,0:T(8,128)(2,1)S(1)}, f16[152,256]{1,0:T(8,128)(2,1)S(1)}, u32[]{:S(2)}, u32[]{:S(2)}) %collective-permute-start.9) | collective-permute-done | bytes 77856 | tf_op jit(solution)/shard_map/ppermute | solution.py:359
  25.9 0.7 %shard_map.105 = (f32[144,256]{1,0:T(8,128)S(1)}, f32[144,256]{1,0:T(8,128)S(1)}, f32[152,256]{1,0:T(8,128)S(1)}) custom-call(s32[18]{0:T(128)S(1)} %get-tuple-element.31.sums_ref, f32[144,256]{1,0:T(8,128)S(1)} %get-tuple-element.32.keep_ref, f32[152,256]{1,0:T(8,128)S(1)} %convert_element_type.31.got_ref), custom_call_target="tpu_custom_call" | custom-call | tf_op jit(solution)/shard_map/pallas_call | solution.py:469
  26.7 1.3 %collective-permute-start.10 = (f16[152,256]{1,0:T(8,128)(2,1)S(1)}, f16[152,256]{1,0:T(8,128)(2,1)S(1)}, u32[]{:S(2)}, u32[]{:S(2)}) collective-permute-start(f16[152,256]{1,0:T(8,128)(2,1)S(1)} %convert_element_type.32), channel_id=1, source_target_pairs={{8,0},{12,4},{16,8},{20,12},{24,16},{28,20},{9,1},{13,5},{17,9},{2... | collective-permute-start | bytes 233480 | tf_op jit(solution)/shard_map/ppermute | solution.py:375
  28.0 1.7 %shard_map.109 = (f32[2,144,256]{2,1,0:T(8,128)S(1)}, f32[2,152,256]{2,1,0:T(8,128)S(1)}) custom-call(s32[32]{0:T(128)S(1)} %pad_add_fusion.2.sh_ref, s32[18]{0:T(128)S(1)} %get-tuple-element.31.sums_ref, bf16[2,128,512]{2,1,0:T(8,128)(2,1)S(1)} %copy-done, f32[8,512]{1,0:T(8,128)S(1)} %get-tuple-element.30.next_ref, ...), custom_call_target="tpu_custom_call" | custom-call | tf_op jit(solution)/shard_map/pallas_call | solution.py:473
  29.7 1.9 %collective-permute-start.13 = (f16[2,152,256]{2,1,0:T(8,128)(2,1)S(1)}, f16[2,152,256]{2,1,0:T(8,128)(2,1)S(1)}, u32[]{:S(2)}, u32[]{:S(2)}) collective-permute-start(f16[2,152,256]{2,1,0:T(8,128)(2,1)S(1)} %convert_element_type.38), channel_id=1, source_target_pairs={{0,4},{4,0},{8,12},{12,8},{16,20},{20,16},{24,28},{28,24},{1,5},{5... | collective-permute-start | bytes 466952 | tf_op jit(solution)/shard_map/ppermute | solution.py:359
  31.6 1.4 %collective-permute-done.10 = f16[152,256]{1,0:T(8,128)(2,1)S(1)} collective-permute-done((f16[152,256]{1,0:T(8,128)(2,1)S(1)}, f16[152,256]{1,0:T(8,128)(2,1)S(1)}, u32[]{:S(2)}, u32[]{:S(2)}) %collective-permute-start.10) | collective-permute-done | bytes 77856 | tf_op jit(solution)/shard_map/ppermute | solution.py:375
  33.0 1.3 %shard_map.106 = (f32[144,256]{1,0:T(8,128)}, f32[144,256]{1,0:T(8,128)S(1)}, f32[152,256]{1,0:T(8,128)S(1)}) custom-call(s32[18]{0:T(128)S(1)} %get-tuple-element.31.sums_ref, f32[144,256]{1,0:T(8,128)S(1)} %get-tuple-element.35.both_ref, f32[152,256]{1,0:T(8,128)S(1)} %convert_element_type.33.got_ref), custom_call_target="tpu_custom_call" | custom-call | tf_op jit(solution)/shard_map/pallas_call | solution.py:485
  34.2 1.3 %collective-permute-start.11 = (f16[152,256]{1,0:T(8,128)(2,1)S(1)}, f16[152,256]{1,0:T(8,128)(2,1)S(1)}, u32[]{:S(2)}, u32[]{:S(2)}) collective-permute-start(f16[152,256]{1,0:T(8,128)(2,1)S(1)} %convert_element_type.34), channel_id=1, source_target_pairs={{16,0},{20,4},{24,8},{28,12},{17,1},{21,5},{25,9},{29,13},{18,2},{... | collective-permute-start | bytes 233480 | tf_op jit(solution)/shard_map/ppermute | solution.py:375
  35.5 5.9 %collective-permute-done.11 = f16[152,256]{1,0:T(8,128)(2,1)S(1)} collective-permute-done((f16[152,256]{1,0:T(8,128)(2,1)S(1)}, f16[152,256]{1,0:T(8,128)(2,1)S(1)}, u32[]{:S(2)}, u32[]{:S(2)}) %collective-permute-start.11) | collective-permute-done | bytes 77856 | tf_op jit(solution)/shard_map/ppermute | solution.py:375
  41.4 0.8 %shard_map.107 = (f32[144,256]{1,0:T(8,128)S(1)}, f32[152,256]{1,0:T(8,128)S(1)}, f32[144,256]{1,0:T(8,128)S(1)}) custom-call(s32[18]{0:T(128)S(1)} %get-tuple-element.31.sums_ref, f32[144,256]{1,0:T(8,128)S(1)} %get-tuple-element.34.late_ref.after_ref, f32[152,256]{1,0:T(8,128)S(1)} %convert_element_type.35.got_ref, f32[144,256]{1,0:T(8,128)S(1)} %get-tuple-element.38.refs_0_), custom_call_target="tpu_custom_call" | custom-call | tf_op jit(solution)/shard_map/pallas_call | solution.py:492
  42.2 0.0 collective-permute-done.13
  42.2 1.4 %shard_map.110 = f32[32,1,128]{2,1,0:T(1,128)} custom-call(f32[2]{0:T(128)S(1)} %get-tuple-element.42.wind_in, f32[144,256]{1,0:T(8,128)S(1)} %get-tuple-element.39.keep_ref, f32[144,256]{1,0:T(8,128)S(1)} %get-tuple-element.43.send_ref, f32[2,144,256]{2,1,0:T(8,128)S(1)} %get-tuple-element.44.z_ref, f32[2,152,256]{2,1,0:T(8,128)S(1)} %convert_element_type.39.zgot_ref), custom_call_target="tpu_custom_call" | custom-call | tf_op jit(solution)/shard_map/pallas_call | solution.py:499
  43.6 4.2 %all-to-all-start = ((f32[32,1,128]{2,1,0:T(1,128)}), f32[32,1,128]{2,1,0:T(1,128)S(1)}, u32[]{:S(2)}, u32[]{:S(2)}) async-start(f32[32,1,128]{2,1,0:T(1,128)} %shard_map.110), calls=%async_computation | async-start | bytes 32768 | tf_op jit(solution)/shard_map/all_to_all | solution.py:504
  47.8 1.8 %collective-permute-start.12 = (f16[152,256]{1,0:T(8,128)(2,1)S(1)}, f16[152,256]{1,0:T(8,128)(2,1)S(1)}, u32[]{:S(2)}, u32[]{:S(2)}) collective-permute-start(f16[152,256]{1,0:T(8,128)(2,1)S(1)} %convert_element_type.36), channel_id=1, source_target_pairs={{0,4},{4,0},{8,12},{12,8},{16,20},{20,16},{24,28},{28,24},{1,5},{5... | collective-permute-start | bytes 233480 | tf_op jit(solution)/shard_map/ppermute | solution.py:359
  49.6 5.2 %all-to-all-done = f32[32,1,128]{2,1,0:T(1,128)S(1)} async-done(((f32[32,1,128]{2,1,0:T(1,128)}), f32[32,1,128]{2,1,0:T(1,128)S(1)}, u32[]{:S(2)}, u32[]{:S(2)}) %all-to-all-start) | async-done | bytes 16416 | tf_op jit(solution)/shard_map/all_to_all | solution.py:504
  54.9 0.1 slice_reduce_fusion
  54.9 0.5 negate_multiply_fusion
  55.4 0.0 collective-permute-done.12
  55.5 1.6 %shard_map.108 = f32[2,128,512]{2,1,0:T(8,128)} custom-call(s32[32]{0:T(128)S(1)} %pad_add_fusion.2.sh_ref, s32[18]{0:T(128)S(1)} %get-tuple-element.31.sums_ref, f32[144,256]{1,0:T(8,128)S(1)} %get-tuple-element.39.keep_ref, f32[152,256]{1,0:T(8,128)S(1)} %convert_element_type.37.got_ref, f32[2,128,512]{2,1,0:T(8,128)S(1)} %get-tuple-element.41.loc_ref), custom_call_target="tpu_custom_call" | custom-call | bytes 1572864 | tf_op jit(solution)/shard_map/pallas_call | solution.py:505
  (10 shorter events, 0.1 us)
Async XLA Ops:
  0.6 17.5 %copy-start.1 = (s32[128,512]{1,0:T(8,128)S(1)}, s32[128,512]{1,0:T(8,128)}, u32[]{:S(2)}) copy-start(s32[128,512]{1,0:T(8,128)} %refs_8_.1) | copy-start | bytes 786436
  0.6 4.8 %copy-start.2 = (bf16[2,2,64,256]{3,2,1,0:T(8,128)(2,1)S(1)}, bf16[2,2,64,256]{3,2,1,0:T(8,128)(2,1)}, u32[]{:S(2)}) copy-start(bf16[2,2,64,256]{3,2,1,0:T(8,128)(2,1)} %refs_4_.1) | copy-start | bytes 393220
  2.4 3.6 %copy-start.3 = (s32[2,2]{1,0:T(2,128)S(1)}, s32[2,2]{1,0:T(2,128)}, u32[]{:S(2)}) copy-start(s32[2,2]{1,0:T(2,128)} %param.11) | copy-start | bytes 52
  2.4 9.9 %collective-permute-start.4 = (bf16[304,256]{1,0:T(8,128)(2,1)S(1)}, bf16[304,256]{1,0:T(8,128)(2,1)S(1)}, u32[]{:S(2)}, u32[]{:S(2)}) collective-permute-start(bf16[304,256]{1,0:T(8,128)(2,1)S(1)} %get-tuple-element.24.refs_0_), channel_id=1, source_target_pairs={{0,2},{1,3},{2,0},{3,1},{4,6},{5,7},{6,4},{7,5},{8,10},{9,11},{10,... | collective-permute-start | bytes 466952 | tf_op jit(solution)/shard_map/ppermute | solution.py:359
  5.4 6.8 %collective-permute-start.7 = (bf16[2,2,64,256]{3,2,1,0:T(8,128)(2,1)S(1)}, bf16[2,2,64,256]{3,2,1,0:T(8,128)(2,1)S(1)}, u32[]{:S(2)}, u32[]{:S(2)}) collective-permute-start(bf16[2,2,64,256]{3,2,1,0:T(8,128)(2,1)S(1)} %copy-done.2), channel_id=1, source_target_pairs={{0,2},{1,3},{2,0},{3,1},{4,6},{5,7},{6,4},{7,5},{8,10},{9,11},{10,... | collective-permute-start | bytes 393224 | tf_op jit(solution)/shard_map/ppermute | solution.py:359
  5.5 12.6 %collective-permute-start.3 = (bf16[304,256]{1,0:T(8,128)(2,1)S(1)}, bf16[304,256]{1,0:T(8,128)(2,1)S(1)}, u32[]{:S(2)}, u32[]{:S(2)}) collective-permute-start(bf16[304,256]{1,0:T(8,128)(2,1)S(1)} %get-tuple-element.24.refs_0_), channel_id=1, source_target_pairs={{0,1},{1,0},{2,3},{3,2},{4,5},{5,4},{6,7},{7,6},{8,9},{9,8},{10,11... | collective-permute-start | bytes 466952 | tf_op jit(solution)/shard_map/ppermute | solution.py:359
  5.5 12.6 %collective-permute-start.6 = (bf16[2,2,64,256]{3,2,1,0:T(8,128)(2,1)S(1)}, bf16[2,2,64,256]{3,2,1,0:T(8,128)(2,1)S(1)}, u32[]{:S(2)}, u32[]{:S(2)}) collective-permute-start(bf16[2,2,64,256]{3,2,1,0:T(8,128)(2,1)S(1)} %copy-done.2), channel_id=1, source_target_pairs={{0,1},{1,0},{2,3},{3,2},{4,5},{5,4},{6,7},{7,6},{8,9},{9,8},{10,11... | collective-permute-start | bytes 393224 | tf_op jit(solution)/shard_map/ppermute | solution.py:359
  6.1 3.6 %collective-permute-start = (s32[4]{0:T(128)S(1)}, s32[4]{0:T(128)S(1)}, u32[]{:S(2)}, u32[]{:S(2)}) collective-permute-start(s32[4]{0:T(128)S(1)} %reshape.7), channel_id=1, source_target_pairs={{0,4},{4,0},{8,12},{12,8},{16,20},{20,16},{24,28},{28,24},{1,5},{5... | collective-permute-start | bytes 56 | tf_op jit(solution)/shard_map/ppermute | solution.py:359
  9.8 3.6 %collective-permute-start.1 = (s32[8]{0:T(128)S(1)}, s32[8]{0:T(128)S(1)}, u32[]{:S(2)}, u32[]{:S(2)}) collective-permute-start(s32[8]{0:T(128)S(1)} %pad_add_fusion), channel_id=1, source_target_pairs={{0,8},{4,12},{8,0},{12,4},{16,24},{20,28},{24,16},{28,20},{1,9},{5... | collective-permute-start | bytes 104 | tf_op jit(solution)/shard_map/ppermute | solution.py:359
  12.3 5.8 %collective-permute-start.8 = (bf16[2,2,64,256]{3,2,1,0:T(8,128)(2,1)S(1)}, bf16[2,2,64,256]{3,2,1,0:T(8,128)(2,1)S(1)}, u32[]{:S(2)}, u32[]{:S(2)}) collective-permute-start(bf16[2,2,64,256]{3,2,1,0:T(8,128)(2,1)S(1)} %collective-permute-done.7.refs_6_), channel_id=1, source_target_pairs={{0,1},{1,0},{2,3},{3,2},{4,5},{5,4},{6,7},{7,6},{8,9},{9,8},{10,11... | collective-permute-start | bytes 393224 | tf_op jit(solution)/shard_map/ppermute | solution.py:359
  12.3 5.8 %collective-permute-start.5 = (bf16[304,256]{1,0:T(8,128)(2,1)S(1)}, bf16[304,256]{1,0:T(8,128)(2,1)S(1)}, u32[]{:S(2)}, u32[]{:S(2)}) collective-permute-start(bf16[304,256]{1,0:T(8,128)(2,1)S(1)} %collective-permute-done.4.refs_2_), channel_id=1, source_target_pairs={{0,1},{1,0},{2,3},{3,2},{4,5},{5,4},{6,7},{7,6},{8,9},{9,8},{10,11... | collective-permute-start | bytes 466952 | tf_op jit(solution)/shard_map/ppermute | solution.py:359
  13.4 4.6 %collective-permute-start.2 = (s32[16]{0:T(128)S(1)}, s32[16]{0:T(128)S(1)}, u32[]{:S(2)}, u32[]{:S(2)}) collective-permute-start(s32[16]{0:T(128)S(1)} %pad_add_fusion.1), channel_id=1, source_target_pairs={{0,16},{4,20},{8,24},{12,28},{16,0},{20,4},{24,8},{28,12},{1,17},{... | collective-permute-start | bytes 200 | tf_op jit(solution)/shard_map/ppermute | solution.py:359
  18.1 1.5 %copy-start = (bf16[2,128,512]{2,1,0:T(8,128)(2,1)S(1)}, bf16[2,128,512]{2,1,0:T(8,128)(2,1)}, u32[]{:S(2)}) copy-start(bf16[2,128,512]{2,1,0:T(8,128)(2,1)} %phases_ref.3) | copy-start | bytes 786436
  21.4 4.5 %collective-permute-start.9 = (f16[152,256]{1,0:T(8,128)(2,1)S(1)}, f16[152,256]{1,0:T(8,128)(2,1)S(1)}, u32[]{:S(2)}, u32[]{:S(2)}) collective-permute-start(f16[152,256]{1,0:T(8,128)(2,1)S(1)} %convert_element_type.30), channel_id=1, source_target_pairs={{0,4},{4,0},{8,12},{12,8},{16,20},{20,16},{24,28},{28,24},{1,5},{5... | collective-permute-start | bytes 233480 | tf_op jit(solution)/shard_map/ppermute | solution.py:359
  26.7 6.3 %collective-permute-start.10 = (f16[152,256]{1,0:T(8,128)(2,1)S(1)}, f16[152,256]{1,0:T(8,128)(2,1)S(1)}, u32[]{:S(2)}, u32[]{:S(2)}) collective-permute-start(f16[152,256]{1,0:T(8,128)(2,1)S(1)} %convert_element_type.32), channel_id=1, source_target_pairs={{8,0},{12,4},{16,8},{20,12},{24,16},{28,20},{9,1},{13,5},{17,9},{2... | collective-permute-start | bytes 233480 | tf_op jit(solution)/shard_map/ppermute | solution.py:375
  29.7 12.5 %collective-permute-start.13 = (f16[2,152,256]{2,1,0:T(8,128)(2,1)S(1)}, f16[2,152,256]{2,1,0:T(8,128)(2,1)S(1)}, u32[]{:S(2)}, u32[]{:S(2)}) collective-permute-start(f16[2,152,256]{2,1,0:T(8,128)(2,1)S(1)} %convert_element_type.38), channel_id=1, source_target_pairs={{0,4},{4,0},{8,12},{12,8},{16,20},{20,16},{24,28},{28,24},{1,5},{5... | collective-permute-start | bytes 466952 | tf_op jit(solution)/shard_map/ppermute | solution.py:359
  34.2 7.2 %collective-permute-start.11 = (f16[152,256]{1,0:T(8,128)(2,1)S(1)}, f16[152,256]{1,0:T(8,128)(2,1)S(1)}, u32[]{:S(2)}, u32[]{:S(2)}) collective-permute-start(f16[152,256]{1,0:T(8,128)(2,1)S(1)} %convert_element_type.34), channel_id=1, source_target_pairs={{16,0},{20,4},{24,8},{28,12},{17,1},{21,5},{25,9},{29,13},{18,2},{... | collective-permute-start | bytes 233480 | tf_op jit(solution)/shard_map/ppermute | solution.py:375
  43.6 11.3 %all-to-all-start = ((f32[32,1,128]{2,1,0:T(1,128)}), f32[32,1,128]{2,1,0:T(1,128)S(1)}, u32[]{:S(2)}, u32[]{:S(2)}) async-start(f32[32,1,128]{2,1,0:T(1,128)} %shard_map.110), calls=%async_computation | async-start | bytes 32768 | tf_op jit(solution)/shard_map/all_to_all | solution.py:504
  47.8 7.7 %collective-permute-start.12 = (f16[152,256]{1,0:T(8,128)(2,1)S(1)}, f16[152,256]{1,0:T(8,128)(2,1)S(1)}, u32[]{:S(2)}, u32[]{:S(2)}) collective-permute-start(f16[152,256]{1,0:T(8,128)(2,1)S(1)} %convert_element_type.36), channel_id=1, source_target_pairs={{0,4},{4,0},{8,12},{12,8},{16,20},{20,16},{24,28},{28,24},{1,5},{5... | collective-permute-start | bytes 233480 | tf_op jit(solution)/shard_map/ppermute | solution.py:359

commit v5 on v4

--- a/solution.py
+++ b/solution.py
@@ -164,10 +164,13 @@
     return jnp.where(y == 0, low, high), jnp.where(y == 0, high, low)
 
 
-def pack(ref, value):
-    rows, width = value.shape
+def exponent(value, width):
     top = jnp.full((8, width), jnp.maximum(jnp.max(jnp.abs(value)), 1e-30))
-    power = jnp.ceil(jnp.log2(top))
+    return jnp.ceil(jnp.log2(top))
+
+
+def pack(ref, value, power):
+    rows = value.shape[0]
     ref[:rows] = value * jnp.exp2(-power[:1])
     ref[rows:] = power
 
@@ -198,40 +201,35 @@
     sums_ref[2 * count + 1] = last[1]
 
 
-def segment_kernel(
-    sh_ref, g_ref, phases_ref, next_ref, loc_ref, keep_ref, send_ref, wind_ref, sums_ref
-):
+def segment_kernel(sh_ref, g_ref, loc_ref, keep_ref, send_ref, sums_ref):
     frames, rows, width = g_ref.shape
-    block = phases_ref.shape[1]
+    block = loc_ref.shape[1]
     halo = rows - block
     tm = lax.axis_index("tm")
     col = columns((rows, width))
     row = lax.broadcasted_iota(jnp.int32, (rows, width), 0)
-    down_sum = jnp.float32(0.0)
-    side_sum = jnp.float32(0.0)
     lam = g_ref[frames - 1]
     loc_ref[frames - 1] = lam[:block]
     for k in reversed(range(frames - 1)):
         a, b = sh_ref[2 * k], sh_ref[2 * k + 1]
         inside = (col < width - b) & (row < rows - a)
         prior = jnp.where(inside, decay_rate * turned(lam, rows - a, width - b), 0.0)
-        down, side = diffs(phases_ref, next_ref, k)
-        down_sum = down_sum + jnp.sum(prior[:block] * down)
-        side_sum = side_sum + jnp.sum(prior[:block] * side)
         lam = g_ref[k] + prior
         loc_ref[k] = lam[:block]
-    wind_ref[0] = down_sum
-    wind_ref[1] = side_sum
     fill_sums(sh_ref, frames, sums_ref)
     a_cum, b_cum = sums_ref[2 * tm], sums_ref[2 * tm + 1]
+    power = exponent(lam, width // 2)
     canvas = turned(lam, halo - a_cum, width - lax.rem(b_cum, width))
     canvas = jnp.where(row >= halo - a_cum, canvas, 0.0)
     keep, send = halves(canvas, tm % 2)
     keep_ref[...] = keep
-    pack(send_ref, send)
-
-
-def z_kernel(halo, sh_ref, sums_ref, phases_ref, next_ref, after_ref, keep_ref, send_ref):
+    pack(send_ref, send, power)
+
+
+def z_kernel(
+    halo, sh_ref, sums_ref, phases_ref, next_ref, g_ref, loc_ref, after_ref,
+    keep_ref, send_ref, wind_ref,
+):
     frames, block, width = phases_ref.shape
     tm = lax.axis_index("tm")
     a_cum, b_cum = sums_ref[2 * tm + 2], sums_ref[2 * tm + 3]
@@ -239,22 +237,28 @@
     col = columns((block, width))
     pad = jnp.zeros((halo, width), jnp.float32)
     sums = [jnp.zeros((block + halo, width), jnp.float32) for _ in range(2)]
+    winds = [jnp.float32(0.0), jnp.float32(0.0)]
     for k in reversed(range(frames)):
         a, b = sh_ref[2 * k], sh_ref[2 * k + 1]
         a_cum = a_cum - a
         b_cum = b_cum - b
         b_own = b_own + b
         for i, diff in enumerate(diffs(phases_ref, next_ref, k)):
+            if k < frames - 1:
+                winds[i] = winds[i] + jnp.sum((loc_ref[k] - g_ref[k, :block]) * diff)
             diff = jnp.where(col < width - b_own, decay_rate ** (frames - k) * diff, 0.0)
             diff = jnp.concatenate([diff, pad], axis=0)
             sums[i] = sums[i] + turned(diff, halo - a_cum, width - lax.rem(b_cum, width))
     for i in range(2):
         keep, send = halves(sums[i], tm % 2)
         keep_ref[i] = keep
-        pack(send_ref.at[i], send)
-
-
-def combine_kernel(frames, width, sums_ref, keep_ref, got_ref, late_ref, both_ref, send_ref):
+        pack(send_ref.at[i], send, exponent(send, width // 2))
+        wind_ref[i] = winds[i]
+
+
+def combine_kernel(
+    frames, width, sums_ref, keep_ref, sent_ref, got_ref, late_ref, both_ref, send_ref
+):
     rows, part = keep_ref.shape
     tm = lax.axis_index("tm")
     pair, y = tm // 2, tm % 2
@@ -266,10 +270,10 @@
     pos = columns((rows, part)) + y * part
     both = early + dropped(decay_rate**frames * late, pos, width, b_cum, b_cum - b_from)
     both_ref[...] = both
-    pack(send_ref, both)
-
-
-def later_pairs(frames, width, reach, sums_ref, got_ref):
+    pack(send_ref, both, jnp.maximum(sent_ref[rows:], got_ref[rows:]) + 1.0)
+
+
+def later_pairs(frames, width, reach, sums_ref, sent_ref, got_ref):
     rows = got_ref.shape[0] - 8
     part = got_ref.shape[1]
     tm = lax.axis_index("tm")
@@ -279,44 +283,42 @@
     got = jnp.where(pair + reach < pairs, unpack(got_ref), 0.0)
     b_cum = sums_ref[4 * jnp.minimum(pair + reach, pairs) + 1]
     b_from, b_next = sums_ref[4 * pair + 1], sums_ref[4 * pair + 5]
+    power = jnp.where(pair + reach < pairs, jnp.maximum(sent_ref[rows:], got_ref[rows:]), sent_ref[rows:])
     weight = decay_rate ** (2 * frames * reach)
     weight_next = decay_rate ** (2 * frames * (reach - 1))
     incl = dropped(weight * got, pos, width, b_cum, b_cum - b_from)
-    return incl, dropped(weight_next * got, pos, width, b_cum, b_cum - b_next)
-
-
-def step_kernel(frames, width, reach, sums_ref, both_ref, got_ref, *refs):
-    incl, excl = later_pairs(frames, width, reach, sums_ref, got_ref)
+    return incl, dropped(weight_next * got, pos, width, b_cum, b_cum - b_next), power
+
+
+def step_kernel(frames, width, reach, sums_ref, both_ref, sent_ref, got_ref, *refs):
+    incl, excl, power = later_pairs(frames, width, reach, sums_ref, sent_ref, got_ref)
     incl_ref, excl_ref, send_ref = refs[-3:]
     both = both_ref[...] + incl
     incl_ref[...] = both
     excl_ref[...] = excl + refs[0][...] if len(refs) == 4 else excl
-    pack(send_ref, both)
-
-
-def carry_kernel(frames, width, reach, sums_ref, late_ref, got_ref, *refs):
-    keep_ref, send_ref, raw_ref = refs[-3:]
+    pack(send_ref, both, power + 1.0)
+
+
+def carry_kernel(
+    frames, width, reach, sums_ref, wind_in, late_ref, sent_ref, got_ref, z_ref, zgot_ref, *refs
+):
+    keep_ref, send_ref, wind_ref = refs[-3:]
     rows, part = late_ref.shape
     tm = lax.axis_index("tm")
     pair, y = tm // 2, tm % 2
-    _, late = later_pairs(frames, width, reach, sums_ref, got_ref)
+    _, late, power = later_pairs(frames, width, reach, sums_ref, sent_ref, got_ref)
     if len(refs) == 4:
         late = late + refs[0][...]
     b_from, b_cum = sums_ref[4 * pair + 3], sums_ref[4 * pair + 5]
     pos = columns((rows, part)) + y * part
     moved = dropped(decay_rate**frames * late, pos, width, b_cum, b_cum - b_from)
     early = late_ref[...] + moved
-    keep_ref[...] = jnp.where(y == 0, early, late)
+    keep = jnp.where(y == 0, early, late)
     send = jnp.where(y == 0, late, early)
-    raw_ref[...] = send
-    pack(send_ref, send)
-
-
-def wind_kernel(wind_in, keep_ref, send_ref, z_ref, zgot_ref, wind_ref):
+    keep_ref[...] = keep
+    pack(send_ref, send, power + 2.0)
     sums = [
-        wind_in[i]
-        + jnp.sum(keep_ref[...] * z_ref[i] + send_ref[...] * unpack(zgot_ref.at[i]))
-        for i in range(2)
+        wind_in[i] + jnp.sum(keep * z_ref[i] + send * unpack(zgot_ref.at[i])) for i in range(2)
     ]
     lane = lax.broadcasted_iota(jnp.int32, wind_ref.shape, 2)
     wind_ref[...] = jnp.where(lane == 0, sums[0], jnp.where(lane == 1, sums[1], 0.0))
@@ -364,7 +366,8 @@
     held = {0: value}
     bit = count // 2
     while bit:
-        held.update({d ^ bit: swap(v, "rows", bit) for d, v in list(held.items())})
+        for d, v in list(held.items()):
+            held[d ^ bit] = swap(v, "rows", bit)
         bit //= 2
     return [held[d] for d in range(count)]
 
@@ -413,7 +416,8 @@
     sh_all = shifts.reshape(2 * frames)
     bit = 1
     while bit < n_tm:
-        sh_all = jnp.concatenate([sh_all, swap(sh_all, "tm", bit)])
+        other = swap(sh_all, "tm", bit)
+        sh_all = jnp.concatenate([sh_all, other])
         bit *= 2
     vmem = pl.BlockSpec(memory_space=pltpu.VMEM)
     smem = pl.BlockSpec(memory_space=pltpu.SMEM)
@@ -461,23 +465,24 @@
     )(*m_parts, *d_parts, pupil_mask, *kept)
     half_field = jax.ShapeDtypeStruct((rows, part), jnp.float32)
     message = jax.ShapeDtypeStruct((rows + 8, part), jnp.float32)
-    loc, keep, send, wind_local, sums_all = kernel_call(
+    loc, keep, send, sums_all = kernel_call(
         segment_kernel, 12,
-        (field, half_field, message, pair, jax.ShapeDtypeStruct((2 * n_tm + 2,), jnp.int32)),
-        [smem, vmem, vmem, vmem], (vmem, vmem, vmem, smem, smem),
-    )(sh_all, grads, phases, next_rows)
+        (field, half_field, message, jax.ShapeDtypeStruct((2 * n_tm + 2,), jnp.int32)),
+        [smem, vmem], (vmem, vmem, vmem, smem),
+    )(sh_all, grads)
     late, both, send = kernel_call(
         functools.partial(combine_kernel, frames, width), 6,
-        (half_field, half_field, message), [smem, vmem, vmem], (vmem, vmem, vmem),
-    )(sums_all, keep, swap_half(send))
-    z_keep, z_send = kernel_call(
+        (half_field, half_field, message), [smem] + [vmem] * 3, (vmem, vmem, vmem),
+    )(sums_all, keep, send, swap_half(send))
+    z_keep, z_send, wind_local = kernel_call(
         functools.partial(z_kernel, halo), 12,
         (
             jax.ShapeDtypeStruct((2, rows, part), jnp.float32),
             jax.ShapeDtypeStruct((2, rows + 8, part), jnp.float32),
+            pair,
         ),
-        [smem, smem, vmem, vmem, pl.BlockSpec(memory_space=pl.ANY)], (vmem, vmem),
-    )(sh_all, sums_all, phases, next_rows, late)
+        [smem, smem] + [vmem] * 4 + [pl.BlockSpec(memory_space=pl.ANY)], (vmem, vmem, smem),
+    )(sh_all, sums_all, phases, next_rows, grads, loc, late)
     z_got = swap_half(z_send)
     sums = []
     reach = 1
@@ -485,23 +490,18 @@
         both, excl, send = kernel_call(
             functools.partial(step_kernel, frames, width, reach), 6,
             (half_field, half_field, message),
-            [smem] + [vmem] * (2 + len(sums)), (vmem, vmem, vmem),
-        )(sums_all, both, from_later(send, reach), *sums)
+            [smem] + [vmem] * (3 + len(sums)), (vmem, vmem, vmem),
+        )(sums_all, both, send, from_later(send, reach), *sums)
         sums = [excl]
         reach *= 2
-    keep, send, raw = kernel_call(
-        functools.partial(carry_kernel, frames, width, reach), 6,
-        (half_field, message, half_field),
-        [smem] + [vmem] * (2 + len(sums)), (vmem, vmem, vmem),
-    )(sums_all, late, from_later(send, reach), *sums)
+    n_all = n_tm * n_rows
+    keep, send, wind = kernel_call(
+        functools.partial(carry_kernel, frames, width, reach), 8,
+        (half_field, message, jax.ShapeDtypeStruct((n_all, 1, LANES), jnp.float32)),
+        [smem, smem] + [vmem] * (5 + len(sums)), (vmem, vmem, vmem),
+    )(sums_all, wind_local, late, send, from_later(send, reach), z_keep, z_got, *sums)
+    winds = lax.all_to_all(wind, ("tm", "rows"), 0, 0)
     got = swap_half(send)
-    n_all = n_tm * n_rows
-    wind = kernel_call(
-        wind_kernel, 6,
-        jax.ShapeDtypeStruct((n_all, 1, LANES), jnp.float32),
-        [smem] + [vmem] * 4, vmem,
-    )(wind_local, keep, raw, z_keep, z_got)
-    winds = lax.all_to_all(wind, ("tm", "rows"), 0, 0)
     adjoint = kernel_call(
         final_kernel, 8, field, [smem, smem, vmem, vmem, vmem], vmem,
         cost=12 * frames * block * width,

time: 57.3 us -> 56.2 us (0.981)
  waiting for transfers between devices: 19.3 us -> 18.7 us
  Pallas kernels: 12.4 us -> 11.8 us
    pallas_call x3 -> x2, Pallas kernels: 3.86 us -> 2.9 us  [the longest x1 1.46 us: on_device(): kernel_call(functools.partial(carry_kernel, frames, width, reach), 8, (ha...]
where the time goes in v5:
time: 56.2 us; the launch traced here: 56 us
  starting transfers between devices  23.6 us (42%)
  waiting for transfers between devices  18.7 us (33%)
  Pallas kernels  11.8 us (21%)
  other arithmetic  0.93 us (2%)
  between operations  0.84 us (1%)
    ppermute x12, starting transfers between devices, swap(): return lax.ppermute(value, axis, [(s, s ^ bit) for s in range(count)])  16.8 us
    ppermute x2, waiting for transfers between devices, from_later(): lax.ppermute(value.astype(jnp.float16), 'tm', route).astype(jnp.float32)  6.75 us
    ppermute x12, waiting for transfers between devices, swap(): return lax.ppermute(value, axis, [(s, s ^ bit) for s in range(count)])  6.75 us
    all_to_all x1, waiting for transfers between devices, on_device(): winds = lax.all_to_all(wind, ('tm', 'rows'), 0, 0)  5.25 us
    all_to_all x1, starting transfers between devices, on_device(): winds = lax.all_to_all(wind, ('tm', 'rows'), 0, 0)  4.15 us
    ppermute x2, starting transfers between devices, from_later(): lax.ppermute(value.astype(jnp.float16), 'tm', route).astype(jnp.float32)  2.58 us
    pallas_call x1, Pallas kernels, on_device(): kernel_call(functools.partial(z_kernel, halo), 12, (jax.ShapeDtypeStruct(...  2.17 us
    pallas_call x1, Pallas kernels, on_device(): pl.pallas_call(functools.partial(y_kernel, halo), out_shape=[jax.ShapeDty...  1.74 us
  transfers between devices with their start and end apart: 15, of which 8 were waited for; matrix products, arithmetic and copies ran while one was open for 2% of the time, Pallas kernels for 6%

profile of v5, /device:TPU:0, one launch (start us, length us, event | category | flops | bytes accessed | tf_op | source)
XLA Modules:
  0.0 56.0 jit_solution(7815876766267814745)
XLA Ops:
  0.6 0.0 copy-start
  0.6 0.0 copy-start.2
  0.6 1.7 %transform.1 = (bf16[304,256]{1,0:T(8,128)(2,1)S(1)}, bf16[528,512]{1,0:T(8,128)(2,1)S(1)}, bf16[512,512]{1,0:T(8,128)(2,1)S(1)}, bf16[512,512]{1,0:T(8,128)(2,1)S(1)}, bf16[128,128]{1,0:T(8,128)(2,1)S(1)}) custom-call(bf16[2,128,512]{2,1,0:T(8,128)(2,1)} %phases_ref.1, s32[128,512]{1,0:T(8,128)} %refs_8_.1, bf16[512,256]{1,0:T(8,128)(2,1)} %constant.15.clone.half_hbm, ...), custom_call_target="tpu_custom_call" | custom-call | tf_op jit(solution)/shard_map/transform/pallas_call | solution.py:426
  2.4 0.0 copy-start.3
  2.4 3.0 %collective-permute-start.4 = (bf16[304,256]{1,0:T(8,128)(2,1)S(1)}, bf16[304,256]{1,0:T(8,128)(2,1)S(1)}, u32[]{:S(2)}, u32[]{:S(2)}) collective-permute-start(bf16[304,256]{1,0:T(8,128)(2,1)S(1)} %get-tuple-element.24.refs_0_), channel_id=1, source_target_pairs={{0,2},{1,3},{2,0},{3,1},{4,6},{5,7},{6,4},{7,5},{8,10},{9,11},{10,... | collective-permute-start | bytes 466952 | tf_op jit(solution)/shard_map/ppermute | solution.py:361
  5.4 0.0 copy-done.2
  5.4 0.1 collective-permute-start.7
  5.5 0.0 collective-permute-start.3
  5.5 0.5 collective-permute-start.6
  6.0 0.0 copy-done.3
  6.0 0.1 reshape.7
  6.1 2.0 %collective-permute-start = (s32[4]{0:T(128)S(1)}, s32[4]{0:T(128)S(1)}, u32[]{:S(2)}, u32[]{:S(2)}) collective-permute-start(s32[4]{0:T(128)S(1)} %reshape.7), channel_id=1, source_target_pairs={{0,4},{4,0},{8,12},{12,8},{16,20},{20,16},{24,28},{28,24},{1,5},{5... | collective-permute-start | bytes 56 | tf_op jit(solution)/shard_map/ppermute | solution.py:361
  8.1 1.6 %collective-permute-done = s32[4]{0:T(128)S(1)} collective-permute-done((s32[4]{0:T(128)S(1)}, s32[4]{0:T(128)S(1)}, u32[]{:S(2)}, u32[]{:S(2)}) %collective-permute-start) | collective-permute-done | bytes 48 | tf_op jit(solution)/shard_map/ppermute | solution.py:361
  9.7 0.1 pad_add_fusion
  9.8 2.0 %collective-permute-start.1 = (s32[8]{0:T(128)S(1)}, s32[8]{0:T(128)S(1)}, u32[]{:S(2)}, u32[]{:S(2)}) collective-permute-start(s32[8]{0:T(128)S(1)} %pad_add_fusion), channel_id=1, source_target_pairs={{0,8},{4,12},{8,0},{12,4},{16,24},{20,28},{24,16},{28,20},{1,9},{5... | collective-permute-start | bytes 104 | tf_op jit(solution)/shard_map/ppermute | solution.py:361
  11.8 0.5 collective-permute-done.7.refs_6_
  12.3 0.0 collective-permute-start.8
  12.3 0.0 collective-permute-done.4.refs_2_
  12.3 0.5 collective-permute-start.5
  12.8 0.6 collective-permute-done.1
  13.3 0.1 pad_add_fusion.1
  13.4 3.0 %collective-permute-start.2 = (s32[16]{0:T(128)S(1)}, s32[16]{0:T(128)S(1)}, u32[]{:S(2)}, u32[]{:S(2)}) collective-permute-start(s32[16]{0:T(128)S(1)} %pad_add_fusion.1), channel_id=1, source_target_pairs={{0,16},{4,20},{8,24},{12,28},{16,0},{20,4},{24,8},{28,12},{1,17},{... | collective-permute-start | bytes 200 | tf_op jit(solution)/shard_map/ppermute | solution.py:361
  16.5 1.5 %collective-permute-done.2 = s32[16]{0:T(128)S(1)} collective-permute-done((s32[16]{0:T(128)S(1)}, s32[16]{0:T(128)S(1)}, u32[]{:S(2)}, u32[]{:S(2)}) %collective-permute-start.2) | collective-permute-done | bytes 96 | tf_op jit(solution)/shard_map/ppermute | solution.py:361
  18.0 0.1 pad_add_fusion.2.sh_ref
  18.1 0.0 collective-permute-done.6.refs_5_
  18.1 0.0 collective-permute-done.3.refs_1_
  18.1 0.0 collective-permute-done.8.refs_7_
  18.1 0.0 collective-permute-done.5.refs_3_
  18.1 0.0 copy-done
  18.1 1.5 %grad.1 = (f32[2,144,512]{2,1,0:T(8,128)S(1)}, f32[8,512]{1,0:T(8,128)S(1)}) custom-call(bf16[304,256]{1,0:T(8,128)(2,1)S(1)} %get-tuple-element.24.refs_0_, bf16[304,256]{1,0:T(8,128)(2,1)S(1)} %collective-permute-done.3.refs_1_, bf16[304,256]{1,0:T(8,128)(2,1)S(1)} %collective-permute-done.4.refs_2_, bf16[304,256]{1,0:T(8,128)(2,1)S(1)} %collective-permute-done.5.refs_3_, ...), custom_call_target="tpu_custom_call" | custom-call | tf_op jit(solution)/shard_map/grad/pallas_call | solution.py:447
  19.6 1.4 %shard_map.104 = (f32[2,128,512]{2,1,0:T(8,128)S(1)}, f32[144,256]{1,0:T(8,128)S(1)}, f32[152,256]{1,0:T(8,128)S(1)}, s32[18]{0:T(128)S(1)}) custom-call(s32[32]{0:T(128)S(1)} %pad_add_fusion.2.sh_ref, f32[2,144,512]{2,1,0:T(8,128)S(1)} %get-tuple-element.29.g_ref), custom_call_target="tpu_custom_call" | custom-call | tf_op jit(solution)/shard_map/pallas_call | solution.py:468
  21.1 1.9 %collective-permute-start.9 = (f16[152,256]{1,0:T(8,128)(2,1)S(1)}, f16[152,256]{1,0:T(8,128)(2,1)S(1)}, u32[]{:S(2)}, u32[]{:S(2)}) collective-permute-start(f16[152,256]{1,0:T(8,128)(2,1)S(1)} %convert_element_type.30), channel_id=1, source_target_pairs={{0,4},{4,0},{8,12},{12,8},{16,20},{20,16},{24,28},{28,24},{1,5},{5... | collective-permute-start | bytes 233480 | tf_op jit(solution)/shard_map/ppermute | solution.py:361
  23.0 2.5 %collective-permute-done.9 = f16[152,256]{1,0:T(8,128)(2,1)S(1)} collective-permute-done((f16[152,256]{1,0:T(8,128)(2,1)S(1)}, f16[152,256]{1,0:T(8,128)(2,1)S(1)}, u32[]{:S(2)}, u32[]{:S(2)}) %collective-permute-start.9) | collective-permute-done | bytes 77856 | tf_op jit(solution)/shard_map/ppermute | solution.py:361
  25.6 0.0 copy-start.1
  25.6 0.6 %shard_map.105 = (f32[144,256]{1,0:T(8,128)S(1)}, f32[144,256]{1,0:T(8,128)S(1)}, f32[152,256]{1,0:T(8,128)S(1)}) custom-call(s32[18]{0:T(128)S(1)} %get-tuple-element.30.sums_ref, f32[144,256]{1,0:T(8,128)S(1)} %get-tuple-element.33.keep_ref, f32[152,256]{1,0:T(8,128)S(1)} %get-tuple-element.34.sent_ref, f32[152,256]{1,0:T(8,128)S(1)} %convert_element_type.31.got_ref), custom_call_target="tpu_custom_call" | custom-call | tf_op jit(solution)/shard_map/pallas_call | solution.py:473
  26.2 1.3 %collective-permute-start.10 = (f16[152,256]{1,0:T(8,128)(2,1)S(1)}, f16[152,256]{1,0:T(8,128)(2,1)S(1)}, u32[]{:S(2)}, u32[]{:S(2)}) collective-permute-start(f16[152,256]{1,0:T(8,128)(2,1)S(1)} %convert_element_type.32), channel_id=1, source_target_pairs={{8,0},{12,4},{16,8},{20,12},{24,16},{28,20},{9,1},{13,5},{17,9},{2... | collective-permute-start | bytes 233480 | tf_op jit(solution)/shard_map/ppermute | solution.py:378
  27.5 0.0 copy-done.1
  27.5 2.2 %shard_map.106 = (f32[2,144,256]{2,1,0:T(8,128)S(1)}, f32[2,152,256]{2,1,0:T(8,128)S(1)}, f32[2]{0:T(128)S(1)}) custom-call(s32[32]{0:T(128)S(1)} %pad_add_fusion.2.sh_ref, s32[18]{0:T(128)S(1)} %get-tuple-element.30.sums_ref, bf16[2,128,512]{2,1,0:T(8,128)(2,1)S(1)} %copy-done.1, f32[8,512]{1,0:T(8,128)S(1)} %get-tuple-element.31.next_ref, ...), custom_call_target="tpu_custom_call" | custom-call | tf_op jit(solution)/shard_map/pallas_call | solution.py:477
  29.8 1.9 %collective-permute-start.12 = (f16[2,152,256]{2,1,0:T(8,128)(2,1)S(1)}, f16[2,152,256]{2,1,0:T(8,128)(2,1)S(1)}, u32[]{:S(2)}, u32[]{:S(2)}) collective-permute-start(f16[2,152,256]{2,1,0:T(8,128)(2,1)S(1)} %convert_element_type.36), channel_id=1, source_target_pairs={{0,4},{4,0},{8,12},{12,8},{16,20},{20,16},{24,28},{28,24},{1,5},{5... | collective-permute-start | bytes 466952 | tf_op jit(solution)/shard_map/ppermute | solution.py:361
  31.7 0.9 %collective-permute-done.10 = f16[152,256]{1,0:T(8,128)(2,1)S(1)} collective-permute-done((f16[152,256]{1,0:T(8,128)(2,1)S(1)}, f16[152,256]{1,0:T(8,128)(2,1)S(1)}, u32[]{:S(2)}, u32[]{:S(2)}) %collective-permute-start.10) | collective-permute-done | bytes 77856 | tf_op jit(solution)/shard_map/ppermute | solution.py:378
  32.5 1.3 %shard_map.107 = (f32[144,256]{1,0:T(8,128)}, f32[144,256]{1,0:T(8,128)S(1)}, f32[152,256]{1,0:T(8,128)S(1)}) custom-call(s32[18]{0:T(128)S(1)} %get-tuple-element.30.sums_ref, f32[144,256]{1,0:T(8,128)S(1)} %get-tuple-element.37.both_ref, f32[152,256]{1,0:T(8,128)S(1)} %get-tuple-element.38.sent_ref, f32[152,256]{1,0:T(8,128)S(1)} %convert_element_type.33.got_ref), custom_call_target="tpu_custom_call" | custom-call | tf_op jit(solution)/shard_map/pallas_call | solution.py:490
  33.8 1.3 %collective-permute-start.11 = (f16[152,256]{1,0:T(8,128)(2,1)S(1)}, f16[152,256]{1,0:T(8,128)(2,1)S(1)}, u32[]{:S(2)}, u32[]{:S(2)}) collective-permute-start(f16[152,256]{1,0:T(8,128)(2,1)S(1)} %convert_element_type.34), channel_id=1, source_target_pairs={{16,0},{20,4},{24,8},{28,12},{17,1},{21,5},{25,9},{29,13},{18,2},{... | collective-permute-start | bytes 233480 | tf_op jit(solution)/shard_map/ppermute | solution.py:378
  35.1 5.9 %collective-permute-done.11 = f16[152,256]{1,0:T(8,128)(2,1)S(1)} collective-permute-done((f16[152,256]{1,0:T(8,128)(2,1)S(1)}, f16[152,256]{1,0:T(8,128)(2,1)S(1)}, u32[]{:S(2)}, u32[]{:S(2)}) %collective-permute-start.11) | collective-permute-done | bytes 77856 | tf_op jit(solution)/shard_map/ppermute | solution.py:378
  41.0 0.0 collective-permute-done.12
  41.1 1.5 %shard_map.108 = (f32[144,256]{1,0:T(8,128)S(1)}, f32[152,256]{1,0:T(8,128)S(1)}, f32[32,1,128]{2,1,0:T(1,128)}) custom-call(s32[18]{0:T(128)S(1)} %get-tuple-element.30.sums_ref, f32[2]{0:T(128)S(1)} %get-tuple-element.36.wind_in, f32[144,256]{1,0:T(8,128)S(1)} %get-tuple-element.35.after_ref.late_ref, f32[152,256]{1,0:T(8,128)S(1)} %get-tuple-element.39.sent_ref, ...), custom_call_target="tpu_custom_call" | custom-call | tf_op jit(solution)/shard_map/pallas_call | solution.py:498
  42.5 4.2 %all-to-all-start = ((f32[32,1,128]{2,1,0:T(1,128)}), f32[32,1,128]{2,1,0:T(1,128)S(1)}, u32[]{:S(2)}, u32[]{:S(2)}) async-start(f32[32,1,128]{2,1,0:T(1,128)} %get-tuple-element.45), calls=%async_computation | async-start | bytes 32768 | tf_op jit(solution)/shard_map/all_to_all | solution.py:503
  46.7 1.8 %collective-permute-start.13 = (f16[152,256]{1,0:T(8,128)(2,1)S(1)}, f16[152,256]{1,0:T(8,128)(2,1)S(1)}, u32[]{:S(2)}, u32[]{:S(2)}) collective-permute-start(f16[152,256]{1,0:T(8,128)(2,1)S(1)} %convert_element_type.38), channel_id=1, source_target_pairs={{0,4},{4,0},{8,12},{12,8},{16,20},{20,16},{24,28},{28,24},{1,5},{5... | collective-permute-start | bytes 233480 | tf_op jit(solution)/shard_map/ppermute | solution.py:361
  48.5 5.2 %all-to-all-done = f32[32,1,128]{2,1,0:T(1,128)S(1)} async-done(((f32[32,1,128]{2,1,0:T(1,128)}), f32[32,1,128]{2,1,0:T(1,128)S(1)}, u32[]{:S(2)}, u32[]{:S(2)}) %all-to-all-start) | async-done | bytes 16416 | tf_op jit(solution)/shard_map/all_to_all | solution.py:503
  53.8 0.1 slice_reduce_fusion
  53.8 0.5 negate_multiply_fusion
  54.3 0.0 collective-permute-done.13
  54.4 1.6 %shard_map.109 = f32[2,128,512]{2,1,0:T(8,128)} custom-call(s32[32]{0:T(128)S(1)} %pad_add_fusion.2.sh_ref, s32[18]{0:T(128)S(1)} %get-tuple-element.30.sums_ref, f32[144,256]{1,0:T(8,128)S(1)} %get-tuple-element.43.keep_ref, f32[152,256]{1,0:T(8,128)S(1)} %convert_element_type.39.got_ref, f32[2,128,512]{2,1,0:T(8,128)S(1)} %get-tuple-element.32.loc_ref), custom_call_target="tpu_custom_call" | custom-call | bytes 1572864 | tf_op jit(solution)/shard_map/pallas_call | solution.py:505
  (10 shorter events, 0.1 us)
Async XLA Ops:
  0.6 17.5 %copy-start = (s32[128,512]{1,0:T(8,128)S(1)}, s32[128,512]{1,0:T(8,128)}, u32[]{:S(2)}) copy-start(s32[128,512]{1,0:T(8,128)} %refs_8_.1) | copy-start | bytes 786436
  0.6 4.8 %copy-start.2 = (bf16[2,2,64,256]{3,2,1,0:T(8,128)(2,1)S(1)}, bf16[2,2,64,256]{3,2,1,0:T(8,128)(2,1)}, u32[]{:S(2)}) copy-start(bf16[2,2,64,256]{3,2,1,0:T(8,128)(2,1)} %refs_4_.1) | copy-start | bytes 393220
  2.4 3.6 %copy-start.3 = (s32[2,2]{1,0:T(2,128)S(1)}, s32[2,2]{1,0:T(2,128)}, u32[]{:S(2)}) copy-start(s32[2,2]{1,0:T(2,128)} %param.11) | copy-start | bytes 52
  2.4 9.9 %collective-permute-start.4 = (bf16[304,256]{1,0:T(8,128)(2,1)S(1)}, bf16[304,256]{1,0:T(8,128)(2,1)S(1)}, u32[]{:S(2)}, u32[]{:S(2)}) collective-permute-start(bf16[304,256]{1,0:T(8,128)(2,1)S(1)} %get-tuple-element.24.refs_0_), channel_id=1, source_target_pairs={{0,2},{1,3},{2,0},{3,1},{4,6},{5,7},{6,4},{7,5},{8,10},{9,11},{10,... | collective-permute-start | bytes 466952 | tf_op jit(solution)/shard_map/ppermute | solution.py:361
  5.4 6.8 %collective-permute-start.7 = (bf16[2,2,64,256]{3,2,1,0:T(8,128)(2,1)S(1)}, bf16[2,2,64,256]{3,2,1,0:T(8,128)(2,1)S(1)}, u32[]{:S(2)}, u32[]{:S(2)}) collective-permute-start(bf16[2,2,64,256]{3,2,1,0:T(8,128)(2,1)S(1)} %copy-done.2), channel_id=1, source_target_pairs={{0,2},{1,3},{2,0},{3,1},{4,6},{5,7},{6,4},{7,5},{8,10},{9,11},{10,... | collective-permute-start | bytes 393224 | tf_op jit(solution)/shard_map/ppermute | solution.py:361
  5.5 12.6 %collective-permute-start.3 = (bf16[304,256]{1,0:T(8,128)(2,1)S(1)}, bf16[304,256]{1,0:T(8,128)(2,1)S(1)}, u32[]{:S(2)}, u32[]{:S(2)}) collective-permute-start(bf16[304,256]{1,0:T(8,128)(2,1)S(1)} %get-tuple-element.24.refs_0_), channel_id=1, source_target_pairs={{0,1},{1,0},{2,3},{3,2},{4,5},{5,4},{6,7},{7,6},{8,9},{9,8},{10,11... | collective-permute-start | bytes 466952 | tf_op jit(solution)/shard_map/ppermute | solution.py:361
  5.5 12.6 %collective-permute-start.6 = (bf16[2,2,64,256]{3,2,1,0:T(8,128)(2,1)S(1)}, bf16[2,2,64,256]{3,2,1,0:T(8,128)(2,1)S(1)}, u32[]{:S(2)}, u32[]{:S(2)}) collective-permute-start(bf16[2,2,64,256]{3,2,1,0:T(8,128)(2,1)S(1)} %copy-done.2), channel_id=1, source_target_pairs={{0,1},{1,0},{2,3},{3,2},{4,5},{5,4},{6,7},{7,6},{8,9},{9,8},{10,11... | collective-permute-start | bytes 393224 | tf_op jit(solution)/shard_map/ppermute | solution.py:361
  6.1 3.6 %collective-permute-start = (s32[4]{0:T(128)S(1)}, s32[4]{0:T(128)S(1)}, u32[]{:S(2)}, u32[]{:S(2)}) collective-permute-start(s32[4]{0:T(128)S(1)} %reshape.7), channel_id=1, source_target_pairs={{0,4},{4,0},{8,12},{12,8},{16,20},{20,16},{24,28},{28,24},{1,5},{5... | collective-permute-start | bytes 56 | tf_op jit(solution)/shard_map/ppermute | solution.py:361
  9.8 3.6 %collective-permute-start.1 = (s32[8]{0:T(128)S(1)}, s32[8]{0:T(128)S(1)}, u32[]{:S(2)}, u32[]{:S(2)}) collective-permute-start(s32[8]{0:T(128)S(1)} %pad_add_fusion), channel_id=1, source_target_pairs={{0,8},{4,12},{8,0},{12,4},{16,24},{20,28},{24,16},{28,20},{1,9},{5... | collective-permute-start | bytes 104 | tf_op jit(solution)/shard_map/ppermute | solution.py:361
  12.3 5.8 %collective-permute-start.8 = (bf16[2,2,64,256]{3,2,1,0:T(8,128)(2,1)S(1)}, bf16[2,2,64,256]{3,2,1,0:T(8,128)(2,1)S(1)}, u32[]{:S(2)}, u32[]{:S(2)}) collective-permute-start(bf16[2,2,64,256]{3,2,1,0:T(8,128)(2,1)S(1)} %collective-permute-done.7.refs_6_), channel_id=1, source_target_pairs={{0,1},{1,0},{2,3},{3,2},{4,5},{5,4},{6,7},{7,6},{8,9},{9,8},{10,11... | collective-permute-start | bytes 393224 | tf_op jit(solution)/shard_map/ppermute | solution.py:361
  12.3 5.8 %collective-permute-start.5 = (bf16[304,256]{1,0:T(8,128)(2,1)S(1)}, bf16[304,256]{1,0:T(8,128)(2,1)S(1)}, u32[]{:S(2)}, u32[]{:S(2)}) collective-permute-start(bf16[304,256]{1,0:T(8,128)(2,1)S(1)} %collective-permute-done.4.refs_2_), channel_id=1, source_target_pairs={{0,1},{1,0},{2,3},{3,2},{4,5},{5,4},{6,7},{7,6},{8,9},{9,8},{10,11... | collective-permute-start | bytes 466952 | tf_op jit(solution)/shard_map/ppermute | solution.py:361
  13.4 4.6 %collective-permute-start.2 = (s32[16]{0:T(128)S(1)}, s32[16]{0:T(128)S(1)}, u32[]{:S(2)}, u32[]{:S(2)}) collective-permute-start(s32[16]{0:T(128)S(1)} %pad_add_fusion.1), channel_id=1, source_target_pairs={{0,16},{4,20},{8,24},{12,28},{16,0},{20,4},{24,8},{28,12},{1,17},{... | collective-permute-start | bytes 200 | tf_op jit(solution)/shard_map/ppermute | solution.py:361
  21.1 4.5 %collective-permute-start.9 = (f16[152,256]{1,0:T(8,128)(2,1)S(1)}, f16[152,256]{1,0:T(8,128)(2,1)S(1)}, u32[]{:S(2)}, u32[]{:S(2)}) collective-permute-start(f16[152,256]{1,0:T(8,128)(2,1)S(1)} %convert_element_type.30), channel_id=1, source_target_pairs={{0,4},{4,0},{8,12},{12,8},{16,20},{20,16},{24,28},{28,24},{1,5},{5... | collective-permute-start | bytes 233480 | tf_op jit(solution)/shard_map/ppermute | solution.py:361
  25.6 2.0 %copy-start.1 = (bf16[2,128,512]{2,1,0:T(8,128)(2,1)S(1)}, bf16[2,128,512]{2,1,0:T(8,128)(2,1)}, u32[]{:S(2)}) copy-start(bf16[2,128,512]{2,1,0:T(8,128)(2,1)} %phases_ref.1) | copy-start | bytes 786436
  26.2 6.3 %collective-permute-start.10 = (f16[152,256]{1,0:T(8,128)(2,1)S(1)}, f16[152,256]{1,0:T(8,128)(2,1)S(1)}, u32[]{:S(2)}, u32[]{:S(2)}) collective-permute-start(f16[152,256]{1,0:T(8,128)(2,1)S(1)} %convert_element_type.32), channel_id=1, source_target_pairs={{8,0},{12,4},{16,8},{20,12},{24,16},{28,20},{9,1},{13,5},{17,9},{2... | collective-permute-start | bytes 233480 | tf_op jit(solution)/shard_map/ppermute | solution.py:378
  29.8 11.3 %collective-permute-start.12 = (f16[2,152,256]{2,1,0:T(8,128)(2,1)S(1)}, f16[2,152,256]{2,1,0:T(8,128)(2,1)S(1)}, u32[]{:S(2)}, u32[]{:S(2)}) collective-permute-start(f16[2,152,256]{2,1,0:T(8,128)(2,1)S(1)} %convert_element_type.36), channel_id=1, source_target_pairs={{0,4},{4,0},{8,12},{12,8},{16,20},{20,16},{24,28},{28,24},{1,5},{5... | collective-permute-start | bytes 466952 | tf_op jit(solution)/shard_map/ppermute | solution.py:361
  33.8 7.2 %collective-permute-start.11 = (f16[152,256]{1,0:T(8,128)(2,1)S(1)}, f16[152,256]{1,0:T(8,128)(2,1)S(1)}, u32[]{:S(2)}, u32[]{:S(2)}) collective-permute-start(f16[152,256]{1,0:T(8,128)(2,1)S(1)} %convert_element_type.34), channel_id=1, source_target_pairs={{16,0},{20,4},{24,8},{28,12},{17,1},{21,5},{25,9},{29,13},{18,2},{... | collective-permute-start | bytes 233480 | tf_op jit(solution)/shard_map/ppermute | solution.py:378
  42.5 11.3 %all-to-all-start = ((f32[32,1,128]{2,1,0:T(1,128)}), f32[32,1,128]{2,1,0:T(1,128)S(1)}, u32[]{:S(2)}, u32[]{:S(2)}) async-start(f32[32,1,128]{2,1,0:T(1,128)} %get-tuple-element.45), calls=%async_computation | async-start | bytes 32768 | tf_op jit(solution)/shard_map/all_to_all | solution.py:503
  46.7 7.7 %collective-permute-start.13 = (f16[152,256]{1,0:T(8,128)(2,1)S(1)}, f16[152,256]{1,0:T(8,128)(2,1)S(1)}, u32[]{:S(2)}, u32[]{:S(2)}) collective-permute-start(f16[152,256]{1,0:T(8,128)(2,1)S(1)} %convert_element_type.38), channel_id=1, source_target_pairs={{0,4},{4,0},{8,12},{12,8},{16,20},{20,16},{24,28},{28,24},{1,5},{5... | collective-permute-start | bytes 233480 | tf_op jit(solution)/shard_map/ppermute | solution.py:361

commit v6 on v5

--- a/solution.py
+++ b/solution.py
@@ -22,11 +22,6 @@
     cos_t = (np.cos(angle) * factor).astype(jnp.bfloat16)
     sin_t = (-np.sin(angle) * factor).astype(jnp.bfloat16)
     return np.concatenate([cos_t, sin_t], axis=0)
-
-
-def own_shift(sh_ref, frames, j, k):
-    at = 2 * ((j ^ lax.axis_index("tm")) * frames + k)
-    return sh_ref[at], sh_ref[at + 1]
 
 
 def dot(a, b):
@@ -158,161 +153,145 @@
         g_ref[k, block:] = jnp.where(live_over, g[block:], 0.0)
 
 
-def halves(value, y):
-    width = value.shape[1]
-    low, high = value[:, : width // 2], value[:, width // 2 :]
+def halves(value, rows, start, y):
+    low, high = value[:rows], value[start : start + rows]
     return jnp.where(y == 0, low, high), jnp.where(y == 0, high, low)
+
+
+def back(value, down, right):
+    rows, width = value.shape
+    row = lax.broadcasted_iota(jnp.int32, value.shape, 0)
+    inside = (columns(value.shape) < width - right) & (row < rows - down)
+    return jnp.where(inside, turned(value, rows - down, width - right), 0.0)
+
+
+def own_shifts(sh_ref, first, stop):
+    down, right = jnp.int32(0), jnp.int32(0)
+    for k in range(first, stop):
+        down, right = down + sh_ref[2 * k], right + sh_ref[2 * k + 1]
+    return down, right
 
 
 def exponent(value, width):
     top = jnp.full((8, width), jnp.maximum(jnp.max(jnp.abs(value)), 1e-30))
-    return jnp.ceil(jnp.log2(top))
-
-
-def pack(ref, value, power):
+    return jnp.ceil(jnp.log2(top))[:1]
+
+
+def pack(ref, value, power, down=0, right=0):
     rows = value.shape[0]
-    ref[:rows] = value * jnp.exp2(-power[:1])
-    ref[rows:] = power
+    ref[:rows] = value * jnp.exp2(-power)
+    line = lax.broadcasted_iota(jnp.int32, (8, value.shape[1]), 0)
+    shift = jnp.where(line == 1, down, right).astype(jnp.float32)
+    ref[rows:] = jnp.where(line == 0, power, shift)
+
+
+def power_of(ref):
+    rows = ref.shape[0] - 8
+    return ref[rows : rows + 1]
+
+
+def shift_of(ref):
+    rows = ref.shape[0] - 8
+    return ref[rows + 1, 0].astype(jnp.int32), ref[rows + 2, 0].astype(jnp.int32)
 
 
 def unpack(ref):
-    rows = ref.shape[0] - 8
-    return ref[:rows] * jnp.exp2(ref[rows : rows + 1])
-
-
-def dropped(value, pos, width, b_cum, b_here):
-    c = pos + lax.rem(b_cum, width)
-    c = jnp.where(c >= width, c - width, c)
-    return jnp.where(c >= b_here, value, 0.0)
-
-
-def fill_sums(sh_ref, frames, sums_ref):
-    def add(j, sums):
-        sums_ref[2 * j] = sums[0]
-        sums_ref[2 * j + 1] = sums[1]
-        for k in range(frames):
-            a, b = own_shift(sh_ref, frames, j, k)
-            sums = (sums[0] + a, sums[1] + b)
-        return sums
-
-    count = lax.axis_size("tm")
-    last = lax.fori_loop(0, count, add, (jnp.int32(0), jnp.int32(0)))
-    sums_ref[2 * count] = last[0]
-    sums_ref[2 * count + 1] = last[1]
-
-
-def segment_kernel(sh_ref, g_ref, loc_ref, keep_ref, send_ref, sums_ref):
-    frames, rows, width = g_ref.shape
-    block = loc_ref.shape[1]
-    halo = rows - block
-    tm = lax.axis_index("tm")
-    col = columns((rows, width))
-    row = lax.broadcasted_iota(jnp.int32, (rows, width), 0)
+    return ref[: ref.shape[0] - 8] * jnp.exp2(power_of(ref))
+
+
+def segment_kernel(sh_ref, g_ref, loc_ref, keep_ref, send_ref):
+    frames, block, _ = loc_ref.shape
     lam = g_ref[frames - 1]
     loc_ref[frames - 1] = lam[:block]
     for k in reversed(range(frames - 1)):
-        a, b = sh_ref[2 * k], sh_ref[2 * k + 1]
-        inside = (col < width - b) & (row < rows - a)
-        prior = jnp.where(inside, decay_rate * turned(lam, rows - a, width - b), 0.0)
-        lam = g_ref[k] + prior
+        lam = g_ref[k] + decay_rate * back(lam, sh_ref[2 * k], sh_ref[2 * k + 1])
         loc_ref[k] = lam[:block]
-    fill_sums(sh_ref, frames, sums_ref)
-    a_cum, b_cum = sums_ref[2 * tm], sums_ref[2 * tm + 1]
-    power = exponent(lam, width // 2)
-    canvas = turned(lam, halo - a_cum, width - lax.rem(b_cum, width))
-    canvas = jnp.where(row >= halo - a_cum, canvas, 0.0)
-    keep, send = halves(canvas, tm % 2)
+    keep, send = halves(lam, keep_ref.shape[0], block // 2, lax.axis_index("tm") % 2)
     keep_ref[...] = keep
-    pack(send_ref, send, power)
+    pack(send_ref, send, exponent(lam, lam.shape[1]), *own_shifts(sh_ref, 0, frames))
 
 
 def z_kernel(
-    halo, sh_ref, sums_ref, phases_ref, next_ref, g_ref, loc_ref, after_ref,
-    keep_ref, send_ref, wind_ref,
+    sh_ref, phases_ref, next_ref, g_ref, loc_ref, after_ref, keep_ref, send_ref, wind_ref
 ):
     frames, block, width = phases_ref.shape
-    tm = lax.axis_index("tm")
-    a_cum, b_cum = sums_ref[2 * tm + 2], sums_ref[2 * tm + 3]
-    b_own = jnp.int32(0)
-    col = columns((block, width))
-    pad = jnp.zeros((halo, width), jnp.float32)
-    sums = [jnp.zeros((block + halo, width), jnp.float32) for _ in range(2)]
+    part = keep_ref.shape[1]
+    rows = block // 2 + part
+    pad = jnp.zeros((rows - block, width), jnp.float32)
+    col = columns((rows, width))
+    row = lax.broadcasted_iota(jnp.int32, (part, width), 0)
+    sums = [jnp.zeros((rows, width), jnp.float32) for _ in range(2)]
     winds = [jnp.float32(0.0), jnp.float32(0.0)]
     for k in reversed(range(frames)):
-        a, b = sh_ref[2 * k], sh_ref[2 * k + 1]
-        a_cum = a_cum - a
-        b_cum = b_cum - b
-        b_own = b_own + b
+        down, right = own_shifts(sh_ref, k, frames)
         for i, diff in enumerate(diffs(phases_ref, next_ref, k)):
             if k < frames - 1:
                 winds[i] = winds[i] + jnp.sum((loc_ref[k] - g_ref[k, :block]) * diff)
-            diff = jnp.where(col < width - b_own, decay_rate ** (frames - k) * diff, 0.0)
-            diff = jnp.concatenate([diff, pad], axis=0)
-            sums[i] = sums[i] + turned(diff, halo - a_cum, width - lax.rem(b_cum, width))
+            diff = jnp.concatenate([decay_rate ** (frames - k) * diff, pad], axis=0)
+            sums[i] = sums[i] + jnp.where(col >= right, turned(diff, down, right), 0.0)
+    y = lax.axis_index("tm") % 2
     for i in range(2):
-        keep, send = halves(sums[i], tm % 2)
-        keep_ref[i] = keep
-        pack(send_ref.at[i], send, exponent(send, width // 2))
+        low = jnp.where(row < block // 2, sums[i][:part], 0.0)
+        high = sums[i][block // 2 :]
+        keep_ref[i] = jnp.where(y == 0, low, high)
+        send = jnp.where(y == 0, high, low)
+        pack(send_ref.at[i], send, exponent(send, width))
         wind_ref[i] = winds[i]
 
 
 def combine_kernel(
-    frames, width, sums_ref, keep_ref, sent_ref, got_ref, late_ref, both_ref, send_ref
+    frames, sh_ref, keep_ref, sent_ref, got_ref, late_ref, both_ref, send_ref, info_ref
 ):
-    rows, part = keep_ref.shape
-    tm = lax.axis_index("tm")
-    pair, y = tm // 2, tm % 2
+    y = lax.axis_index("tm") % 2
     keep, got = keep_ref[...], unpack(got_ref)
     early = jnp.where(y == 0, keep, got)
     late = jnp.where(y == 0, got, keep)
     late_ref[...] = late
-    b_from, b_cum = sums_ref[4 * pair + 1], sums_ref[4 * pair + 3]
-    pos = columns((rows, part)) + y * part
-    both = early + dropped(decay_rate**frames * late, pos, width, b_cum, b_cum - b_from)
+    own = own_shifts(sh_ref, 0, frames)
+    other = shift_of(got_ref)
+    first = [jnp.where(y == 0, own[i], other[i]) for i in range(2)]
+    total = [own[i] + other[i] for i in range(2)]
+    for i in range(2):
+        info_ref[i] = total[i] - first[i]
+        info_ref[2 + i] = total[i]
+    both = early + decay_rate**frames * back(late, *first)
     both_ref[...] = both
-    pack(send_ref, both, jnp.maximum(sent_ref[rows:], got_ref[rows:]) + 1.0)
-
-
-def later_pairs(frames, width, reach, sums_ref, sent_ref, got_ref):
-    rows = got_ref.shape[0] - 8
-    part = got_ref.shape[1]
-    tm = lax.axis_index("tm")
-    pair, y = tm // 2, tm % 2
-    pos = columns((rows, part)) + y * part
-    pairs = lax.axis_size("tm") // 2
-    got = jnp.where(pair + reach < pairs, unpack(got_ref), 0.0)
-    b_cum = sums_ref[4 * jnp.minimum(pair + reach, pairs) + 1]
-    b_from, b_next = sums_ref[4 * pair + 1], sums_ref[4 * pair + 5]
-    power = jnp.where(pair + reach < pairs, jnp.maximum(sent_ref[rows:], got_ref[rows:]), sent_ref[rows:])
-    weight = decay_rate ** (2 * frames * reach)
-    weight_next = decay_rate ** (2 * frames * (reach - 1))
-    incl = dropped(weight * got, pos, width, b_cum, b_cum - b_from)
-    return incl, dropped(weight_next * got, pos, width, b_cum, b_cum - b_next), power
-
-
-def step_kernel(frames, width, reach, sums_ref, both_ref, sent_ref, got_ref, *refs):
-    incl, excl, power = later_pairs(frames, width, reach, sums_ref, sent_ref, got_ref)
+    pack(send_ref, both, jnp.maximum(power_of(sent_ref), power_of(got_ref)) + 1.0, *total)
+
+
+def from_pairs(reach, sent_ref, got_ref):
+    pair = lax.axis_index("tm") // 2
+    there = pair + reach < lax.axis_size("tm") // 2
+    power = power_of(sent_ref)
+    power = jnp.where(there, jnp.maximum(power, power_of(got_ref)), power)
+    return jnp.where(there, unpack(got_ref), 0.0), power
+
+
+def step_kernel(frames, reach, info_ref, both_ref, sent_ref, got_ref, *refs):
     incl_ref, excl_ref, send_ref = refs[-3:]
-    both = both_ref[...] + incl
+    got, power = from_pairs(reach, sent_ref, got_ref)
+    span, more = shift_of(sent_ref), shift_of(got_ref)
+    both = both_ref[...] + decay_rate ** (2 * frames * reach) * back(got, *span)
     incl_ref[...] = both
-    excl_ref[...] = excl + refs[0][...] if len(refs) == 4 else excl
-    pack(send_ref, both, power + 1.0)
+    if reach == 1:
+        excl_ref[...] = got
+    else:
+        apart = [span[i] - info_ref[2 + i] for i in range(2)]
+        excl_ref[...] = refs[0][...] + decay_rate ** (2 * frames * (reach - 1)) * back(got, *apart)
+    pack(send_ref, both, power + 1.0, span[0] + more[0], span[1] + more[1])
 
 
 def carry_kernel(
-    frames, width, reach, sums_ref, wind_in, late_ref, sent_ref, got_ref, z_ref, zgot_ref, *refs
+    frames, reach, info_ref, wind_in, late_ref, sent_ref, got_ref, z_ref, zgot_ref, *refs
 ):
     keep_ref, send_ref, wind_ref = refs[-3:]
-    rows, part = late_ref.shape
-    tm = lax.axis_index("tm")
-    pair, y = tm // 2, tm % 2
-    _, late, power = later_pairs(frames, width, reach, sums_ref, sent_ref, got_ref)
-    if len(refs) == 4:
-        late = late + refs[0][...]
-    b_from, b_cum = sums_ref[4 * pair + 3], sums_ref[4 * pair + 5]
-    pos = columns((rows, part)) + y * part
-    moved = dropped(decay_rate**frames * late, pos, width, b_cum, b_cum - b_from)
-    early = late_ref[...] + moved
+    y = lax.axis_index("tm") % 2
+    late, power = from_pairs(reach, sent_ref, got_ref)
+    if reach > 1:
+        span = shift_of(sent_ref)
+        apart = [span[i] - info_ref[2 + i] for i in range(2)]
+        late = refs[0][...] + decay_rate ** (2 * frames * (reach - 1)) * back(late, *apart)
+    early = late_ref[...] + decay_rate**frames * back(late, info_ref[0], info_ref[1])
     keep = jnp.where(y == 0, early, late)
     send = jnp.where(y == 0, late, early)
     keep_ref[...] = keep
@@ -324,26 +303,16 @@
     wind_ref[...] = jnp.where(lane == 0, sums[0], jnp.where(lane == 1, sums[1], 0.0))
 
 
-def final_kernel(sh_ref, sums_ref, keep_ref, got_ref, loc_ref, adj_ref):
-    frames, block, width = loc_ref.shape
-    rows = keep_ref.shape[0]
-    halo = rows - block
-    tm = lax.axis_index("tm")
+def final_kernel(sh_ref, keep_ref, got_ref, loc_ref, adj_ref):
+    frames, block, _ = loc_ref.shape
+    y = lax.axis_index("tm") % 2
     keep, got = keep_ref[...], unpack(got_ref)
-    low = jnp.where(tm % 2 == 0, keep, got)
-    high = jnp.where(tm % 2 == 0, got, keep)
-    canvas = jnp.concatenate([low, high], axis=1)
-    a_cum, b_cum = sums_ref[2 * tm + 2], sums_ref[2 * tm + 3]
-    col = columns((block, width))
-    b_own = jnp.int32(0)
+    low = jnp.where(y == 0, keep, got)
+    high = jnp.where(y == 0, got, keep)
+    field = jnp.concatenate([low[: block // 2], high], axis=0)
     for k in reversed(range(frames)):
-        a, b = sh_ref[2 * k], sh_ref[2 * k + 1]
-        a_cum = a_cum - a
-        b_cum = b_cum - b
-        b_own = b_own + b
-        moved = turned(canvas, rows - halo + a_cum, b_cum)[:block]
-        moved = jnp.where(col < width - b_own, decay_rate ** (frames - k) * moved, 0.0)
-        adj_ref[k] = loc_ref[k] + moved
+        moved = back(field, *own_shifts(sh_ref, k, frames))[:block]
+        adj_ref[k] = loc_ref[k] + decay_rate ** (frames - k) * moved
 
 
 def diffs(phases_ref, next_ref, k):
@@ -400,10 +369,10 @@
     n_tm = lax.axis_size("tm")
     frames_all = frames * n_tm
     focal = focal_data.shape[3]
-    halo = min(frames_all // 2, width // (4 * n_rows))
-    halo = -(-halo // 16) * 16
+    reach_rows = -(-min(frames_all // 2, width // (4 * n_rows)) // 8) * 8
+    halo = -(-reach_rows // 16) * 16
     rows = block + halo
-    part = width // 2
+    part = block // 2 + reach_rows
     pairs = n_tm // 2
     half = focal // 2
     cs = tables(width, focal)
@@ -413,12 +382,7 @@
     y_table = np.concatenate([cs[:half], cs[focal : focal + half]], axis=0).T
     flip = np.zeros((half, half), cs.dtype)
     flip[(half - np.arange(half)) % half, np.arange(half)] = 1
-    sh_all = shifts.reshape(2 * frames)
-    bit = 1
-    while bit < n_tm:
-        other = swap(sh_all, "tm", bit)
-        sh_all = jnp.concatenate([sh_all, other])
-        bit *= 2
+    own = shifts.reshape(2 * frames)
     vmem = pl.BlockSpec(memory_space=pltpu.VMEM)
     smem = pl.BlockSpec(memory_space=pltpu.SMEM)
     hbm = pl.BlockSpec(memory_space=pltpu.HBM)
@@ -463,49 +427,48 @@
         compiler_params=pltpu.CompilerParams(vmem_limit_bytes=24 << 20),
         name="grad",
     )(*m_parts, *d_parts, pupil_mask, *kept)
-    half_field = jax.ShapeDtypeStruct((rows, part), jnp.float32)
-    message = jax.ShapeDtypeStruct((rows + 8, part), jnp.float32)
-    loc, keep, send, sums_all = kernel_call(
-        segment_kernel, 12,
-        (field, half_field, message, jax.ShapeDtypeStruct((2 * n_tm + 2,), jnp.int32)),
-        [smem, vmem], (vmem, vmem, vmem, smem),
-    )(sh_all, grads)
-    late, both, send = kernel_call(
-        functools.partial(combine_kernel, frames, width), 6,
-        (half_field, half_field, message), [smem] + [vmem] * 3, (vmem, vmem, vmem),
-    )(sums_all, keep, send, swap_half(send))
+    half_field = jax.ShapeDtypeStruct((part, width), jnp.float32)
+    message = jax.ShapeDtypeStruct((part + 8, width), jnp.float32)
+    loc, keep, send = kernel_call(
+        segment_kernel, 12, (field, half_field, message), [smem, vmem], (vmem,) * 3
+    )(own, grads)
+    late, both, send, info = kernel_call(
+        functools.partial(combine_kernel, frames), 6,
+        (half_field, half_field, message, jax.ShapeDtypeStruct((4,), jnp.int32)),
+        [smem] + [vmem] * 3, (vmem, vmem, vmem, smem),
+    )(own, keep, send, swap_half(send))
     z_keep, z_send, wind_local = kernel_call(
-        functools.partial(z_kernel, halo), 12,
+        z_kernel, 12,
         (
-            jax.ShapeDtypeStruct((2, rows, part), jnp.float32),
-            jax.ShapeDtypeStruct((2, rows + 8, part), jnp.float32),
+            jax.ShapeDtypeStruct((2, part, width), jnp.float32),
+            jax.ShapeDtypeStruct((2, part + 8, width), jnp.float32),
             pair,
         ),
-        [smem, smem] + [vmem] * 4 + [pl.BlockSpec(memory_space=pl.ANY)], (vmem, vmem, smem),
-    )(sh_all, sums_all, phases, next_rows, grads, loc, late)
+        [smem] + [vmem] * 4 + [pl.BlockSpec(memory_space=pl.ANY)], (vmem, vmem, smem),
+    )(own, phases, next_rows, grads, loc, late)
     z_got = swap_half(z_send)
     sums = []
     reach = 1
     while 2 * reach < pairs:
         both, excl, send = kernel_call(
-            functools.partial(step_kernel, frames, width, reach), 6,
+            functools.partial(step_kernel, frames, reach), 6,
             (half_field, half_field, message),
             [smem] + [vmem] * (3 + len(sums)), (vmem, vmem, vmem),
-        )(sums_all, both, send, from_later(send, reach), *sums)
+        )(info, both, send, from_later(send, reach), *sums)
         sums = [excl]
         reach *= 2
     n_all = n_tm * n_rows
     keep, send, wind = kernel_call(
-        functools.partial(carry_kernel, frames, width, reach), 8,
+        functools.partial(carry_kernel, frames, reach), 8,
         (half_field, message, jax.ShapeDtypeStruct((n_all, 1, LANES), jnp.float32)),
         [smem, smem] + [vmem] * (5 + len(sums)), (vmem, vmem, vmem),
-    )(sums_all, wind_local, late, send, from_later(send, reach), z_keep, z_got, *sums)
+    )(info, wind_local, late, send, from_later(send, reach), z_keep, z_got, *sums)
     winds = lax.all_to_all(wind, ("tm", "rows"), 0, 0)
     got = swap_half(send)
     adjoint = kernel_call(
-        final_kernel, 8, field, [smem, smem, vmem, vmem, vmem], vmem,
+        final_kernel, 8, field, [smem, vmem, vmem, vmem], vmem,
         cost=12 * frames * block * width,
-    )(sh_all, sums_all, keep, got, loc)
+    )(own, keep, got, loc)
     wind_grad = -jnp.sum(winds[:, 0, :2], axis=0) / (width * frames_all)
     return adjoint, wind_grad
 

time: 56.2 us -> 52.2 us (0.929)
  starting transfers between devices: 23.6 us -> 15.7 us
  waiting for transfers between devices: 18.7 us -> 22.5 us
    ppermute x12 -> x9, starting transfers between devices: 16.8 us -> 9.11 us  [swap(): return lax.ppermute(value, axis, [(s, s ^ bit) for s in range(count)])]
    ppermute x12 -> x9, waiting for transfers between devices: 6.75 us -> 10.3 us  [swap(): return lax.ppermute(value, axis, [(s, s ^ bit) for s in range(count)])]
  transfers between devices with their start and end apart: 15 -> 12, of which waited for: 8 -> 7; matrix products, arithmetic and copies ran while one was open for 2% -> 1% of each run, Pallas kernels for 6% -> 7%
where the time goes in v6:
time: 52.2 us; the launch traced here: 52 us
  waiting for transfers between devices  22.5 us (43%)
  starting transfers between devices  15.7 us (30%)
  Pallas kernels  12.2 us (23%)
  between operations  0.81 us (2%)
  other arithmetic  0.72 us (1%)
    ppermute x9, waiting for transfers between devices, swap(): return lax.ppermute(value, axis, [(s, s ^ bit) for s in range(count)])  10.3 us
    ppermute x9, starting transfers between devices, swap(): return lax.ppermute(value, axis, [(s, s ^ bit) for s in range(count)])  9.11 us
    ppermute x2, waiting for transfers between devices, from_later(): lax.ppermute(value.astype(jnp.float16), 'tm', route).astype(jnp.float32)  6.98 us
    all_to_all x1, waiting for transfers between devices, on_device(): winds = lax.all_to_all(wind, ('tm', 'rows'), 0, 0)  5.25 us
    all_to_all x1, starting transfers between devices, on_device(): winds = lax.all_to_all(wind, ('tm', 'rows'), 0, 0)  4.04 us
    ppermute x2, starting transfers between devices, from_later(): lax.ppermute(value.astype(jnp.float16), 'tm', route).astype(jnp.float32)  2.58 us
    pallas_call x1, Pallas kernels, on_device(): kernel_call(z_kernel, 12, (jax.ShapeDtypeStruct((2, part, width), jnp.flo...  2.14 us
    pallas_call x1, Pallas kernels, on_device(): pl.pallas_call(functools.partial(y_kernel, halo), out_shape=[jax.ShapeDty...  1.74 us
  transfers between devices with their start and end apart: 12, of which 7 were waited for; matrix products, arithmetic and copies ran while one was open for 1% of the time, Pallas kernels for 7%

profile of v6, /device:TPU:0, one launch (start us, length us, event | category | flops | bytes accessed | tf_op | source)
XLA Modules:
  0.0 52.0 jit_solution(15682798371684162776)
XLA Ops:
  0.6 0.0 copy-start
  0.6 0.0 copy-start.2
  0.6 1.7 %transform.1 = (bf16[304,256]{1,0:T(8,128)(2,1)S(1)}, bf16[528,512]{1,0:T(8,128)(2,1)S(1)}, bf16[512,512]{1,0:T(8,128)(2,1)S(1)}, bf16[512,512]{1,0:T(8,128)(2,1)S(1)}, bf16[128,128]{1,0:T(8,128)(2,1)S(1)}) custom-call(bf16[2,128,512]{2,1,0:T(8,128)(2,1)} %phases_ref.1, s32[128,512]{1,0:T(8,128)} %refs_8_.1, bf16[512,256]{1,0:T(8,128)(2,1)} %constant.15.clone.half_hbm, ...), custom_call_target="tpu_custom_call" | custom-call | tf_op jit(solution)/shard_map/transform/pallas_call | solution.py:390
  2.4 0.0 copy-start.3
  2.4 3.0 %collective-permute-start.1 = (bf16[304,256]{1,0:T(8,128)(2,1)S(1)}, bf16[304,256]{1,0:T(8,128)(2,1)S(1)}, u32[]{:S(2)}, u32[]{:S(2)}) collective-permute-start(bf16[304,256]{1,0:T(8,128)(2,1)S(1)} %get-tuple-element.24.refs_0_), channel_id=1, source_target_pairs={{0,2},{1,3},{2,0},{3,1},{4,6},{5,7},{6,4},{7,5},{8,10},{9,11},{10,... | collective-permute-start | bytes 466952 | tf_op jit(solution)/shard_map/ppermute | solution.py:330
  5.4 0.0 copy-done.2
  5.4 0.1 collective-permute-start.4
  5.5 0.0 collective-permute-start
  5.5 4.8 %collective-permute-done.1.refs_2_ = bf16[304,256]{1,0:T(8,128)(2,1)S(1)} collective-permute-done((bf16[304,256]{1,0:T(8,128)(2,1)S(1)}, bf16[304,256]{1,0:T(8,128)(2,1)S(1)}, u32[]{:S(2)}, u32[]{:S(2)}) %collective-permute-start.1) | collective-permute-done | bytes 155680 | tf_op jit(solution)/shard_map/ppermute | solution.py:330
  10.3 0.0 collective-permute-start.2
  10.3 0.5 collective-permute-start.3
  10.8 1.4 %collective-permute-done.4.refs_6_ = bf16[2,2,64,256]{3,2,1,0:T(8,128)(2,1)S(1)} collective-permute-done((bf16[2,2,64,256]{3,2,1,0:T(8,128)(2,1)S(1)}, bf16[2,2,64,256]{3,2,1,0:T(8,128)(2,1)S(1)}, u32[]{:S(2)}, u32[]{:S(2)}) %collective-permute-start.4) | collective-permute-done | bytes 131104 | tf_op jit(solution)/shard_map/ppermute | solution.py:330
  12.3 0.0 collective-permute-start.5
  12.3 0.0 copy-done.3
  12.3 0.1 reshape.7.sh_ref
  12.4 0.0 collective-permute-done.3.refs_5_
  12.4 0.0 collective-permute-done.refs_1_
  12.4 1.3 %collective-permute-done.5.refs_7_ = bf16[2,2,64,256]{3,2,1,0:T(8,128)(2,1)S(1)} collective-permute-done((bf16[2,2,64,256]{3,2,1,0:T(8,128)(2,1)S(1)}, bf16[2,2,64,256]{3,2,1,0:T(8,128)(2,1)S(1)}, u32[]{:S(2)}, u32[]{:S(2)}) %collective-permute-start.5) | collective-permute-done | bytes 131104 | tf_op jit(solution)/shard_map/ppermute | solution.py:330
  13.6 0.0 collective-permute-done.2.refs_3_
  13.6 0.0 copy-done
  13.6 1.5 %grad.1 = (f32[2,144,512]{2,1,0:T(8,128)S(1)}, f32[8,512]{1,0:T(8,128)S(1)}) custom-call(bf16[304,256]{1,0:T(8,128)(2,1)S(1)} %get-tuple-element.24.refs_0_, bf16[304,256]{1,0:T(8,128)(2,1)S(1)} %collective-permute-done.refs_1_, bf16[304,256]{1,0:T(8,128)(2,1)S(1)} %collective-permute-done.1.refs_2_, bf16[304,256]{1,0:T(8,128)(2,1)S(1)} %collective-permute-done.2.refs_3_, ...), custom_call_target="tpu_custom_call" | custom-call | tf_op jit(solution)/shard_map/grad/pallas_call | solution.py:411
  15.1 0.9 %shard_map.104 = (f32[2,128,512]{2,1,0:T(8,128)S(1)}, f32[72,512]{1,0:T(8,128)S(1)}, f32[80,512]{1,0:T(8,128)S(1)}) custom-call(s32[4]{0:T(128)S(1)} %reshape.7.sh_ref, f32[2,144,512]{2,1,0:T(8,128)S(1)} %get-tuple-element.29.g_ref), custom_call_target="tpu_custom_call" | custom-call | tf_op jit(solution)/shard_map/pallas_call | solution.py:432
  16.1 1.8 %collective-permute-start.6 = (f16[80,512]{1,0:T(8,128)(2,1)S(1)}, f16[80,512]{1,0:T(8,128)(2,1)S(1)}, u32[]{:S(2)}, u32[]{:S(2)}) collective-permute-start(f16[80,512]{1,0:T(8,128)(2,1)S(1)} %convert_element_type.30), channel_id=1, source_target_pairs={{0,4},{4,0},{8,12},{12,8},{16,20},{20,16},{24,28},{28,24},{1,5},{5... | collective-permute-start | bytes 245768 | tf_op jit(solution)/shard_map/ppermute | solution.py:330
  17.9 2.8 %collective-permute-done.6 = f16[80,512]{1,0:T(8,128)(2,1)S(1)} collective-permute-done((f16[80,512]{1,0:T(8,128)(2,1)S(1)}, f16[80,512]{1,0:T(8,128)(2,1)S(1)}, u32[]{:S(2)}, u32[]{:S(2)}) %collective-permute-start.6) | collective-permute-done | bytes 81952 | tf_op jit(solution)/shard_map/ppermute | solution.py:330
  20.7 0.0 copy-start.1
  20.7 1.2 %shard_map.105 = (f32[72,512]{1,0:T(8,128)S(1)}, f32[72,512]{1,0:T(8,128)S(1)}, f32[80,512]{1,0:T(8,128)S(1)}, s32[4]{0:T(128)S(1)}) custom-call(s32[4]{0:T(128)S(1)} %reshape.7.sh_ref, f32[72,512]{1,0:T(8,128)S(1)} %get-tuple-element.30.keep_ref, f32[80,512]{1,0:T(8,128)S(1)} %get-tuple-element.31.sent_ref, f32[80,512]{1,0:T(8,128)S(1)} %convert_element_type.31.got_ref), custom_call_target="tpu_custom_call" | custom-call | tf_op jit(solution)/shard_map/pallas_call | solution.py:435
  21.9 1.3 %collective-permute-start.7 = (f16[80,512]{1,0:T(8,128)(2,1)S(1)}, f16[80,512]{1,0:T(8,128)(2,1)S(1)}, u32[]{:S(2)}, u32[]{:S(2)}) collective-permute-start(f16[80,512]{1,0:T(8,128)(2,1)S(1)} %convert_element_type.32), channel_id=1, source_target_pairs={{8,0},{12,4},{16,8},{20,12},{24,16},{28,20},{9,1},{13,5},{17,9},{2... | collective-permute-start | bytes 245768 | tf_op jit(solution)/shard_map/ppermute | solution.py:347
  23.2 0.0 copy-done.1
  23.2 2.1 %shard_map.106 = (f32[2,72,512]{2,1,0:T(8,128)S(1)}, f32[2,80,512]{2,1,0:T(8,128)S(1)}, f32[2]{0:T(128)S(1)}) custom-call(s32[4]{0:T(128)S(1)} %reshape.7.sh_ref, bf16[2,128,512]{2,1,0:T(8,128)(2,1)S(1)} %copy-done.1, f32[8,512]{1,0:T(8,128)S(1)} %get-tuple-element.33.next_ref, f32[2,144,512]{2,1,0:T(8,128)S(1)} %get-tuple-element.29.g_ref, ...), custom_call_target="tpu_custom_call" | custom-call | tf_op jit(solution)/shard_map/pallas_call | solution.py:440
  25.4 1.8 %collective-permute-start.9 = (f16[2,80,512]{2,1,0:T(8,128)(2,1)S(1)}, f16[2,80,512]{2,1,0:T(8,128)(2,1)S(1)}, u32[]{:S(2)}, u32[]{:S(2)}) collective-permute-start(f16[2,80,512]{2,1,0:T(8,128)(2,1)S(1)} %convert_element_type.36), channel_id=1, source_target_pairs={{0,4},{4,0},{8,12},{12,8},{16,20},{20,16},{24,28},{28,24},{1,5},{5... | collective-permute-start | bytes 491528 | tf_op jit(solution)/shard_map/ppermute | solution.py:330
  27.2 1.0 %collective-permute-done.7 = f16[80,512]{1,0:T(8,128)(2,1)S(1)} collective-permute-done((f16[80,512]{1,0:T(8,128)(2,1)S(1)}, f16[80,512]{1,0:T(8,128)(2,1)S(1)}, u32[]{:S(2)}, u32[]{:S(2)}) %collective-permute-start.7) | collective-permute-done | bytes 81952 | tf_op jit(solution)/shard_map/ppermute | solution.py:347
  28.3 1.4 %shard_map.107 = (f32[72,512]{1,0:T(8,128)}, f32[72,512]{1,0:T(8,128)S(1)}, f32[80,512]{1,0:T(8,128)S(1)}) custom-call(s32[4]{0:T(128)S(1)} %get-tuple-element.32.info_ref, f32[72,512]{1,0:T(8,128)S(1)} %get-tuple-element.37.both_ref, f32[80,512]{1,0:T(8,128)S(1)} %get-tuple-element.38.sent_ref, f32[80,512]{1,0:T(8,128)S(1)} %convert_element_type.33.got_ref), custom_call_target="tpu_custom_call" | custom-call | tf_op jit(solution)/shard_map/pallas_call | solution.py:453
  29.7 1.3 %collective-permute-start.8 = (f16[80,512]{1,0:T(8,128)(2,1)S(1)}, f16[80,512]{1,0:T(8,128)(2,1)S(1)}, u32[]{:S(2)}, u32[]{:S(2)}) collective-permute-start(f16[80,512]{1,0:T(8,128)(2,1)S(1)} %convert_element_type.34), channel_id=1, source_target_pairs={{16,0},{20,4},{24,8},{28,12},{17,1},{21,5},{25,9},{29,13},{18,2},{... | collective-permute-start | bytes 245768 | tf_op jit(solution)/shard_map/ppermute | solution.py:347
  31.0 5.9 %collective-permute-done.8 = f16[80,512]{1,0:T(8,128)(2,1)S(1)} collective-permute-done((f16[80,512]{1,0:T(8,128)(2,1)S(1)}, f16[80,512]{1,0:T(8,128)(2,1)S(1)}, u32[]{:S(2)}, u32[]{:S(2)}) %collective-permute-start.8) | collective-permute-done | bytes 81952 | tf_op jit(solution)/shard_map/ppermute | solution.py:347
  36.9 0.0 collective-permute-done.9
  37.0 1.7 %shard_map.108 = (f32[72,512]{1,0:T(8,128)S(1)}, f32[80,512]{1,0:T(8,128)S(1)}, f32[32,1,128]{2,1,0:T(1,128)}) custom-call(s32[4]{0:T(128)S(1)} %get-tuple-element.32.info_ref, f32[2]{0:T(128)S(1)} %get-tuple-element.36.wind_in, f32[72,512]{1,0:T(8,128)S(1)} %get-tuple-element.35.after_ref.late_ref, f32[80,512]{1,0:T(8,128)S(1)} %get-tuple-element.39.sent_ref, ...), custom_call_target="tpu_custom_call" | custom-call | tf_op jit(solution)/shard_map/pallas_call | solution.py:461
  38.6 4.0 %all-to-all-start = ((f32[32,1,128]{2,1,0:T(1,128)}), f32[32,1,128]{2,1,0:T(1,128)S(1)}, u32[]{:S(2)}, u32[]{:S(2)}) async-start(f32[32,1,128]{2,1,0:T(1,128)} %get-tuple-element.45), calls=%async_computation | async-start | bytes 32768 | tf_op jit(solution)/shard_map/all_to_all | solution.py:466
  42.7 1.8 %collective-permute-start.10 = (f16[80,512]{1,0:T(8,128)(2,1)S(1)}, f16[80,512]{1,0:T(8,128)(2,1)S(1)}, u32[]{:S(2)}, u32[]{:S(2)}) collective-permute-start(f16[80,512]{1,0:T(8,128)(2,1)S(1)} %convert_element_type.38), channel_id=1, source_target_pairs={{0,4},{4,0},{8,12},{12,8},{16,20},{20,16},{24,28},{28,24},{1,5},{5... | collective-permute-start | bytes 245768 | tf_op jit(solution)/shard_map/ppermute | solution.py:330
  44.5 5.2 %all-to-all-done = f32[32,1,128]{2,1,0:T(1,128)S(1)} async-done(((f32[32,1,128]{2,1,0:T(1,128)}), f32[32,1,128]{2,1,0:T(1,128)S(1)}, u32[]{:S(2)}, u32[]{:S(2)}) %all-to-all-start) | async-done | bytes 16416 | tf_op jit(solution)/shard_map/all_to_all | solution.py:466
  49.8 0.1 slice_reduce_fusion
  49.8 0.5 negate_multiply_fusion
  50.3 0.0 collective-permute-done.10
  50.4 1.6 %shard_map.109 = f32[2,128,512]{2,1,0:T(8,128)} custom-call(s32[4]{0:T(128)S(1)} %reshape.7.sh_ref, f32[72,512]{1,0:T(8,128)S(1)} %get-tuple-element.43.keep_ref, f32[80,512]{1,0:T(8,128)S(1)} %convert_element_type.39.got_ref, f32[2,128,512]{2,1,0:T(8,128)S(1)} %get-tuple-element.34.loc_ref), custom_call_target="tpu_custom_call" | custom-call | bytes 1572864 | tf_op jit(solution)/shard_map/pallas_call | solution.py:468
  (10 shorter events, 0.2 us)
Async XLA Ops:
  0.6 13.0 %copy-start = (s32[128,512]{1,0:T(8,128)S(1)}, s32[128,512]{1,0:T(8,128)}, u32[]{:S(2)}) copy-start(s32[128,512]{1,0:T(8,128)} %refs_8_.1) | copy-start | bytes 786436
  0.6 4.8 %copy-start.2 = (bf16[2,2,64,256]{3,2,1,0:T(8,128)(2,1)S(1)}, bf16[2,2,64,256]{3,2,1,0:T(8,128)(2,1)}, u32[]{:S(2)}) copy-start(bf16[2,2,64,256]{3,2,1,0:T(8,128)(2,1)} %refs_4_.1) | copy-start | bytes 393220
  2.4 9.9 %copy-start.3 = (s32[2,2]{1,0:T(2,128)S(1)}, s32[2,2]{1,0:T(2,128)}, u32[]{:S(2)}) copy-start(s32[2,2]{1,0:T(2,128)} %param.11) | copy-start | bytes 52
  2.4 7.9 %collective-permute-start.1 = (bf16[304,256]{1,0:T(8,128)(2,1)S(1)}, bf16[304,256]{1,0:T(8,128)(2,1)S(1)}, u32[]{:S(2)}, u32[]{:S(2)}) collective-permute-start(bf16[304,256]{1,0:T(8,128)(2,1)S(1)} %get-tuple-element.24.refs_0_), channel_id=1, source_target_pairs={{0,2},{1,3},{2,0},{3,1},{4,6},{5,7},{6,4},{7,5},{8,10},{9,11},{10,... | collective-permute-start | bytes 466952 | tf_op jit(solution)/shard_map/ppermute | solution.py:330
  5.4 6.8 %collective-permute-start.4 = (bf16[2,2,64,256]{3,2,1,0:T(8,128)(2,1)S(1)}, bf16[2,2,64,256]{3,2,1,0:T(8,128)(2,1)S(1)}, u32[]{:S(2)}, u32[]{:S(2)}) collective-permute-start(bf16[2,2,64,256]{3,2,1,0:T(8,128)(2,1)S(1)} %copy-done.2), channel_id=1, source_target_pairs={{0,2},{1,3},{2,0},{3,1},{4,6},{5,7},{6,4},{7,5},{8,10},{9,11},{10,... | collective-permute-start | bytes 393224 | tf_op jit(solution)/shard_map/ppermute | solution.py:330
  5.5 6.8 %collective-permute-start = (bf16[304,256]{1,0:T(8,128)(2,1)S(1)}, bf16[304,256]{1,0:T(8,128)(2,1)S(1)}, u32[]{:S(2)}, u32[]{:S(2)}) collective-permute-start(bf16[304,256]{1,0:T(8,128)(2,1)S(1)} %get-tuple-element.24.refs_0_), channel_id=1, source_target_pairs={{0,1},{1,0},{2,3},{3,2},{4,5},{5,4},{6,7},{7,6},{8,9},{9,8},{10,11... | collective-permute-start | bytes 466952 | tf_op jit(solution)/shard_map/ppermute | solution.py:330
  10.3 3.3 %collective-permute-start.2 = (bf16[304,256]{1,0:T(8,128)(2,1)S(1)}, bf16[304,256]{1,0:T(8,128)(2,1)S(1)}, u32[]{:S(2)}, u32[]{:S(2)}) collective-permute-start(bf16[304,256]{1,0:T(8,128)(2,1)S(1)} %collective-permute-done.1.refs_2_), channel_id=1, source_target_pairs={{0,1},{1,0},{2,3},{3,2},{4,5},{5,4},{6,7},{7,6},{8,9},{9,8},{10,11... | collective-permute-start | bytes 466952 | tf_op jit(solution)/shard_map/ppermute | solution.py:330
  10.3 2.0 %collective-permute-start.3 = (bf16[2,2,64,256]{3,2,1,0:T(8,128)(2,1)S(1)}, bf16[2,2,64,256]{3,2,1,0:T(8,128)(2,1)S(1)}, u32[]{:S(2)}, u32[]{:S(2)}) collective-permute-start(bf16[2,2,64,256]{3,2,1,0:T(8,128)(2,1)S(1)} %copy-done.2), channel_id=1, source_target_pairs={{0,1},{1,0},{2,3},{3,2},{4,5},{5,4},{6,7},{7,6},{8,9},{9,8},{10,11... | collective-permute-start | bytes 393224 | tf_op jit(solution)/shard_map/ppermute | solution.py:330
  12.3 1.3 %collective-permute-start.5 = (bf16[2,2,64,256]{3,2,1,0:T(8,128)(2,1)S(1)}, bf16[2,2,64,256]{3,2,1,0:T(8,128)(2,1)S(1)}, u32[]{:S(2)}, u32[]{:S(2)}) collective-permute-start(bf16[2,2,64,256]{3,2,1,0:T(8,128)(2,1)S(1)} %collective-permute-done.4.refs_6_), channel_id=1, source_target_pairs={{0,1},{1,0},{2,3},{3,2},{4,5},{5,4},{6,7},{7,6},{8,9},{9,8},{10,11... | collective-permute-start | bytes 393224 | tf_op jit(solution)/shard_map/ppermute | solution.py:330
  16.1 4.6 %collective-permute-start.6 = (f16[80,512]{1,0:T(8,128)(2,1)S(1)}, f16[80,512]{1,0:T(8,128)(2,1)S(1)}, u32[]{:S(2)}, u32[]{:S(2)}) collective-permute-start(f16[80,512]{1,0:T(8,128)(2,1)S(1)} %convert_element_type.30), channel_id=1, source_target_pairs={{0,4},{4,0},{8,12},{12,8},{16,20},{20,16},{24,28},{28,24},{1,5},{5... | collective-permute-start | bytes 245768 | tf_op jit(solution)/shard_map/ppermute | solution.py:330
  20.7 2.5 %copy-start.1 = (bf16[2,128,512]{2,1,0:T(8,128)(2,1)S(1)}, bf16[2,128,512]{2,1,0:T(8,128)(2,1)}, u32[]{:S(2)}) copy-start(bf16[2,128,512]{2,1,0:T(8,128)(2,1)} %phases_ref.1) | copy-start | bytes 786436
  21.9 6.3 %collective-permute-start.7 = (f16[80,512]{1,0:T(8,128)(2,1)S(1)}, f16[80,512]{1,0:T(8,128)(2,1)S(1)}, u32[]{:S(2)}, u32[]{:S(2)}) collective-permute-start(f16[80,512]{1,0:T(8,128)(2,1)S(1)} %convert_element_type.32), channel_id=1, source_target_pairs={{8,0},{12,4},{16,8},{20,12},{24,16},{28,20},{9,1},{13,5},{17,9},{2... | collective-permute-start | bytes 245768 | tf_op jit(solution)/shard_map/ppermute | solution.py:347
  25.4 11.5 %collective-permute-start.9 = (f16[2,80,512]{2,1,0:T(8,128)(2,1)S(1)}, f16[2,80,512]{2,1,0:T(8,128)(2,1)S(1)}, u32[]{:S(2)}, u32[]{:S(2)}) collective-permute-start(f16[2,80,512]{2,1,0:T(8,128)(2,1)S(1)} %convert_element_type.36), channel_id=1, source_target_pairs={{0,4},{4,0},{8,12},{12,8},{16,20},{20,16},{24,28},{28,24},{1,5},{5... | collective-permute-start | bytes 491528 | tf_op jit(solution)/shard_map/ppermute | solution.py:330
  29.7 7.2 %collective-permute-start.8 = (f16[80,512]{1,0:T(8,128)(2,1)S(1)}, f16[80,512]{1,0:T(8,128)(2,1)S(1)}, u32[]{:S(2)}, u32[]{:S(2)}) collective-permute-start(f16[80,512]{1,0:T(8,128)(2,1)S(1)} %convert_element_type.34), channel_id=1, source_target_pairs={{16,0},{20,4},{24,8},{28,12},{17,1},{21,5},{25,9},{29,13},{18,2},{... | collective-permute-start | bytes 245768 | tf_op jit(solution)/shard_map/ppermute | solution.py:347
  38.6 11.2 %all-to-all-start = ((f32[32,1,128]{2,1,0:T(1,128)}), f32[32,1,128]{2,1,0:T(1,128)S(1)}, u32[]{:S(2)}, u32[]{:S(2)}) async-start(f32[32,1,128]{2,1,0:T(1,128)} %get-tuple-element.45), calls=%async_computation | async-start | bytes 32768 | tf_op jit(solution)/shard_map/all_to_all | solution.py:466
  42.7 7.7 %collective-permute-start.10 = (f16[80,512]{1,0:T(8,128)(2,1)S(1)}, f16[80,512]{1,0:T(8,128)(2,1)S(1)}, u32[]{:S(2)}, u32[]{:S(2)}) collective-permute-start(f16[80,512]{1,0:T(8,128)(2,1)S(1)} %convert_element_type.38), channel_id=1, source_target_pairs={{0,4},{4,0},{8,12},{12,8},{16,20},{20,16},{24,28},{28,24},{1,5},{5... | collective-permute-start | bytes 245768 | tf_op jit(solution)/shard_map/ppermute | solution.py:330

commit v7 on v6

--- a/solution.py
+++ b/solution.py
@@ -38,8 +38,8 @@
 
 
 def y_kernel(halo, phases_hbm, mask_hbm, half_hbm, *refs):
-    count = (len(refs) - 5) // 2
-    y_ref = refs[count]
+    count = (len(refs) - 6) // 2
+    y_ref, side_ref = refs[count], refs[-5]
     phases_ref, mask_ref, half_ref, sem = refs[-4:]
     ins = [(phases_hbm, phases_ref), (mask_hbm, mask_ref), (half_hbm, half_ref)]
     copies = [(refs[i], refs[count + 1 + i]) for i in range(count)]
@@ -74,8 +74,17 @@
     mask = mask_ref[:halo].astype(jnp.float32).astype(jnp.bfloat16)
     for i in range(parts):
         y_ref[at + i * halo : at + (i + 1) * halo] = mask[:, i * focal : (i + 1) * focal]
+    side_ref[...] = half_phases(phases_ref, 1 - lax.axis_index("tm") % 2)
     for copy in copies[3:]:
         copy.wait()
+
+
+def half_phases(phases_ref, y):
+    block = phases_ref.shape[1]
+    part = block // 2 + 8
+    low = phases_ref[:, :part].astype(jnp.float32)
+    high = phases_ref[:, block - part :].astype(jnp.float32)
+    return jnp.where(y == 0, low, high).astype(jnp.bfloat16)
 
 
 def zero_freq_value(width):
@@ -177,12 +186,15 @@
     return jnp.ceil(jnp.log2(top))[:1]
 
 
-def pack(ref, value, power, down=0, right=0):
+def pack(ref, value, power, down=0, right=0, more=()):
     rows = value.shape[0]
     ref[:rows] = value * jnp.exp2(-power)
     line = lax.broadcasted_iota(jnp.int32, (8, value.shape[1]), 0)
     shift = jnp.where(line == 1, down, right).astype(jnp.float32)
-    ref[rows:] = jnp.where(line == 0, power, shift)
+    tail = jnp.where(line == 0, power, shift)
+    for i, extra in enumerate(more):
+        tail = jnp.where(line == 3 + i, extra, tail)
+    ref[rows:] = tail
 
 
 def power_of(ref):
@@ -199,7 +211,7 @@
     return ref[: ref.shape[0] - 8] * jnp.exp2(power_of(ref))
 
 
-def segment_kernel(sh_ref, g_ref, loc_ref, keep_ref, send_ref):
+def segment_kernel(sh_ref, g_ref, next_ref, loc_ref, keep_ref, send_keep_ref, send_ref):
     frames, block, _ = loc_ref.shape
     lam = g_ref[frames - 1]
     loc_ref[frames - 1] = lam[:block]
@@ -208,41 +220,83 @@
         loc_ref[k] = lam[:block]
     keep, send = halves(lam, keep_ref.shape[0], block // 2, lax.axis_index("tm") % 2)
     keep_ref[...] = keep
-    pack(send_ref, send, exponent(lam, lam.shape[1]), *own_shifts(sh_ref, 0, frames))
+    power = exponent(lam, lam.shape[1])
+    shift = own_shifts(sh_ref, 0, frames)
+    pack(send_keep_ref, keep, power, *shift)
+    each = jnp.zeros((1, lam.shape[1]), jnp.float32)
+    lane = columns(each.shape)
+    for i in range(2 * frames):
+        each = jnp.where(lane == i, sh_ref[i].astype(jnp.float32), each)
+    more = [next_ref[k : k + 1] for k in range(frames)] + [each]
+    pack(send_ref, send, power, *shift, more)
+
+
+def half_diffs(here, last):
+    rows, width = here.shape
+    row = lax.broadcasted_iota(jnp.int32, here.shape, 0)
+    below = jnp.where(row == rows - 1, last, pltpu.roll(here, rows - 1, 0))
+    right = jnp.where(columns(here.shape) == width - 1, 0.0, pltpu.roll(here, width - 1, 1))
+    return below - here, right - here
+
+
+def half_products(side, lasts, shifts, y, rows):
+    frames, part, width = side.shape
+    half = part - 8
+    line = lax.broadcasted_iota(jnp.int32, (part, width), 0)
+    col = columns((part, width))
+    sums = [jnp.zeros((part, width), jnp.float32) for _ in range(2)]
+    down, right = jnp.int32(0), jnp.int32(0)
+    for k in reversed(range(frames)):
+        down, right = down + shifts[k][0], right + shifts[k][1]
+        low = jnp.where(y == 0, down, 0)
+        high = jnp.where(y == 0, half, half + down)
+        inside = (line >= low) & (line < high) & (col >= right)
+        for i, diff in enumerate(half_diffs(side[k].astype(jnp.float32), lasts[k])):
+            moved = turned(diff, jnp.where(y == 0, down, half + down), right)
+            sums[i] = sums[i] + jnp.where(inside, decay_rate ** (frames - k) * moved, 0.0)
+    if rows > part:
+        pad = jnp.zeros((rows - part, width), jnp.float32)
+        sums = [jnp.concatenate([v, pad], axis=0) for v in sums]
+    return sums
 
 
 def z_kernel(
-    sh_ref, phases_ref, next_ref, g_ref, loc_ref, after_ref, keep_ref, send_ref, wind_ref
+    sh_ref, phases_ref, side_ref, next_ref, got_ref, g_ref, loc_ref, own_ref, other_ref, wind_ref
 ):
-    frames, block, width = phases_ref.shape
-    part = keep_ref.shape[1]
-    rows = block // 2 + part
-    pad = jnp.zeros((rows - block, width), jnp.float32)
-    col = columns((rows, width))
-    row = lax.broadcasted_iota(jnp.int32, (part, width), 0)
-    sums = [jnp.zeros((rows, width), jnp.float32) for _ in range(2)]
+    frames, block, _ = phases_ref.shape
+    rows = own_ref.shape[1]
+    y = lax.axis_index("tm") % 2
+    shifts = [(sh_ref[2 * k], sh_ref[2 * k + 1]) for k in range(frames)]
+    lasts = [next_ref[k : k + 1] for k in range(frames)]
+    own = half_products(half_phases(phases_ref, y), lasts, shifts, y, rows)
+    at = got_ref.shape[0] - 8
+    spot = at + 3 + frames
+    shifts = [
+        tuple(got_ref[spot, 2 * k + i].astype(jnp.int32) for i in range(2)) for k in range(frames)
+    ]
+    lasts = [got_ref[at + 3 + k : at + 4 + k] for k in range(frames)]
+    other = half_products(side_ref[...], lasts, shifts, y, rows)
     winds = [jnp.float32(0.0), jnp.float32(0.0)]
-    for k in reversed(range(frames)):
-        down, right = own_shifts(sh_ref, k, frames)
-        for i, diff in enumerate(diffs(phases_ref, next_ref, k)):
-            if k < frames - 1:
-                winds[i] = winds[i] + jnp.sum((loc_ref[k] - g_ref[k, :block]) * diff)
-            diff = jnp.concatenate([decay_rate ** (frames - k) * diff, pad], axis=0)
-            sums[i] = sums[i] + jnp.where(col >= right, turned(diff, down, right), 0.0)
-    y = lax.axis_index("tm") % 2
+    for k in range(frames - 1):
+        prior = loc_ref[k] - g_ref[k, :block]
+        for i, diff in enumerate(
+            half_diffs(phases_ref[k].astype(jnp.float32), next_ref[k : k + 1])
+        ):
+            winds[i] = winds[i] + jnp.sum(prior * diff)
     for i in range(2):
-        low = jnp.where(row < block // 2, sums[i][:part], 0.0)
-        high = sums[i][block // 2 :]
-        keep_ref[i] = jnp.where(y == 0, low, high)
-        send = jnp.where(y == 0, high, low)
-        pack(send_ref.at[i], send, exponent(send, width))
+        own_ref[i] = own[i]
+        other_ref[i] = other[i]
         wind_ref[i] = winds[i]
 
 
 def combine_kernel(
-    frames, sh_ref, keep_ref, sent_ref, got_ref, late_ref, both_ref, send_ref, info_ref
+    frames, sh_ref, keep_ref, sent_ref, got_ref, near_ref, far_ref,
+    late_ref, incl_ref, excl_ref, send_ref, info_ref,
 ):
-    y = lax.axis_index("tm") % 2
+    tm = lax.axis_index("tm")
+    y = tm % 2
+    there = tm // 2 + 1 < lax.axis_size("tm") // 2
+    weight = decay_rate**frames
     keep, got = keep_ref[...], unpack(got_ref)
     early = jnp.where(y == 0, keep, got)
     late = jnp.where(y == 0, got, keep)
@@ -251,12 +305,23 @@
     other = shift_of(got_ref)
     first = [jnp.where(y == 0, own[i], other[i]) for i in range(2)]
     total = [own[i] + other[i] for i in range(2)]
+    near, far = unpack(near_ref), unpack(far_ref)
+    near_shift, far_shift = shift_of(near_ref), shift_of(far_ref)
+    next_first = [jnp.where(y == 0, near_shift[i], far_shift[i]) for i in range(2)]
+    next_late = jnp.where(y == 0, far, near)
+    following = jnp.where(y == 0, near, far) + weight * back(next_late, *next_first)
+    following = jnp.where(there, following, 0.0)
+    excl_ref[...] = following
+    both = early + weight * back(late, *first) + weight * weight * back(following, *total)
+    incl_ref[...] = both
     for i in range(2):
         info_ref[i] = total[i] - first[i]
         info_ref[2 + i] = total[i]
-    both = early + decay_rate**frames * back(late, *first)
-    both_ref[...] = both
-    pack(send_ref, both, jnp.maximum(power_of(sent_ref), power_of(got_ref)) + 1.0, *total)
+    power = jnp.maximum(power_of(sent_ref), power_of(got_ref))
+    further = jnp.maximum(power_of(near_ref), power_of(far_ref))
+    power = jnp.where(there, jnp.maximum(power, further), power)
+    span = [total[i] + near_shift[i] + far_shift[i] for i in range(2)]
+    pack(send_ref, both, power + 2.0, *span)
 
 
 def from_pairs(reach, sent_ref, got_ref):
@@ -267,37 +332,33 @@
     return jnp.where(there, unpack(got_ref), 0.0), power
 
 
-def step_kernel(frames, reach, info_ref, both_ref, sent_ref, got_ref, *refs):
-    incl_ref, excl_ref, send_ref = refs[-3:]
+def step_kernel(frames, reach, info_ref, both_ref, excl_in, sent_ref, got_ref, *refs):
+    incl_ref, excl_ref, send_ref = refs
     got, power = from_pairs(reach, sent_ref, got_ref)
     span, more = shift_of(sent_ref), shift_of(got_ref)
     both = both_ref[...] + decay_rate ** (2 * frames * reach) * back(got, *span)
     incl_ref[...] = both
-    if reach == 1:
-        excl_ref[...] = got
-    else:
-        apart = [span[i] - info_ref[2 + i] for i in range(2)]
-        excl_ref[...] = refs[0][...] + decay_rate ** (2 * frames * (reach - 1)) * back(got, *apart)
+    apart = [span[i] - info_ref[2 + i] for i in range(2)]
+    excl_ref[...] = excl_in[...] + decay_rate ** (2 * frames * (reach - 1)) * back(got, *apart)
     pack(send_ref, both, power + 1.0, span[0] + more[0], span[1] + more[1])
 
 
 def carry_kernel(
-    frames, reach, info_ref, wind_in, late_ref, sent_ref, got_ref, z_ref, zgot_ref, *refs
+    frames, reach, info_ref, wind_in, late_ref, excl_ref, sent_ref, got_ref, own_ref, other_ref,
+    keep_ref, send_ref, wind_ref,
 ):
-    keep_ref, send_ref, wind_ref = refs[-3:]
     y = lax.axis_index("tm") % 2
-    late, power = from_pairs(reach, sent_ref, got_ref)
-    if reach > 1:
-        span = shift_of(sent_ref)
-        apart = [span[i] - info_ref[2 + i] for i in range(2)]
-        late = refs[0][...] + decay_rate ** (2 * frames * (reach - 1)) * back(late, *apart)
+    got, power = from_pairs(reach, sent_ref, got_ref)
+    span = shift_of(sent_ref)
+    apart = [span[i] - info_ref[2 + i] for i in range(2)]
+    late = excl_ref[...] + decay_rate ** (2 * frames * (reach - 1)) * back(got, *apart)
     early = late_ref[...] + decay_rate**frames * back(late, info_ref[0], info_ref[1])
     keep = jnp.where(y == 0, early, late)
     send = jnp.where(y == 0, late, early)
     keep_ref[...] = keep
     pack(send_ref, send, power + 2.0)
     sums = [
-        wind_in[i] + jnp.sum(keep * z_ref[i] + send * unpack(zgot_ref.at[i])) for i in range(2)
+        wind_in[i] + jnp.sum(keep * own_ref[i] + send * other_ref[i]) for i in range(2)
     ]
     lane = lax.broadcasted_iota(jnp.int32, wind_ref.shape, 2)
     wind_ref[...] = jnp.where(lane == 0, sums[0], jnp.where(lane == 1, sums[1], 0.0))
@@ -315,16 +376,6 @@
         adj_ref[k] = loc_ref[k] + decay_rate ** (frames - k) * moved
 
 
-def diffs(phases_ref, next_ref, k):
-    _, block, width = phases_ref.shape
-    here = phases_ref[k].astype(jnp.float32)
-    last = next_ref[k : k + 1]
-    row = lax.broadcasted_iota(jnp.int32, (block, width), 0)
-    below = jnp.where(row == block - 1, last, pltpu.roll(here, block - 1, 0))
-    right = jnp.where(columns((block, width)) == width - 1, 0.0, pltpu.roll(here, width - 1, 1))
-    return below - here, right - here
-
-
 def swap(value, axis, bit):
     count = lax.axis_size(axis)
     return lax.ppermute(value, axis, [(s, s ^ bit) for s in range(count)])
@@ -341,14 +392,10 @@
     return [held[d] for d in range(count)]
 
 
-def from_later(value, pairs_away):
+def permute_16(value, target):
     count = lax.axis_size("tm")
-    route = [(s, s - 2 * pairs_away) for s in range(2 * pairs_away, count)]
+    route = [(s, target(s)) for s in range(count) if 0 <= target(s) < count]
     return lax.ppermute(value.astype(jnp.float16), "tm", route).astype(jnp.float32)
-
-
-def swap_half(value):
-    return swap(value.astype(jnp.float16), "tm", 1).astype(jnp.float32)
 
 
 def kernel_call(body, vmem_mib, out_shape, in_specs, out_specs, cost=0):
@@ -387,14 +434,16 @@
     smem = pl.BlockSpec(memory_space=pltpu.SMEM)
     hbm = pl.BlockSpec(memory_space=pltpu.HBM)
     kept = [tt, cs, cs_turned, flip]
-    y, *kept = pl.pallas_call(
+    side_shape = (frames, block // 2 + 8, width)
+    y, *kept, side = pl.pallas_call(
         functools.partial(y_kernel, halo),
         out_shape=[
             jax.ShapeDtypeStruct((frames * block + 16 + halo * width // focal, focal), jnp.bfloat16)
         ]
-        + [jax.ShapeDtypeStruct(t.shape, jnp.bfloat16) for t in kept],
+        + [jax.ShapeDtypeStruct(t.shape, jnp.bfloat16) for t in kept]
+        + [jax.ShapeDtypeStruct(side_shape, jnp.bfloat16)],
         in_specs=[hbm] * (3 + len(kept)),
-        out_specs=[vmem] * (1 + len(kept)),
+        out_specs=[vmem] * (2 + len(kept)),
         scratch_shapes=[
             pltpu.VMEM(phases.shape, phases.dtype),
             pltpu.VMEM(pupil_mask.shape, pupil_mask.dtype),
@@ -406,6 +455,7 @@
     )(*[pltpu.with_memory_space_constraint(t, pltpu.HBM) for t in (phases, pupil_mask, y_table, *kept)])
     d_parts = gather_rows(focal_data)
     m_parts = gather_rows(y)
+    side = swap(side, "tm", 1)
     field = jax.ShapeDtypeStruct((frames, block, width), jnp.float32)
     pair = jax.ShapeDtypeStruct((2,), jnp.float32)
     grads, next_rows = pl.pallas_call(
@@ -429,42 +479,40 @@
     )(*m_parts, *d_parts, pupil_mask, *kept)
     half_field = jax.ShapeDtypeStruct((part, width), jnp.float32)
     message = jax.ShapeDtypeStruct((part + 8, width), jnp.float32)
-    loc, keep, send = kernel_call(
-        segment_kernel, 12, (field, half_field, message), [smem, vmem], (vmem,) * 3
-    )(own, grads)
-    late, both, send, info = kernel_call(
+    loc, keep, send_keep, send = kernel_call(
+        segment_kernel, 12,
+        (field, half_field, message, message), [smem, vmem, vmem], (vmem,) * 4,
+    )(own, grads, next_rows)
+    near = permute_16(send_keep, lambda s: s - 2)
+    far = permute_16(send, lambda s: (s - 2) ^ 1)
+    got = permute_16(send, lambda s: s ^ 1)
+    late, both, excl, send, info = kernel_call(
         functools.partial(combine_kernel, frames), 6,
-        (half_field, half_field, message, jax.ShapeDtypeStruct((4,), jnp.int32)),
-        [smem] + [vmem] * 3, (vmem, vmem, vmem, smem),
-    )(own, keep, send, swap_half(send))
-    z_keep, z_send, wind_local = kernel_call(
-        z_kernel, 12,
-        (
-            jax.ShapeDtypeStruct((2, part, width), jnp.float32),
-            jax.ShapeDtypeStruct((2, part + 8, width), jnp.float32),
-            pair,
-        ),
-        [smem] + [vmem] * 4 + [pl.BlockSpec(memory_space=pl.ANY)], (vmem, vmem, smem),
-    )(own, phases, next_rows, grads, loc, late)
-    z_got = swap_half(z_send)
-    sums = []
-    reach = 1
+        (half_field, half_field, half_field, message, jax.ShapeDtypeStruct((4,), jnp.int32)),
+        [smem] + [vmem] * 5, (vmem, vmem, vmem, vmem, smem),
+    )(own, keep, send, got, near, far)
+    products = jax.ShapeDtypeStruct((2, part, width), jnp.float32)
+    own_z, other_z, wind_local = kernel_call(
+        z_kernel, 12, (products, products, pair), [smem] + [vmem] * 6,
+        (vmem, vmem, smem),
+    )(own, phases, side, next_rows, got, grads, loc)
+    reach = 2
     while 2 * reach < pairs:
+        got = permute_16(send, lambda s, r=reach: s - 2 * r)
         both, excl, send = kernel_call(
             functools.partial(step_kernel, frames, reach), 6,
-            (half_field, half_field, message),
-            [smem] + [vmem] * (3 + len(sums)), (vmem, vmem, vmem),
-        )(info, both, send, from_later(send, reach), *sums)
-        sums = [excl]
+            (half_field, half_field, message), [smem] + [vmem] * 4, (vmem, vmem, vmem),
+        )(info, both, excl, send, got)
         reach *= 2
+    got = permute_16(send, lambda s: s - 2 * reach)
     n_all = n_tm * n_rows
     keep, send, wind = kernel_call(
         functools.partial(carry_kernel, frames, reach), 8,
         (half_field, message, jax.ShapeDtypeStruct((n_all, 1, LANES), jnp.float32)),
-        [smem, smem] + [vmem] * (5 + len(sums)), (vmem, vmem, vmem),
-    )(info, wind_local, late, send, from_later(send, reach), z_keep, z_got, *sums)
+        [smem, smem] + [vmem] * 6, (vmem, vmem, vmem),
+    )(info, wind_local, late, excl, send, got, own_z, other_z)
     winds = lax.all_to_all(wind, ("tm", "rows"), 0, 0)
-    got = swap_half(send)
+    got = permute_16(send, lambda s: s ^ 1)
     adjoint = kernel_call(
         final_kernel, 8, field, [smem, vmem, vmem, vmem], vmem,
         cost=12 * frames * block * width,

time: 52.2 us -> 50.6 us (0.969)
  Pallas kernels: 12.2 us -> 11.3 us
  starting transfers between devices: 15.7 us -> 14.9 us
    ppermute x9 -> x7, starting transfers between devices: 9.11 us -> 3.96 us  [swap(): return lax.ppermute(value, axis, [(s, s ^ bit) for s in range(count)])]
    ppermute x2 -> x5, starting transfers between devices: 2.58 us -> 7.54 us  [permute_16(): lax.ppermute(value.astype(jnp.float16), 'tm', route).astype(jnp.float32)]
    ppermute x2 -> x5, waiting for transfers between devices: 6.98 us -> 9.79 us  [permute_16(): lax.ppermute(value.astype(jnp.float16), 'tm', route).astype(jnp.float32)]
    ppermute x9 -> x7, waiting for transfers between devices: 10.3 us -> 7.49 us  [swap(): return lax.ppermute(value, axis, [(s, s ^ bit) for s in range(count)])]
    pallas_call x3 -> x2, Pallas kernels: 4.44 us -> 3.15 us  [the longest x1 2.23 us: on_device(): kernel_call(z_kernel, 12, (products, products, pair), [smem] + [vmem] * 6...]
    all_to_all x1, starting transfers between devices: 4.04 us -> 3.41 us  [on_device(): winds = lax.all_to_all(wind, ('tm', 'rows'), 0, 0)]
  transfers between devices with their start and end apart: 12 -> 13, of which waited for: 7 -> 7; matrix products, arithmetic and copies ran while one was open for 1% -> 1% of each run, Pallas kernels for 7% -> 8%
where the time goes in v7:
time: 50.6 us; the launch traced here: 50.3 us
  waiting for transfers between devices  22.5 us (44%)
  starting transfers between devices  14.9 us (29%)
  Pallas kernels  11.3 us (22%)
  between operations  0.81 us (2%)
  other arithmetic  0.68 us (1%)
    ppermute x5, waiting for transfers between devices, permute_16(): lax.ppermute(value.astype(jnp.float16), 'tm', route).astype(jnp.float32)  9.79 us
    ppermute x5, starting transfers between devices, permute_16(): lax.ppermute(value.astype(jnp.float16), 'tm', route).astype(jnp.float32)  7.54 us
    ppermute x7, waiting for transfers between devices, swap(): return lax.ppermute(value, axis, [(s, s ^ bit) for s in range(count)])  7.49 us
    all_to_all x1, waiting for transfers between devices, on_device(): winds = lax.all_to_all(wind, ('tm', 'rows'), 0, 0)  5.25 us
    ppermute x7, starting transfers between devices, swap(): return lax.ppermute(value, axis, [(s, s ^ bit) for s in range(count)])  3.96 us
    all_to_all x1, starting transfers between devices, on_device(): winds = lax.all_to_all(wind, ('tm', 'rows'), 0, 0)  3.41 us
    pallas_call x1, Pallas kernels, on_device(): kernel_call(z_kernel, 12, (products, products, pair), [smem] + [vmem] * 6...  2.23 us
    pallas_call x1, Pallas kernels, on_device(): pl.pallas_call(functools.partial(y_kernel, halo), out_shape=[jax.ShapeDty...  1.74 us
  transfers between devices with their start and end apart: 13, of which 7 were waited for; matrix products, arithmetic and copies ran while one was open for 1% of the time, Pallas kernels for 8%

profile of v7, /device:TPU:0, one launch (start us, length us, event | category | flops | bytes accessed | tf_op | source)
XLA Modules:
  0.0 50.3 jit_solution(17181810097536106932)
XLA Ops:
  0.6 0.0 copy-start
  0.6 0.0 copy-start.2
  0.6 1.7 %transform.1 = (bf16[304,256]{1,0:T(8,128)(2,1)S(1)}, bf16[528,512]{1,0:T(8,128)(2,1)S(1)}, bf16[512,512]{1,0:T(8,128)(2,1)S(1)}, bf16[512,512]{1,0:T(8,128)(2,1...) custom-call(bf16[2,128,512]{2,1,0:T(8,128)(2,1)} %phases_ref.1, s32[128,512]{1,0:T(8,128)} %refs_8_.1, ...), custom_call_target="tpu_custom_call" | custom-call | tf_op jit(solution)/shard_map/transform/pallas_call | solution.py:438
  2.4 0.0 copy-start.3
  2.4 3.0 %collective-permute-start.1 = (bf16[304,256]{1,0:T(8,128)(2,1)S(1)}, bf16[304,256]{1,0:T(8,128)(2,1)S(1)}, u32[]{:S(2)}, u32[]{:S(2)}) collective-permute-start(bf16[304,256]{1,0:T(8,128)(2,1)S(1)} %get-tuple-element.24.refs_0_), channel_id=1, source_target_pairs={{0,2},{1,3},{2,0},{3,1},{4,6},{5,7},{6,4},{7,5},{8,10},{9,11},{10,... | collective-permute-start | bytes 466952 | tf_op jit(solution)/shard_map/ppermute | solution.py:381
  5.4 0.0 copy-done.2
  5.4 0.1 collective-permute-start.4
  5.5 0.0 collective-permute-start
  5.5 4.8 %collective-permute-done.1.refs_2_ = bf16[304,256]{1,0:T(8,128)(2,1)S(1)} collective-permute-done((bf16[304,256]{1,0:T(8,128)(2,1)S(1)}, bf16[304,256]{1,0:T(8,128)(2,1)S(1)}, u32[]{:S(2)}, u32[]{:S(2)}) %collective-permute-start.1) | collective-permute-done | bytes 155680 | tf_op jit(solution)/shard_map/ppermute | solution.py:381
  10.3 0.0 collective-permute-start.2
  10.3 0.5 %collective-permute-start.3 = (bf16[2,2,64,256]{3,2,1,0:T(8,128)(2,1)S(1)}, bf16[2,2,64,256]{3,2,1,0:T(8,128)(2,1)S(1)}, u32[]{:S(2)}, u32[]{:S(2)}) collective-permute-start(bf16[2,2,64,256]{3,2,1,0:T(8,128)(2,1)S(1)} %copy-done.2), channel_id=1, source_target_pairs={{0,1},{1,0},{2,3},{3,2},{4,5},{5,4},{6,7},{7,6},{8,9},{9,8},{10,11... | collective-permute-start | bytes 393224 | tf_op jit(solution)/shard_map/ppermute | solution.py:381
  10.8 1.4 %collective-permute-done.4.refs_6_ = bf16[2,2,64,256]{3,2,1,0:T(8,128)(2,1)S(1)} collective-permute-done((bf16[2,2,64,256]{3,2,1,0:T(8,128)(2,1)S(1)}, bf16[2,2,64,256]{3,2,1,0:T(8,128)(2,1)S(1)}, u32[]{:S(2)}, u32[]{:S(2)}) %collective-permute-start.4) | collective-permute-done | bytes 131104 | tf_op jit(solution)/shard_map/ppermute | solution.py:381
  12.3 0.0 collective-permute-start.5
  12.3 0.0 copy-done.3
  12.3 0.1 reshape.7.sh_ref
  12.4 0.0 collective-permute-done.3.refs_5_
  12.4 0.0 collective-permute-done.refs_1_
  12.4 1.3 %collective-permute-done.5.refs_7_ = bf16[2,2,64,256]{3,2,1,0:T(8,128)(2,1)S(1)} collective-permute-done((bf16[2,2,64,256]{3,2,1,0:T(8,128)(2,1)S(1)}, bf16[2,2,64,256]{3,2,1,0:T(8,128)(2,1)S(1)}, u32[]{:S(2)}, u32[]{:S(2)}) %collective-permute-start.5) | collective-permute-done | bytes 131104 | tf_op jit(solution)/shard_map/ppermute | solution.py:381
  13.6 0.0 collective-permute-done.2.refs_3_
  13.6 0.0 copy-done
  13.6 1.5 %grad.1 = (f32[2,144,512]{2,1,0:T(8,128)S(1)}, f32[8,512]{1,0:T(8,128)S(1)}) custom-call(bf16[304,256]{1,0:T(8,128)(2,1)S(1)} %get-tuple-element.24.refs_0_, bf16[304,256]{1,0:T(8,128)(2,1)S(1)} %collective-permute-done.refs_1_, bf16[304,256]{1,0:T(8,128)(2,1)S(1)} %collective-permute-done.1.refs_2_, bf16[304,256]{1,0:T(8,128)(2,1)S(1)} %collective-permute-done.2.refs_3_, ...), custom_call_target="tpu_custom_call" | custom-call | tf_op jit(solution)/shard_map/grad/pallas_call | solution.py:461
  15.1 0.9 %shard_map.104 = (f32[2,128,512]{2,1,0:T(8,128)S(1)}, f32[72,512]{1,0:T(8,128)S(1)}, f32[80,512]{1,0:T(8,128)S(1)}, f32[80,512]{1,0:T(8,128)S(1)}) custom-call(s32[4]{0:T(128)S(1)} %reshape.7.sh_ref, f32[2,144,512]{2,1,0:T(8,128)S(1)} %get-tuple-element.29.g_ref, f32[8,512]{1,0:T(8,128)S(1)} %get-tuple-element.30.next_ref), custom_call_target="tpu_custom_call" | custom-call | tf_op jit(solution)/shard_map/pallas_call | solution.py:482
  16.1 1.8 %collective-permute-start.6 = (f16[80,512]{1,0:T(8,128)(2,1)S(1)}, f16[80,512]{1,0:T(8,128)(2,1)S(1)}, u32[]{:S(2)}, u32[]{:S(2)}) collective-permute-start(f16[80,512]{1,0:T(8,128)(2,1)S(1)} %convert_element_type.28), channel_id=1, source_target_pairs={{0,4},{4,0},{8,12},{12,8},{16,20},{20,16},{24,28},{28,24},{1,5},{5... | collective-permute-start | bytes 245768 | tf_op jit(solution)/shard_map/ppermute | solution.py:398
  17.9 1.3 %collective-permute-start.7 = (f16[80,512]{1,0:T(8,128)(2,1)S(1)}, f16[80,512]{1,0:T(8,128)(2,1)S(1)}, u32[]{:S(2)}, u32[]{:S(2)}) collective-permute-start(f16[80,512]{1,0:T(8,128)(2,1)S(1)} %convert_element_type.30), channel_id=1, source_target_pairs={{8,0},{12,4},{16,8},{20,12},{24,16},{28,20},{9,1},{13,5},{17,9},{2... | collective-permute-start | bytes 245768 | tf_op jit(solution)/shard_map/ppermute | solution.py:398
  19.2 1.3 %collective-permute-start.8 = (f16[80,512]{1,0:T(8,128)(2,1)S(1)}, f16[80,512]{1,0:T(8,128)(2,1)S(1)}, u32[]{:S(2)}, u32[]{:S(2)}) collective-permute-start(f16[80,512]{1,0:T(8,128)(2,1)S(1)} %convert_element_type.28), channel_id=1, source_target_pairs={{8,4},{12,0},{16,12},{20,8},{24,20},{28,16},{9,5},{13,1},{17,13},{... | collective-permute-start | bytes 245768 | tf_op jit(solution)/shard_map/ppermute | solution.py:398
  20.5 0.3 collective-permute-start.9
  20.9 0.0 collective-permute-done.6
  20.9 3.4 %collective-permute-done.7 = f16[80,512]{1,0:T(8,128)(2,1)S(1)} collective-permute-done((f16[80,512]{1,0:T(8,128)(2,1)S(1)}, f16[80,512]{1,0:T(8,128)(2,1)S(1)}, u32[]{:S(2)}, u32[]{:S(2)}) %collective-permute-start.7) | collective-permute-done | bytes 81952 | tf_op jit(solution)/shard_map/ppermute | solution.py:398
  24.3 2.1 %collective-permute-done.8 = f16[80,512]{1,0:T(8,128)(2,1)S(1)} collective-permute-done((f16[80,512]{1,0:T(8,128)(2,1)S(1)}, f16[80,512]{1,0:T(8,128)(2,1)S(1)}, u32[]{:S(2)}, u32[]{:S(2)}) %collective-permute-start.8) | collective-permute-done | bytes 81952 | tf_op jit(solution)/shard_map/ppermute | solution.py:398
  26.5 0.0 copy-start.1
  26.5 1.6 %shard_map.105 = (f32[72,512]{1,0:T(8,128)S(1)}, f32[72,512]{1,0:T(8,128)}, f32[72,512]{1,0:T(8,128)S(1)}, f32[80,512]{1,0:T(8,128)S(1)}, s32[4]{0:T(128)S(1)}) custom-call(s32[4]{0:T(128)S(1)} %reshape.7.sh_ref, f32[72,512]{1,0:T(8,128)S(1)} %get-tuple-element.31.keep_ref, f32[80,512]{1,0:T(8,128)S(1)} %get-tuple-element.32.sent_ref, ...), custom_call_target="tpu_custom_call" | custom-call | tf_op jit(solution)/shard_map/pallas_call | solution.py:489
  28.1 1.3 %collective-permute-start.10 = (f16[80,512]{1,0:T(8,128)(2,1)S(1)}, f16[80,512]{1,0:T(8,128)(2,1)S(1)}, u32[]{:S(2)}, u32[]{:S(2)}) collective-permute-start(f16[80,512]{1,0:T(8,128)(2,1)S(1)} %convert_element_type.33), channel_id=1, source_target_pairs={{16,0},{20,4},{24,8},{28,12},{17,1},{21,5},{25,9},{29,13},{18,2},{... | collective-permute-start | bytes 245768 | tf_op jit(solution)/shard_map/ppermute | solution.py:398
  29.4 0.0 collective-permute-done.9.side_ref
  29.5 0.0 copy-done.1
  29.5 2.2 %shard_map.106 = (f32[2,72,512]{2,1,0:T(8,128)S(1)}, f32[2,72,512]{2,1,0:T(8,128)S(1)}, f32[2]{0:T(128)S(1)}) custom-call(s32[4]{0:T(128)S(1)} %reshape.7.sh_ref, bf16[2,128,512]{2,1,0:T(8,128)(2,1)S(1)} %copy-done.1, bf16[2,72,512]{2,1,0:T(8,128)(2,1)S(1)} %collective-permute-done.9.side_ref, f32[8,512]{1,0:T(8,128)S(1)} %get-tuple-element.30.next_ref, ...), custom_call_target="tpu_custom_call" | custom-call | tf_op jit(solution)/shard_map/pallas_call | solution.py:495
  31.7 4.2 %collective-permute-done.10 = f16[80,512]{1,0:T(8,128)(2,1)S(1)} collective-permute-done((f16[80,512]{1,0:T(8,128)(2,1)S(1)}, f16[80,512]{1,0:T(8,128)(2,1)S(1)}, u32[]{:S(2)}, u32[]{:S(2)}) %collective-permute-start.10) | collective-permute-done | bytes 81952 | tf_op jit(solution)/shard_map/ppermute | solution.py:398
  35.9 1.6 %shard_map.107 = (f32[72,512]{1,0:T(8,128)S(1)}, f32[80,512]{1,0:T(8,128)S(1)}, f32[32,1,128]{2,1,0:T(1,128)}) custom-call(s32[4]{0:T(128)S(1)} %get-tuple-element.34.info_ref, f32[2]{0:T(128)S(1)} %get-tuple-element.37.wind_in, f32[72,512]{1,0:T(8,128)S(1)} %get-tuple-element.38.late_ref, f32[72,512]{1,0:T(8,128)S(1)} %get-tuple-element.39.excl_ref, ...), custom_call_target="tpu_custom_call" | custom-call | tf_op jit(solution)/shard_map/pallas_call | solution.py:509
  37.6 3.4 %all-to-all-start = ((f32[32,1,128]{2,1,0:T(1,128)}), f32[32,1,128]{2,1,0:T(1,128)S(1)}, u32[]{:S(2)}, u32[]{:S(2)}) async-start(f32[32,1,128]{2,1,0:T(1,128)} %get-tuple-element.45), calls=%async_computation | async-start | bytes 32768 | tf_op jit(solution)/shard_map/all_to_all | solution.py:514
  41.0 1.8 %collective-permute-start.11 = (f16[80,512]{1,0:T(8,128)(2,1)S(1)}, f16[80,512]{1,0:T(8,128)(2,1)S(1)}, u32[]{:S(2)}, u32[]{:S(2)}) collective-permute-start(f16[80,512]{1,0:T(8,128)(2,1)S(1)} %convert_element_type.35), channel_id=1, source_target_pairs={{0,4},{4,0},{8,12},{12,8},{16,20},{20,16},{24,28},{28,24},{1,5},{5... | collective-permute-start | bytes 245768 | tf_op jit(solution)/shard_map/ppermute | solution.py:398
  42.8 5.2 %all-to-all-done = f32[32,1,128]{2,1,0:T(1,128)S(1)} async-done(((f32[32,1,128]{2,1,0:T(1,128)}), f32[32,1,128]{2,1,0:T(1,128)S(1)}, u32[]{:S(2)}, u32[]{:S(2)}) %all-to-all-start) | async-done | bytes 16416 | tf_op jit(solution)/shard_map/all_to_all | solution.py:514
  48.1 0.1 slice_reduce_fusion
  48.1 0.5 %negate_multiply_fusion = f32[2]{0:T(128)} fusion(f32[2]{0:T(128)S(1)} %slice_reduce_fusion), kind=kLoop, calls=%fused_computation.1 | loop fusion | flops 4 | bytes 16 | tf_op jit(solution)/shard_map/div | solution.py:520
  48.7 0.0 collective-permute-done.11
  48.7 1.6 %shard_map.108 = f32[2,128,512]{2,1,0:T(8,128)} custom-call(s32[4]{0:T(128)S(1)} %reshape.7.sh_ref, f32[72,512]{1,0:T(8,128)S(1)} %get-tuple-element.43.keep_ref, f32[80,512]{1,0:T(8,128)S(1)} %convert_element_type.36.got_ref, f32[2,128,512]{2,1,0:T(8,128)S(1)} %get-tuple-element.36.loc_ref), custom_call_target="tpu_custom_call" | custom-call | bytes 1572864 | tf_op jit(solution)/shard_map/pallas_call | solution.py:516
  (9 shorter events, 0.1 us)
Async XLA Ops:
  0.6 13.0 %copy-start = (s32[128,512]{1,0:T(8,128)S(1)}, s32[128,512]{1,0:T(8,128)}, u32[]{:S(2)}) copy-start(s32[128,512]{1,0:T(8,128)} %refs_8_.1) | copy-start | bytes 786436
  0.6 4.8 %copy-start.2 = (bf16[2,2,64,256]{3,2,1,0:T(8,128)(2,1)S(1)}, bf16[2,2,64,256]{3,2,1,0:T(8,128)(2,1)}, u32[]{:S(2)}) copy-start(bf16[2,2,64,256]{3,2,1,0:T(8,128)(2,1)} %refs_4_.1) | copy-start | bytes 393220
  2.4 9.9 %copy-start.3 = (s32[2,2]{1,0:T(2,128)S(1)}, s32[2,2]{1,0:T(2,128)}, u32[]{:S(2)}) copy-start(s32[2,2]{1,0:T(2,128)} %param.11) | copy-start | bytes 52
  2.4 7.9 %collective-permute-start.1 = (bf16[304,256]{1,0:T(8,128)(2,1)S(1)}, bf16[304,256]{1,0:T(8,128)(2,1)S(1)}, u32[]{:S(2)}, u32[]{:S(2)}) collective-permute-start(bf16[304,256]{1,0:T(8,128)(2,1)S(1)} %get-tuple-element.24.refs_0_), channel_id=1, source_target_pairs={{0,2},{1,3},{2,0},{3,1},{4,6},{5,7},{6,4},{7,5},{8,10},{9,11},{10,... | collective-permute-start | bytes 466952 | tf_op jit(solution)/shard_map/ppermute | solution.py:381
  5.4 6.8 %collective-permute-start.4 = (bf16[2,2,64,256]{3,2,1,0:T(8,128)(2,1)S(1)}, bf16[2,2,64,256]{3,2,1,0:T(8,128)(2,1)S(1)}, u32[]{:S(2)}, u32[]{:S(2)}) collective-permute-start(bf16[2,2,64,256]{3,2,1,0:T(8,128)(2,1)S(1)} %copy-done.2), channel_id=1, source_target_pairs={{0,2},{1,3},{2,0},{3,1},{4,6},{5,7},{6,4},{7,5},{8,10},{9,11},{10,... | collective-permute-start | bytes 393224 | tf_op jit(solution)/shard_map/ppermute | solution.py:381
  5.5 6.8 %collective-permute-start = (bf16[304,256]{1,0:T(8,128)(2,1)S(1)}, bf16[304,256]{1,0:T(8,128)(2,1)S(1)}, u32[]{:S(2)}, u32[]{:S(2)}) collective-permute-start(bf16[304,256]{1,0:T(8,128)(2,1)S(1)} %get-tuple-element.24.refs_0_), channel_id=1, source_target_pairs={{0,1},{1,0},{2,3},{3,2},{4,5},{5,4},{6,7},{7,6},{8,9},{9,8},{10,11... | collective-permute-start | bytes 466952 | tf_op jit(solution)/shard_map/ppermute | solution.py:381
  10.3 3.3 %collective-permute-start.2 = (bf16[304,256]{1,0:T(8,128)(2,1)S(1)}, bf16[304,256]{1,0:T(8,128)(2,1)S(1)}, u32[]{:S(2)}, u32[]{:S(2)}) collective-permute-start(bf16[304,256]{1,0:T(8,128)(2,1)S(1)} %collective-permute-done.1.refs_2_), channel_id=1, source_target_pairs={{0,1},{1,0},{2,3},{3,2},{4,5},{5,4},{6,7},{7,6},{8,9},{9,8},{10,11... | collective-permute-start | bytes 466952 | tf_op jit(solution)/shard_map/ppermute | solution.py:381
  10.3 2.0 %collective-permute-start.3 = (bf16[2,2,64,256]{3,2,1,0:T(8,128)(2,1)S(1)}, bf16[2,2,64,256]{3,2,1,0:T(8,128)(2,1)S(1)}, u32[]{:S(2)}, u32[]{:S(2)}) collective-permute-start(bf16[2,2,64,256]{3,2,1,0:T(8,128)(2,1)S(1)} %copy-done.2), channel_id=1, source_target_pairs={{0,1},{1,0},{2,3},{3,2},{4,5},{5,4},{6,7},{7,6},{8,9},{9,8},{10,11... | collective-permute-start | bytes 393224 | tf_op jit(solution)/shard_map/ppermute | solution.py:381
  12.3 1.3 %collective-permute-start.5 = (bf16[2,2,64,256]{3,2,1,0:T(8,128)(2,1)S(1)}, bf16[2,2,64,256]{3,2,1,0:T(8,128)(2,1)S(1)}, u32[]{:S(2)}, u32[]{:S(2)}) collective-permute-start(bf16[2,2,64,256]{3,2,1,0:T(8,128)(2,1)S(1)} %collective-permute-done.4.refs_6_), channel_id=1, source_target_pairs={{0,1},{1,0},{2,3},{3,2},{4,5},{5,4},{6,7},{7,6},{8,9},{9,8},{10,11... | collective-permute-start | bytes 393224 | tf_op jit(solution)/shard_map/ppermute | solution.py:381
  16.1 4.8 %collective-permute-start.6 = (f16[80,512]{1,0:T(8,128)(2,1)S(1)}, f16[80,512]{1,0:T(8,128)(2,1)S(1)}, u32[]{:S(2)}, u32[]{:S(2)}) collective-permute-start(f16[80,512]{1,0:T(8,128)(2,1)S(1)} %convert_element_type.28), channel_id=1, source_target_pairs={{0,4},{4,0},{8,12},{12,8},{16,20},{20,16},{24,28},{28,24},{1,5},{5... | collective-permute-start | bytes 245768 | tf_op jit(solution)/shard_map/ppermute | solution.py:398
  17.9 6.4 %collective-permute-start.7 = (f16[80,512]{1,0:T(8,128)(2,1)S(1)}, f16[80,512]{1,0:T(8,128)(2,1)S(1)}, u32[]{:S(2)}, u32[]{:S(2)}) collective-permute-start(f16[80,512]{1,0:T(8,128)(2,1)S(1)} %convert_element_type.30), channel_id=1, source_target_pairs={{8,0},{12,4},{16,8},{20,12},{24,16},{28,20},{9,1},{13,5},{17,9},{2... | collective-permute-start | bytes 245768 | tf_op jit(solution)/shard_map/ppermute | solution.py:398
  19.2 7.2 %collective-permute-start.8 = (f16[80,512]{1,0:T(8,128)(2,1)S(1)}, f16[80,512]{1,0:T(8,128)(2,1)S(1)}, u32[]{:S(2)}, u32[]{:S(2)}) collective-permute-start(f16[80,512]{1,0:T(8,128)(2,1)S(1)} %convert_element_type.28), channel_id=1, source_target_pairs={{8,4},{12,0},{16,12},{20,8},{24,20},{28,16},{9,5},{13,1},{17,13},{... | collective-permute-start | bytes 245768 | tf_op jit(solution)/shard_map/ppermute | solution.py:398
  20.5 8.9 %collective-permute-start.9 = (bf16[2,72,512]{2,1,0:T(8,128)(2,1)S(1)}, bf16[2,72,512]{2,1,0:T(8,128)(2,1)S(1)}, u32[]{:S(2)}, u32[]{:S(2)}) collective-permute-start(bf16[2,72,512]{2,1,0:T(8,128)(2,1)S(1)} %get-tuple-element.35), channel_id=1, source_target_pairs={{0,4},{4,0},{8,12},{12,8},{16,20},{20,16},{24,28},{28,24},{1,5},{5... | collective-permute-start | bytes 442376 | tf_op jit(solution)/shard_map/ppermute | solution.py:381
  26.5 3.0 %copy-start.1 = (bf16[2,128,512]{2,1,0:T(8,128)(2,1)S(1)}, bf16[2,128,512]{2,1,0:T(8,128)(2,1)}, u32[]{:S(2)}) copy-start(bf16[2,128,512]{2,1,0:T(8,128)(2,1)} %phases_ref.1) | copy-start | bytes 786436
  28.1 7.8 %collective-permute-start.10 = (f16[80,512]{1,0:T(8,128)(2,1)S(1)}, f16[80,512]{1,0:T(8,128)(2,1)S(1)}, u32[]{:S(2)}, u32[]{:S(2)}) collective-permute-start(f16[80,512]{1,0:T(8,128)(2,1)S(1)} %convert_element_type.33), channel_id=1, source_target_pairs={{16,0},{20,4},{24,8},{28,12},{17,1},{21,5},{25,9},{29,13},{18,2},{... | collective-permute-start | bytes 245768 | tf_op jit(solution)/shard_map/ppermute | solution.py:398
  37.6 10.5 %all-to-all-start = ((f32[32,1,128]{2,1,0:T(1,128)}), f32[32,1,128]{2,1,0:T(1,128)S(1)}, u32[]{:S(2)}, u32[]{:S(2)}) async-start(f32[32,1,128]{2,1,0:T(1,128)} %get-tuple-element.45), calls=%async_computation | async-start | bytes 32768 | tf_op jit(solution)/shard_map/all_to_all | solution.py:514
  41.0 7.7 %collective-permute-start.11 = (f16[80,512]{1,0:T(8,128)(2,1)S(1)}, f16[80,512]{1,0:T(8,128)(2,1)S(1)}, u32[]{:S(2)}, u32[]{:S(2)}) collective-permute-start(f16[80,512]{1,0:T(8,128)(2,1)S(1)} %convert_element_type.35), channel_id=1, source_target_pairs={{0,4},{4,0},{8,12},{12,8},{16,20},{20,16},{24,28},{28,24},{1,5},{5... | collective-permute-start | bytes 245768 | tf_op jit(solution)/shard_map/ppermute | solution.py:398

commit v8 on v7

--- a/solution.py
+++ b/solution.py
@@ -37,7 +37,7 @@
     return lax.broadcasted_iota(jnp.int32, shape, 1)
 
 
-def y_kernel(halo, phases_hbm, mask_hbm, half_hbm, *refs):
+def y_kernel(reach_rows, phases_hbm, mask_hbm, half_hbm, *refs):
     count = (len(refs) - 6) // 2
     y_ref, side_ref = refs[count], refs[-5]
     phases_ref, mask_ref, half_ref, sem = refs[-4:]
@@ -71,9 +71,10 @@
     y_ref[at : at + 16] = edge.astype(jnp.bfloat16)
     y_ref[at : at + 16, :block] = (edge[:, :block] + dc).astype(jnp.bfloat16)
     at = at + 16
-    mask = mask_ref[:halo].astype(jnp.float32).astype(jnp.bfloat16)
+    mask = mask_ref[:reach_rows].astype(jnp.float32).astype(jnp.bfloat16)
     for i in range(parts):
-        y_ref[at + i * halo : at + (i + 1) * halo] = mask[:, i * focal : (i + 1) * focal]
+        here = slice(at + i * reach_rows, at + (i + 1) * reach_rows)
+        y_ref[here] = mask[:, i * focal : (i + 1) * focal]
     side_ref[...] = half_phases(phases_ref, 1 - lax.axis_index("tm") % 2)
     for copy in copies[3:]:
         copy.wait()
@@ -95,7 +96,7 @@
     return lax.dot_general(a, b, (((1,), (1,)), ((), ())), preferred_element_type=jnp.float32)
 
 
-def grad_kernel(n_rows, halo, *refs):
+def grad_kernel(n_rows, reach_rows, halo, *refs):
     m_refs, d_refs = refs[:n_rows], refs[n_rows : 2 * n_rows]
     mask_ref, tt_ref, cs_ref, turned_ref, flip_ref = refs[2 * n_rows : 2 * n_rows + 5]
     g_ref, next_ref = refs[2 * n_rows + 5 : 2 * n_rows + 7]
@@ -122,8 +123,8 @@
                     next_ref[k : k + 1, i * focal : (i + 1) * focal] = edge[line : line + 1]
             at = at + 16
             for i in range(parts):
-                over_ref[:, i * focal : (i + 1) * focal] = m_refs[d][
-                    at + i * halo : at + (i + 1) * halo
+                over_ref[:reach_rows, i * focal : (i + 1) * focal] = m_refs[d][
+                    at + i * reach_rows : at + (i + 1) * reach_rows
                 ].astype(jnp.float32)
 
     for d in range(n_rows):
@@ -436,9 +437,11 @@
     kept = [tt, cs, cs_turned, flip]
     side_shape = (frames, block // 2 + 8, width)
     y, *kept, side = pl.pallas_call(
-        functools.partial(y_kernel, halo),
+        functools.partial(y_kernel, reach_rows),
         out_shape=[
-            jax.ShapeDtypeStruct((frames * block + 16 + halo * width // focal, focal), jnp.bfloat16)
+            jax.ShapeDtypeStruct(
+                (frames * block + 16 + reach_rows * width // focal, focal), jnp.bfloat16
+            )
         ]
         + [jax.ShapeDtypeStruct(t.shape, jnp.bfloat16) for t in kept]
         + [jax.ShapeDtypeStruct(side_shape, jnp.bfloat16)],
@@ -459,7 +462,7 @@
     field = jax.ShapeDtypeStruct((frames, block, width), jnp.float32)
     pair = jax.ShapeDtypeStruct((2,), jnp.float32)
     grads, next_rows = pl.pallas_call(
-        functools.partial(grad_kernel, n_rows, halo),
+        functools.partial(grad_kernel, n_rows, reach_rows, halo),
         out_shape=(
             jax.ShapeDtypeStruct((frames, rows, width), jnp.float32),
             jax.ShapeDtypeStruct((-(-frames // 8) * 8, width), jnp.float32),

time: 50.6 us -> 50.4 us (level)
  no operation moved by 1% of the time
where the time goes in v8:
time: 50.4 us; the launch traced here: 50.1 us
  waiting for transfers between devices  22.4 us (44%)
  starting transfers between devices  14.9 us (30%)
  Pallas kernels  11.3 us (22%)
  between operations  0.81 us (2%)
  other arithmetic  0.68 us (1%)
    ppermute x5, waiting for transfers between devices, permute_16(): lax.ppermute(value.astype(jnp.float16), 'tm', route).astype(jnp.float32)  9.79 us
    ppermute x5, starting transfers between devices, permute_16(): lax.ppermute(value.astype(jnp.float16), 'tm', route).astype(jnp.float32)  7.55 us
    ppermute x7, waiting for transfers between devices, swap(): return lax.ppermute(value, axis, [(s, s ^ bit) for s in range(count)])  7.32 us
    all_to_all x1, waiting for transfers between devices, on_device(): winds = lax.all_to_all(wind, ('tm', 'rows'), 0, 0)  5.25 us
    ppermute x7, starting transfers between devices, swap(): return lax.ppermute(value, axis, [(s, s ^ bit) for s in range(count)])  3.95 us
    all_to_all x1, starting transfers between devices, on_device(): winds = lax.all_to_all(wind, ('tm', 'rows'), 0, 0)  3.41 us
    pallas_call x1, Pallas kernels, on_device(): kernel_call(z_kernel, 12, (products, products, pair), [smem] + [vmem] * 6...  2.22 us
    pallas_call x1, Pallas kernels, on_device(): pl.pallas_call(functools.partial(y_kernel, reach_rows), out_shape=[jax.Sh...  1.74 us
  transfers between devices with their start and end apart: 13, of which 7 were waited for; matrix products, arithmetic and copies ran while one was open for 1% of the time, Pallas kernels for 8%

profile of v8, /device:TPU:0, one launch (start us, length us, event | category | flops | bytes accessed | tf_op | source)
XLA Modules:
  0.0 50.1 jit_solution(14754746964450389278)
XLA Ops:
  0.6 0.0 copy-start
  0.6 0.0 copy-start.2
  0.6 1.7 %transform.1 = (bf16[288,256]{1,0:T(8,128)(2,1)S(1)}, bf16[528,512]{1,0:T(8,128)(2,1)S(1)}, bf16[512,512]{1,0:T(8,128)(2,1)S(1)}, bf16[512,512]{1,0:T(8,128)(2,1...) custom-call(bf16[2,128,512]{2,1,0:T(8,128)(2,1)} %phases_ref.1, s32[128,512]{1,0:T(8,128)} %refs_8_.1, ...), custom_call_target="tpu_custom_call" | custom-call | tf_op jit(solution)/shard_map/transform/pallas_call | solution.py:439
  2.4 0.0 copy-start.3
  2.4 3.0 %collective-permute-start.1 = (bf16[288,256]{1,0:T(8,128)(2,1)S(1)}, bf16[288,256]{1,0:T(8,128)(2,1)S(1)}, u32[]{:S(2)}, u32[]{:S(2)}) collective-permute-start(bf16[288,256]{1,0:T(8,128)(2,1)S(1)} %get-tuple-element.24.refs_0_), channel_id=1, source_target_pairs={{0,2},{1,3},{2,0},{3,1},{4,6},{5,7},{6,4},{7,5},{8,10},{9,11},{10,... | collective-permute-start | bytes 442376 | tf_op jit(solution)/shard_map/ppermute | solution.py:382
  5.4 0.0 copy-done.2
  5.4 0.1 collective-permute-start.4
  5.5 0.0 collective-permute-start
  5.5 4.6 %collective-permute-done.1.refs_2_ = bf16[288,256]{1,0:T(8,128)(2,1)S(1)} collective-permute-done((bf16[288,256]{1,0:T(8,128)(2,1)S(1)}, bf16[288,256]{1,0:T(8,128)(2,1)S(1)}, u32[]{:S(2)}, u32[]{:S(2)}) %collective-permute-start.1) | collective-permute-done | bytes 147488 | tf_op jit(solution)/shard_map/ppermute | solution.py:382
  10.1 0.0 collective-permute-start.2
  10.1 0.5 %collective-permute-start.3 = (bf16[2,2,64,256]{3,2,1,0:T(8,128)(2,1)S(1)}, bf16[2,2,64,256]{3,2,1,0:T(8,128)(2,1)S(1)}, u32[]{:S(2)}, u32[]{:S(2)}) collective-permute-start(bf16[2,2,64,256]{3,2,1,0:T(8,128)(2,1)S(1)} %copy-done.2), channel_id=1, source_target_pairs={{0,1},{1,0},{2,3},{3,2},{4,5},{5,4},{6,7},{7,6},{8,9},{9,8},{10,11... | collective-permute-start | bytes 393224 | tf_op jit(solution)/shard_map/ppermute | solution.py:382
  10.6 1.4 %collective-permute-done.4.refs_6_ = bf16[2,2,64,256]{3,2,1,0:T(8,128)(2,1)S(1)} collective-permute-done((bf16[2,2,64,256]{3,2,1,0:T(8,128)(2,1)S(1)}, bf16[2,2,64,256]{3,2,1,0:T(8,128)(2,1)S(1)}, u32[]{:S(2)}, u32[]{:S(2)}) %collective-permute-start.4) | collective-permute-done | bytes 131104 | tf_op jit(solution)/shard_map/ppermute | solution.py:382
  12.1 0.0 collective-permute-start.5
  12.1 0.0 copy-done.3
  12.1 0.1 reshape.7.sh_ref
  12.2 0.0 collective-permute-done.3.refs_5_
  12.2 0.0 collective-permute-done.refs_1_
  12.2 1.3 %collective-permute-done.5.refs_7_ = bf16[2,2,64,256]{3,2,1,0:T(8,128)(2,1)S(1)} collective-permute-done((bf16[2,2,64,256]{3,2,1,0:T(8,128)(2,1)S(1)}, bf16[2,2,64,256]{3,2,1,0:T(8,128)(2,1)S(1)}, u32[]{:S(2)}, u32[]{:S(2)}) %collective-permute-start.5) | collective-permute-done | bytes 131104 | tf_op jit(solution)/shard_map/ppermute | solution.py:382
  13.4 0.0 collective-permute-done.2.refs_3_
  13.4 0.0 copy-done
  13.4 1.5 %grad.1 = (f32[2,144,512]{2,1,0:T(8,128)S(1)}, f32[8,512]{1,0:T(8,128)S(1)}) custom-call(bf16[288,256]{1,0:T(8,128)(2,1)S(1)} %get-tuple-element.24.refs_0_, bf16[288,256]{1,0:T(8,128)(2,1)S(1)} %collective-permute-done.refs_1_, bf16[288,256]{1,0:T(8,128)(2,1)S(1)} %collective-permute-done.1.refs_2_, bf16[288,256]{1,0:T(8,128)(2,1)S(1)} %collective-permute-done.2.refs_3_, ...), custom_call_target="tpu_custom_call" | custom-call | tf_op jit(solution)/shard_map/grad/pallas_call | solution.py:464
  15.0 0.9 %shard_map.104 = (f32[2,128,512]{2,1,0:T(8,128)S(1)}, f32[72,512]{1,0:T(8,128)S(1)}, f32[80,512]{1,0:T(8,128)S(1)}, f32[80,512]{1,0:T(8,128)S(1)}) custom-call(s32[4]{0:T(128)S(1)} %reshape.7.sh_ref, f32[2,144,512]{2,1,0:T(8,128)S(1)} %get-tuple-element.29.g_ref, f32[8,512]{1,0:T(8,128)S(1)} %get-tuple-element.30.next_ref), custom_call_target="tpu_custom_call" | custom-call | tf_op jit(solution)/shard_map/pallas_call | solution.py:485
  15.9 1.8 %collective-permute-start.6 = (f16[80,512]{1,0:T(8,128)(2,1)S(1)}, f16[80,512]{1,0:T(8,128)(2,1)S(1)}, u32[]{:S(2)}, u32[]{:S(2)}) collective-permute-start(f16[80,512]{1,0:T(8,128)(2,1)S(1)} %convert_element_type.28), channel_id=1, source_target_pairs={{0,4},{4,0},{8,12},{12,8},{16,20},{20,16},{24,28},{28,24},{1,5},{5... | collective-permute-start | bytes 245768 | tf_op jit(solution)/shard_map/ppermute | solution.py:399
  17.8 1.3 %collective-permute-start.7 = (f16[80,512]{1,0:T(8,128)(2,1)S(1)}, f16[80,512]{1,0:T(8,128)(2,1)S(1)}, u32[]{:S(2)}, u32[]{:S(2)}) collective-permute-start(f16[80,512]{1,0:T(8,128)(2,1)S(1)} %convert_element_type.30), channel_id=1, source_target_pairs={{8,0},{12,4},{16,8},{20,12},{24,16},{28,20},{9,1},{13,5},{17,9},{2... | collective-permute-start | bytes 245768 | tf_op jit(solution)/shard_map/ppermute | solution.py:399
  19.1 1.3 %collective-permute-start.8 = (f16[80,512]{1,0:T(8,128)(2,1)S(1)}, f16[80,512]{1,0:T(8,128)(2,1)S(1)}, u32[]{:S(2)}, u32[]{:S(2)}) collective-permute-start(f16[80,512]{1,0:T(8,128)(2,1)S(1)} %convert_element_type.28), channel_id=1, source_target_pairs={{8,4},{12,0},{16,12},{20,8},{24,20},{28,16},{9,5},{13,1},{17,13},{... | collective-permute-start | bytes 245768 | tf_op jit(solution)/shard_map/ppermute | solution.py:399
  20.4 0.3 collective-permute-start.9
  20.7 0.0 collective-permute-done.6
  20.7 3.4 %collective-permute-done.7 = f16[80,512]{1,0:T(8,128)(2,1)S(1)} collective-permute-done((f16[80,512]{1,0:T(8,128)(2,1)S(1)}, f16[80,512]{1,0:T(8,128)(2,1)S(1)}, u32[]{:S(2)}, u32[]{:S(2)}) %collective-permute-start.7) | collective-permute-done | bytes 81952 | tf_op jit(solution)/shard_map/ppermute | solution.py:399
  24.2 2.1 %collective-permute-done.8 = f16[80,512]{1,0:T(8,128)(2,1)S(1)} collective-permute-done((f16[80,512]{1,0:T(8,128)(2,1)S(1)}, f16[80,512]{1,0:T(8,128)(2,1)S(1)}, u32[]{:S(2)}, u32[]{:S(2)}) %collective-permute-start.8) | collective-permute-done | bytes 81952 | tf_op jit(solution)/shard_map/ppermute | solution.py:399
  26.3 0.0 copy-start.1
  26.3 1.6 %shard_map.105 = (f32[72,512]{1,0:T(8,128)S(1)}, f32[72,512]{1,0:T(8,128)}, f32[72,512]{1,0:T(8,128)S(1)}, f32[80,512]{1,0:T(8,128)S(1)}, s32[4]{0:T(128)S(1)}) custom-call(s32[4]{0:T(128)S(1)} %reshape.7.sh_ref, f32[72,512]{1,0:T(8,128)S(1)} %get-tuple-element.31.keep_ref, f32[80,512]{1,0:T(8,128)S(1)} %get-tuple-element.32.sent_ref, ...), custom_call_target="tpu_custom_call" | custom-call | tf_op jit(solution)/shard_map/pallas_call | solution.py:492
  28.0 1.3 %collective-permute-start.10 = (f16[80,512]{1,0:T(8,128)(2,1)S(1)}, f16[80,512]{1,0:T(8,128)(2,1)S(1)}, u32[]{:S(2)}, u32[]{:S(2)}) collective-permute-start(f16[80,512]{1,0:T(8,128)(2,1)S(1)} %convert_element_type.33), channel_id=1, source_target_pairs={{16,0},{20,4},{24,8},{28,12},{17,1},{21,5},{25,9},{29,13},{18,2},{... | collective-permute-start | bytes 245768 | tf_op jit(solution)/shard_map/ppermute | solution.py:399
  29.3 0.0 collective-permute-done.9.side_ref
  29.3 0.0 copy-done.1
  29.3 2.2 %shard_map.106 = (f32[2,72,512]{2,1,0:T(8,128)S(1)}, f32[2,72,512]{2,1,0:T(8,128)S(1)}, f32[2]{0:T(128)S(1)}) custom-call(s32[4]{0:T(128)S(1)} %reshape.7.sh_ref, bf16[2,128,512]{2,1,0:T(8,128)(2,1)S(1)} %copy-done.1, bf16[2,72,512]{2,1,0:T(8,128)(2,1)S(1)} %collective-permute-done.9.side_ref, f32[8,512]{1,0:T(8,128)S(1)} %get-tuple-element.30.next_ref, ...), custom_call_target="tpu_custom_call" | custom-call | tf_op jit(solution)/shard_map/pallas_call | solution.py:498
  31.5 4.2 %collective-permute-done.10 = f16[80,512]{1,0:T(8,128)(2,1)S(1)} collective-permute-done((f16[80,512]{1,0:T(8,128)(2,1)S(1)}, f16[80,512]{1,0:T(8,128)(2,1)S(1)}, u32[]{:S(2)}, u32[]{:S(2)}) %collective-permute-start.10) | collective-permute-done | bytes 81952 | tf_op jit(solution)/shard_map/ppermute | solution.py:399
  35.7 1.6 %shard_map.107 = (f32[72,512]{1,0:T(8,128)S(1)}, f32[80,512]{1,0:T(8,128)S(1)}, f32[32,1,128]{2,1,0:T(1,128)}) custom-call(s32[4]{0:T(128)S(1)} %get-tuple-element.34.info_ref, f32[2]{0:T(128)S(1)} %get-tuple-element.37.wind_in, f32[72,512]{1,0:T(8,128)S(1)} %get-tuple-element.38.late_ref, f32[72,512]{1,0:T(8,128)S(1)} %get-tuple-element.39.excl_ref, ...), custom_call_target="tpu_custom_call" | custom-call | tf_op jit(solution)/shard_map/pallas_call | solution.py:512
  37.4 3.4 %all-to-all-start = ((f32[32,1,128]{2,1,0:T(1,128)}), f32[32,1,128]{2,1,0:T(1,128)S(1)}, u32[]{:S(2)}, u32[]{:S(2)}) async-start(f32[32,1,128]{2,1,0:T(1,128)} %get-tuple-element.45), calls=%async_computation | async-start | bytes 32768 | tf_op jit(solution)/shard_map/all_to_all | solution.py:517
  40.8 1.8 %collective-permute-start.11 = (f16[80,512]{1,0:T(8,128)(2,1)S(1)}, f16[80,512]{1,0:T(8,128)(2,1)S(1)}, u32[]{:S(2)}, u32[]{:S(2)}) collective-permute-start(f16[80,512]{1,0:T(8,128)(2,1)S(1)} %convert_element_type.35), channel_id=1, source_target_pairs={{0,4},{4,0},{8,12},{12,8},{16,20},{20,16},{24,28},{28,24},{1,5},{5... | collective-permute-start | bytes 245768 | tf_op jit(solution)/shard_map/ppermute | solution.py:399
  42.7 5.2 %all-to-all-done = f32[32,1,128]{2,1,0:T(1,128)S(1)} async-done(((f32[32,1,128]{2,1,0:T(1,128)}), f32[32,1,128]{2,1,0:T(1,128)S(1)}, u32[]{:S(2)}, u32[]{:S(2)}) %all-to-all-start) | async-done | bytes 16416 | tf_op jit(solution)/shard_map/all_to_all | solution.py:517
  47.9 0.1 slice_reduce_fusion
  48.0 0.5 %negate_multiply_fusion = f32[2]{0:T(128)} fusion(f32[2]{0:T(128)S(1)} %slice_reduce_fusion), kind=kLoop, calls=%fused_computation.1 | loop fusion | flops 4 | bytes 16 | tf_op jit(solution)/shard_map/div | solution.py:523
  48.5 0.0 collective-permute-done.11
  48.5 1.6 %shard_map.108 = f32[2,128,512]{2,1,0:T(8,128)} custom-call(s32[4]{0:T(128)S(1)} %reshape.7.sh_ref, f32[72,512]{1,0:T(8,128)S(1)} %get-tuple-element.43.keep_ref, f32[80,512]{1,0:T(8,128)S(1)} %convert_element_type.36.got_ref, f32[2,128,512]{2,1,0:T(8,128)S(1)} %get-tuple-element.36.loc_ref), custom_call_target="tpu_custom_call" | custom-call | bytes 1572864 | tf_op jit(solution)/shard_map/pallas_call | solution.py:519
  (9 shorter events, 0.1 us)
Async XLA Ops:
  0.6 12.8 %copy-start = (s32[128,512]{1,0:T(8,128)S(1)}, s32[128,512]{1,0:T(8,128)}, u32[]{:S(2)}) copy-start(s32[128,512]{1,0:T(8,128)} %refs_8_.1) | copy-start | bytes 786436
  0.6 4.8 %copy-start.2 = (bf16[2,2,64,256]{3,2,1,0:T(8,128)(2,1)S(1)}, bf16[2,2,64,256]{3,2,1,0:T(8,128)(2,1)}, u32[]{:S(2)}) copy-start(bf16[2,2,64,256]{3,2,1,0:T(8,128)(2,1)} %refs_4_.1) | copy-start | bytes 393220
  2.4 9.7 %copy-start.3 = (s32[2,2]{1,0:T(2,128)S(1)}, s32[2,2]{1,0:T(2,128)}, u32[]{:S(2)}) copy-start(s32[2,2]{1,0:T(2,128)} %param.11) | copy-start | bytes 52
  2.4 7.7 %collective-permute-start.1 = (bf16[288,256]{1,0:T(8,128)(2,1)S(1)}, bf16[288,256]{1,0:T(8,128)(2,1)S(1)}, u32[]{:S(2)}, u32[]{:S(2)}) collective-permute-start(bf16[288,256]{1,0:T(8,128)(2,1)S(1)} %get-tuple-element.24.refs_0_), channel_id=1, source_target_pairs={{0,2},{1,3},{2,0},{3,1},{4,6},{5,7},{6,4},{7,5},{8,10},{9,11},{10,... | collective-permute-start | bytes 442376 | tf_op jit(solution)/shard_map/ppermute | solution.py:382
  5.4 6.7 %collective-permute-start.4 = (bf16[2,2,64,256]{3,2,1,0:T(8,128)(2,1)S(1)}, bf16[2,2,64,256]{3,2,1,0:T(8,128)(2,1)S(1)}, u32[]{:S(2)}, u32[]{:S(2)}) collective-permute-start(bf16[2,2,64,256]{3,2,1,0:T(8,128)(2,1)S(1)} %copy-done.2), channel_id=1, source_target_pairs={{0,2},{1,3},{2,0},{3,1},{4,6},{5,7},{6,4},{7,5},{8,10},{9,11},{10,... | collective-permute-start | bytes 393224 | tf_op jit(solution)/shard_map/ppermute | solution.py:382
  5.5 6.7 %collective-permute-start = (bf16[288,256]{1,0:T(8,128)(2,1)S(1)}, bf16[288,256]{1,0:T(8,128)(2,1)S(1)}, u32[]{:S(2)}, u32[]{:S(2)}) collective-permute-start(bf16[288,256]{1,0:T(8,128)(2,1)S(1)} %get-tuple-element.24.refs_0_), channel_id=1, source_target_pairs={{0,1},{1,0},{2,3},{3,2},{4,5},{5,4},{6,7},{7,6},{8,9},{9,8},{10,11... | collective-permute-start | bytes 442376 | tf_op jit(solution)/shard_map/ppermute | solution.py:382
  10.1 3.3 %collective-permute-start.2 = (bf16[288,256]{1,0:T(8,128)(2,1)S(1)}, bf16[288,256]{1,0:T(8,128)(2,1)S(1)}, u32[]{:S(2)}, u32[]{:S(2)}) collective-permute-start(bf16[288,256]{1,0:T(8,128)(2,1)S(1)} %collective-permute-done.1.refs_2_), channel_id=1, source_target_pairs={{0,1},{1,0},{2,3},{3,2},{4,5},{5,4},{6,7},{7,6},{8,9},{9,8},{10,11... | collective-permute-start | bytes 442376 | tf_op jit(solution)/shard_map/ppermute | solution.py:382
  10.1 2.0 %collective-permute-start.3 = (bf16[2,2,64,256]{3,2,1,0:T(8,128)(2,1)S(1)}, bf16[2,2,64,256]{3,2,1,0:T(8,128)(2,1)S(1)}, u32[]{:S(2)}, u32[]{:S(2)}) collective-permute-start(bf16[2,2,64,256]{3,2,1,0:T(8,128)(2,1)S(1)} %copy-done.2), channel_id=1, source_target_pairs={{0,1},{1,0},{2,3},{3,2},{4,5},{5,4},{6,7},{7,6},{8,9},{9,8},{10,11... | collective-permute-start | bytes 393224 | tf_op jit(solution)/shard_map/ppermute | solution.py:382
  12.1 1.3 %collective-permute-start.5 = (bf16[2,2,64,256]{3,2,1,0:T(8,128)(2,1)S(1)}, bf16[2,2,64,256]{3,2,1,0:T(8,128)(2,1)S(1)}, u32[]{:S(2)}, u32[]{:S(2)}) collective-permute-start(bf16[2,2,64,256]{3,2,1,0:T(8,128)(2,1)S(1)} %collective-permute-done.4.refs_6_), channel_id=1, source_target_pairs={{0,1},{1,0},{2,3},{3,2},{4,5},{5,4},{6,7},{7,6},{8,9},{9,8},{10,11... | collective-permute-start | bytes 393224 | tf_op jit(solution)/shard_map/ppermute | solution.py:382
  15.9 4.8 %collective-permute-start.6 = (f16[80,512]{1,0:T(8,128)(2,1)S(1)}, f16[80,512]{1,0:T(8,128)(2,1)S(1)}, u32[]{:S(2)}, u32[]{:S(2)}) collective-permute-start(f16[80,512]{1,0:T(8,128)(2,1)S(1)} %convert_element_type.28), channel_id=1, source_target_pairs={{0,4},{4,0},{8,12},{12,8},{16,20},{20,16},{24,28},{28,24},{1,5},{5... | collective-permute-start | bytes 245768 | tf_op jit(solution)/shard_map/ppermute | solution.py:399
  17.8 6.4 %collective-permute-start.7 = (f16[80,512]{1,0:T(8,128)(2,1)S(1)}, f16[80,512]{1,0:T(8,128)(2,1)S(1)}, u32[]{:S(2)}, u32[]{:S(2)}) collective-permute-start(f16[80,512]{1,0:T(8,128)(2,1)S(1)} %convert_element_type.30), channel_id=1, source_target_pairs={{8,0},{12,4},{16,8},{20,12},{24,16},{28,20},{9,1},{13,5},{17,9},{2... | collective-permute-start | bytes 245768 | tf_op jit(solution)/shard_map/ppermute | solution.py:399
  19.1 7.2 %collective-permute-start.8 = (f16[80,512]{1,0:T(8,128)(2,1)S(1)}, f16[80,512]{1,0:T(8,128)(2,1)S(1)}, u32[]{:S(2)}, u32[]{:S(2)}) collective-permute-start(f16[80,512]{1,0:T(8,128)(2,1)S(1)} %convert_element_type.28), channel_id=1, source_target_pairs={{8,4},{12,0},{16,12},{20,8},{24,20},{28,16},{9,5},{13,1},{17,13},{... | collective-permute-start | bytes 245768 | tf_op jit(solution)/shard_map/ppermute | solution.py:399
  20.4 8.9 %collective-permute-start.9 = (bf16[2,72,512]{2,1,0:T(8,128)(2,1)S(1)}, bf16[2,72,512]{2,1,0:T(8,128)(2,1)S(1)}, u32[]{:S(2)}, u32[]{:S(2)}) collective-permute-start(bf16[2,72,512]{2,1,0:T(8,128)(2,1)S(1)} %get-tuple-element.35), channel_id=1, source_target_pairs={{0,4},{4,0},{8,12},{12,8},{16,20},{20,16},{24,28},{28,24},{1,5},{5... | collective-permute-start | bytes 442376 | tf_op jit(solution)/shard_map/ppermute | solution.py:382
  26.3 3.0 %copy-start.1 = (bf16[2,128,512]{2,1,0:T(8,128)(2,1)S(1)}, bf16[2,128,512]{2,1,0:T(8,128)(2,1)}, u32[]{:S(2)}) copy-start(bf16[2,128,512]{2,1,0:T(8,128)(2,1)} %phases_ref.1) | copy-start | bytes 786436
  28.0 7.8 %collective-permute-start.10 = (f16[80,512]{1,0:T(8,128)(2,1)S(1)}, f16[80,512]{1,0:T(8,128)(2,1)S(1)}, u32[]{:S(2)}, u32[]{:S(2)}) collective-permute-start(f16[80,512]{1,0:T(8,128)(2,1)S(1)} %convert_element_type.33), channel_id=1, source_target_pairs={{16,0},{20,4},{24,8},{28,12},{17,1},{21,5},{25,9},{29,13},{18,2},{... | collective-permute-start | bytes 245768 | tf_op jit(solution)/shard_map/ppermute | solution.py:399
  37.4 10.5 %all-to-all-start = ((f32[32,1,128]{2,1,0:T(1,128)}), f32[32,1,128]{2,1,0:T(1,128)S(1)}, u32[]{:S(2)}, u32[]{:S(2)}) async-start(f32[32,1,128]{2,1,0:T(1,128)} %get-tuple-element.45), calls=%async_computation | async-start | bytes 32768 | tf_op jit(solution)/shard_map/all_to_all | solution.py:517
  40.8 7.7 %collective-permute-start.11 = (f16[80,512]{1,0:T(8,128)(2,1)S(1)}, f16[80,512]{1,0:T(8,128)(2,1)S(1)}, u32[]{:S(2)}, u32[]{:S(2)}) collective-permute-start(f16[80,512]{1,0:T(8,128)(2,1)S(1)} %convert_element_type.35), channel_id=1, source_target_pairs={{0,4},{4,0},{8,12},{12,8},{16,20},{20,16},{24,28},{28,24},{1,5},{5... | collective-permute-start | bytes 245768 | tf_op jit(solution)/shard_map/ppermute | solution.py:399

commit v9 on v8

--- a/solution.py
+++ b/solution.py
@@ -292,7 +292,7 @@
 
 def combine_kernel(
     frames, sh_ref, keep_ref, sent_ref, got_ref, near_ref, far_ref,
-    late_ref, incl_ref, excl_ref, send_ref, info_ref,
+    late_ref, excl_ref, send_ref, info_ref, *incl_refs,
 ):
     tm = lax.axis_index("tm")
     y = tm % 2
@@ -314,7 +314,8 @@
     following = jnp.where(there, following, 0.0)
     excl_ref[...] = following
     both = early + weight * back(late, *first) + weight * weight * back(following, *total)
-    incl_ref[...] = both
+    for ref in incl_refs:
+        ref[...] = both
     for i in range(2):
         info_ref[i] = total[i] - first[i]
         info_ref[2 + i] = total[i]
@@ -322,6 +323,8 @@
     further = jnp.maximum(power_of(near_ref), power_of(far_ref))
     power = jnp.where(there, jnp.maximum(power, further), power)
     span = [total[i] + near_shift[i] + far_shift[i] for i in range(2)]
+    for i in range(2):
+        info_ref[4 + i] = near_shift[i] + far_shift[i]
     pack(send_ref, both, power + 2.0, *span)
 
 
@@ -350,8 +353,11 @@
 ):
     y = lax.axis_index("tm") % 2
     got, power = from_pairs(reach, sent_ref, got_ref)
-    span = shift_of(sent_ref)
-    apart = [span[i] - info_ref[2 + i] for i in range(2)]
+    if reach == 2:
+        apart = [info_ref[4 + i] for i in range(2)]
+    else:
+        span = shift_of(sent_ref)
+        apart = [span[i] - info_ref[2 + i] for i in range(2)]
     late = excl_ref[...] + decay_rate ** (2 * frames * (reach - 1)) * back(got, *apart)
     early = late_ref[...] + decay_rate**frames * back(late, info_ref[0], info_ref[1])
     keep = jnp.where(y == 0, early, late)
@@ -489,10 +495,12 @@
     near = permute_16(send_keep, lambda s: s - 2)
     far = permute_16(send, lambda s: (s - 2) ^ 1)
     got = permute_16(send, lambda s: s ^ 1)
-    late, both, excl, send, info = kernel_call(
+    more = int(pairs > 4)
+    late, excl, send, info, *both = kernel_call(
         functools.partial(combine_kernel, frames), 6,
-        (half_field, half_field, half_field, message, jax.ShapeDtypeStruct((4,), jnp.int32)),
-        [smem] + [vmem] * 5, (vmem, vmem, vmem, vmem, smem),
+        [half_field, half_field, message, jax.ShapeDtypeStruct((6,), jnp.int32)]
+        + [half_field] * more,
+        [smem] + [vmem] * 5, [vmem, vmem, vmem, smem] + [vmem] * more,
     )(own, keep, send, got, near, far)
     products = jax.ShapeDtypeStruct((2, part, width), jnp.float32)
     own_z, other_z, wind_local = kernel_call(
@@ -502,10 +510,10 @@
     reach = 2
     while 2 * reach < pairs:
         got = permute_16(send, lambda s, r=reach: s - 2 * r)
-        both, excl, send = kernel_call(
+        *both, excl, send = kernel_call(
             functools.partial(step_kernel, frames, reach), 6,
             (half_field, half_field, message), [smem] + [vmem] * 4, (vmem, vmem, vmem),
-        )(info, both, excl, send, got)
+        )(info, *both, excl, send, got)
         reach *= 2
     got = permute_16(send, lambda s: s - 2 * reach)
     n_all = n_tm * n_rows

time: 50.4 us -> 50 us (level)
  transfers between devices with their start and end apart: 13 -> 13, of which waited for: 7 -> 7; matrix products, arithmetic and copies ran while one was open for 1% -> 1% of each run, Pallas kernels for 8% -> 7%
where the time goes in v9:
time: 50 us; the launch traced here: 49.8 us
  waiting for transfers between devices  22.4 us (45%)
  starting transfers between devices  14.9 us (30%)
  Pallas kernels  10.9 us (22%)
  between operations  0.81 us (2%)
  other arithmetic  0.68 us (1%)
    ppermute x5, waiting for transfers between devices, permute_16(): lax.ppermute(value.astype(jnp.float16), 'tm', route).astype(jnp.float32)  9.79 us
    ppermute x5, starting transfers between devices, permute_16(): lax.ppermute(value.astype(jnp.float16), 'tm', route).astype(jnp.float32)  7.55 us
    ppermute x7, waiting for transfers between devices, swap(): return lax.ppermute(value, axis, [(s, s ^ bit) for s in range(count)])  7.32 us
    all_to_all x1, waiting for transfers between devices, on_device(): winds = lax.all_to_all(wind, ('tm', 'rows'), 0, 0)  5.25 us
    ppermute x7, starting transfers between devices, swap(): return lax.ppermute(value, axis, [(s, s ^ bit) for s in range(count)])  3.95 us
    all_to_all x1, starting transfers between devices, on_device(): winds = lax.all_to_all(wind, ('tm', 'rows'), 0, 0)  3.41 us
    pallas_call x1, Pallas kernels, on_device(): kernel_call(z_kernel, 12, (products, products, pair), [smem] + [vmem] * 6...  2.22 us
    pallas_call x1, Pallas kernels, on_device(): pl.pallas_call(functools.partial(y_kernel, reach_rows), out_shape=[jax.Sh...  1.74 us
  transfers between devices with their start and end apart: 13, of which 7 were waited for; matrix products, arithmetic and copies ran while one was open for 1% of the time, Pallas kernels for 7%

profile of v9, /device:TPU:0, one launch (start us, length us, event | category | flops | bytes accessed | tf_op | source)
XLA Modules:
  0.0 49.8 jit_solution(13156603202685534937)
XLA Ops:
  0.6 0.0 copy-start
  0.6 0.0 copy-start.2
  0.6 1.7 %transform.1 = (bf16[288,256]{1,0:T(8,128)(2,1)S(1)}, bf16[528,512]{1,0:T(8,128)(2,1)S(1)}, bf16[512,512]{1,0:T(8,128)(2,1)S(1)}, bf16[512,512]{1,0:T(8,128)(2,1...) custom-call(bf16[2,128,512]{2,1,0:T(8,128)(2,1)} %phases_ref.1, s32[128,512]{1,0:T(8,128)} %refs_8_.1, ...), custom_call_target="tpu_custom_call" | custom-call | tf_op jit(solution)/shard_map/transform/pallas_call | solution.py:445
  2.4 0.0 copy-start.3
  2.4 3.0 %collective-permute-start.1 = (bf16[288,256]{1,0:T(8,128)(2,1)S(1)}, bf16[288,256]{1,0:T(8,128)(2,1)S(1)}, u32[]{:S(2)}, u32[]{:S(2)}) collective-permute-start(bf16[288,256]{1,0:T(8,128)(2,1)S(1)} %get-tuple-element.24.refs_0_), channel_id=1, source_target_pairs={{0,2},{1,3},{2,0},{3,1},{4,6},{5,7},{6,4},{7,5},{8,10},{9,11},{10,... | collective-permute-start | bytes 442376 | tf_op jit(solution)/shard_map/ppermute | solution.py:388
  5.4 0.0 copy-done.2
  5.4 0.1 collective-permute-start.4
  5.5 0.0 collective-permute-start
  5.5 4.6 %collective-permute-done.1.refs_2_ = bf16[288,256]{1,0:T(8,128)(2,1)S(1)} collective-permute-done((bf16[288,256]{1,0:T(8,128)(2,1)S(1)}, bf16[288,256]{1,0:T(8,128)(2,1)S(1)}, u32[]{:S(2)}, u32[]{:S(2)}) %collective-permute-start.1) | collective-permute-done | bytes 147488 | tf_op jit(solution)/shard_map/ppermute | solution.py:388
  10.1 0.0 collective-permute-start.2
  10.1 0.5 %collective-permute-start.3 = (bf16[2,2,64,256]{3,2,1,0:T(8,128)(2,1)S(1)}, bf16[2,2,64,256]{3,2,1,0:T(8,128)(2,1)S(1)}, u32[]{:S(2)}, u32[]{:S(2)}) collective-permute-start(bf16[2,2,64,256]{3,2,1,0:T(8,128)(2,1)S(1)} %copy-done.2), channel_id=1, source_target_pairs={{0,1},{1,0},{2,3},{3,2},{4,5},{5,4},{6,7},{7,6},{8,9},{9,8},{10,11... | collective-permute-start | bytes 393224 | tf_op jit(solution)/shard_map/ppermute | solution.py:388
  10.6 1.4 %collective-permute-done.4.refs_6_ = bf16[2,2,64,256]{3,2,1,0:T(8,128)(2,1)S(1)} collective-permute-done((bf16[2,2,64,256]{3,2,1,0:T(8,128)(2,1)S(1)}, bf16[2,2,64,256]{3,2,1,0:T(8,128)(2,1)S(1)}, u32[]{:S(2)}, u32[]{:S(2)}) %collective-permute-start.4) | collective-permute-done | bytes 131104 | tf_op jit(solution)/shard_map/ppermute | solution.py:388
  12.1 0.0 collective-permute-start.5
  12.1 0.0 copy-done.3
  12.1 0.1 reshape.7.sh_ref
  12.2 0.0 collective-permute-done.3.refs_5_
  12.2 0.0 collective-permute-done.refs_1_
  12.2 1.3 %collective-permute-done.5.refs_7_ = bf16[2,2,64,256]{3,2,1,0:T(8,128)(2,1)S(1)} collective-permute-done((bf16[2,2,64,256]{3,2,1,0:T(8,128)(2,1)S(1)}, bf16[2,2,64,256]{3,2,1,0:T(8,128)(2,1)S(1)}, u32[]{:S(2)}, u32[]{:S(2)}) %collective-permute-start.5) | collective-permute-done | bytes 131104 | tf_op jit(solution)/shard_map/ppermute | solution.py:388
  13.4 0.0 collective-permute-done.2.refs_3_
  13.4 0.0 copy-done
  13.4 1.5 %grad.1 = (f32[2,144,512]{2,1,0:T(8,128)S(1)}, f32[8,512]{1,0:T(8,128)S(1)}) custom-call(bf16[288,256]{1,0:T(8,128)(2,1)S(1)} %get-tuple-element.24.refs_0_, bf16[288,256]{1,0:T(8,128)(2,1)S(1)} %collective-permute-done.refs_1_, bf16[288,256]{1,0:T(8,128)(2,1)S(1)} %collective-permute-done.1.refs_2_, bf16[288,256]{1,0:T(8,128)(2,1)S(1)} %collective-permute-done.2.refs_3_, ...), custom_call_target="tpu_custom_call" | custom-call | tf_op jit(solution)/shard_map/grad/pallas_call | solution.py:470
  15.0 0.9 %shard_map.104 = (f32[2,128,512]{2,1,0:T(8,128)S(1)}, f32[72,512]{1,0:T(8,128)S(1)}, f32[80,512]{1,0:T(8,128)S(1)}, f32[80,512]{1,0:T(8,128)S(1)}) custom-call(s32[4]{0:T(128)S(1)} %reshape.7.sh_ref, f32[2,144,512]{2,1,0:T(8,128)S(1)} %get-tuple-element.29.g_ref, f32[8,512]{1,0:T(8,128)S(1)} %get-tuple-element.30.next_ref), custom_call_target="tpu_custom_call" | custom-call | tf_op jit(solution)/shard_map/pallas_call | solution.py:491
  15.9 1.8 %collective-permute-start.6 = (f16[80,512]{1,0:T(8,128)(2,1)S(1)}, f16[80,512]{1,0:T(8,128)(2,1)S(1)}, u32[]{:S(2)}, u32[]{:S(2)}) collective-permute-start(f16[80,512]{1,0:T(8,128)(2,1)S(1)} %convert_element_type.28), channel_id=1, source_target_pairs={{0,4},{4,0},{8,12},{12,8},{16,20},{20,16},{24,28},{28,24},{1,5},{5... | collective-permute-start | bytes 245768 | tf_op jit(solution)/shard_map/ppermute | solution.py:405
  17.8 1.3 %collective-permute-start.7 = (f16[80,512]{1,0:T(8,128)(2,1)S(1)}, f16[80,512]{1,0:T(8,128)(2,1)S(1)}, u32[]{:S(2)}, u32[]{:S(2)}) collective-permute-start(f16[80,512]{1,0:T(8,128)(2,1)S(1)} %convert_element_type.30), channel_id=1, source_target_pairs={{8,0},{12,4},{16,8},{20,12},{24,16},{28,20},{9,1},{13,5},{17,9},{2... | collective-permute-start | bytes 245768 | tf_op jit(solution)/shard_map/ppermute | solution.py:405
  19.1 1.3 %collective-permute-start.8 = (f16[80,512]{1,0:T(8,128)(2,1)S(1)}, f16[80,512]{1,0:T(8,128)(2,1)S(1)}, u32[]{:S(2)}, u32[]{:S(2)}) collective-permute-start(f16[80,512]{1,0:T(8,128)(2,1)S(1)} %convert_element_type.28), channel_id=1, source_target_pairs={{8,4},{12,0},{16,12},{20,8},{24,20},{28,16},{9,5},{13,1},{17,13},{... | collective-permute-start | bytes 245768 | tf_op jit(solution)/shard_map/ppermute | solution.py:405
  20.4 0.3 collective-permute-start.9
  20.7 0.0 collective-permute-done.6
  20.7 3.4 %collective-permute-done.7 = f16[80,512]{1,0:T(8,128)(2,1)S(1)} collective-permute-done((f16[80,512]{1,0:T(8,128)(2,1)S(1)}, f16[80,512]{1,0:T(8,128)(2,1)S(1)}, u32[]{:S(2)}, u32[]{:S(2)}) %collective-permute-start.7) | collective-permute-done | bytes 81952 | tf_op jit(solution)/shard_map/ppermute | solution.py:405
  24.2 2.1 %collective-permute-done.8 = f16[80,512]{1,0:T(8,128)(2,1)S(1)} collective-permute-done((f16[80,512]{1,0:T(8,128)(2,1)S(1)}, f16[80,512]{1,0:T(8,128)(2,1)S(1)}, u32[]{:S(2)}, u32[]{:S(2)}) %collective-permute-start.8) | collective-permute-done | bytes 81952 | tf_op jit(solution)/shard_map/ppermute | solution.py:405
  26.3 0.0 copy-start.1
  26.3 1.3 %shard_map.105 = (f32[72,512]{1,0:T(8,128)S(1)}, f32[72,512]{1,0:T(8,128)S(1)}, f32[80,512]{1,0:T(8,128)S(1)}, s32[6]{0:T(128)S(1)}) custom-call(s32[4]{0:T(128)S(1)} %reshape.7.sh_ref, f32[72,512]{1,0:T(8,128)S(1)} %get-tuple-element.31.keep_ref, f32[80,512]{1,0:T(8,128)S(1)} %get-tuple-element.32.sent_ref, f32[80,512]{1,0:T(8,128)S(1)} %convert_element_type.29.got_ref, ...), custom_call_target="tpu_custom_call" | custom-call | tf_op jit(solution)/shard_map/pallas_call | solution.py:499
  27.6 1.3 %collective-permute-start.10 = (f16[80,512]{1,0:T(8,128)(2,1)S(1)}, f16[80,512]{1,0:T(8,128)(2,1)S(1)}, u32[]{:S(2)}, u32[]{:S(2)}) collective-permute-start(f16[80,512]{1,0:T(8,128)(2,1)S(1)} %convert_element_type.33), channel_id=1, source_target_pairs={{16,0},{20,4},{24,8},{28,12},{17,1},{21,5},{25,9},{29,13},{18,2},{... | collective-permute-start | bytes 245768 | tf_op jit(solution)/shard_map/ppermute | solution.py:405
  28.9 0.0 collective-permute-done.9.side_ref
  29.0 0.0 copy-done.1
  29.0 2.2 %shard_map.106 = (f32[2,72,512]{2,1,0:T(8,128)S(1)}, f32[2,72,512]{2,1,0:T(8,128)S(1)}, f32[2]{0:T(128)S(1)}) custom-call(s32[4]{0:T(128)S(1)} %reshape.7.sh_ref, bf16[2,128,512]{2,1,0:T(8,128)(2,1)S(1)} %copy-done.1, bf16[2,72,512]{2,1,0:T(8,128)(2,1)S(1)} %collective-permute-done.9.side_ref, f32[8,512]{1,0:T(8,128)S(1)} %get-tuple-element.30.next_ref, ...), custom_call_target="tpu_custom_call" | custom-call | tf_op jit(solution)/shard_map/pallas_call | solution.py:506
  31.2 4.2 %collective-permute-done.10 = f16[80,512]{1,0:T(8,128)(2,1)S(1)} collective-permute-done((f16[80,512]{1,0:T(8,128)(2,1)S(1)}, f16[80,512]{1,0:T(8,128)(2,1)S(1)}, u32[]{:S(2)}, u32[]{:S(2)}) %collective-permute-start.10) | collective-permute-done | bytes 81952 | tf_op jit(solution)/shard_map/ppermute | solution.py:405
  35.4 1.6 %shard_map.107 = (f32[72,512]{1,0:T(8,128)S(1)}, f32[80,512]{1,0:T(8,128)S(1)}, f32[32,1,128]{2,1,0:T(1,128)}) custom-call(s32[6]{0:T(128)S(1)} %get-tuple-element.34.info_ref, f32[2]{0:T(128)S(1)} %get-tuple-element.37.wind_in, f32[72,512]{1,0:T(8,128)S(1)} %get-tuple-element.38.late_ref, f32[72,512]{1,0:T(8,128)S(1)} %get-tuple-element.39.excl_ref, ...), custom_call_target="tpu_custom_call" | custom-call | tf_op jit(solution)/shard_map/pallas_call | solution.py:520
  37.0 3.4 %all-to-all-start = ((f32[32,1,128]{2,1,0:T(1,128)}), f32[32,1,128]{2,1,0:T(1,128)S(1)}, u32[]{:S(2)}, u32[]{:S(2)}) async-start(f32[32,1,128]{2,1,0:T(1,128)} %get-tuple-element.45), calls=%async_computation | async-start | bytes 32768 | tf_op jit(solution)/shard_map/all_to_all | solution.py:525
  40.5 1.8 %collective-permute-start.11 = (f16[80,512]{1,0:T(8,128)(2,1)S(1)}, f16[80,512]{1,0:T(8,128)(2,1)S(1)}, u32[]{:S(2)}, u32[]{:S(2)}) collective-permute-start(f16[80,512]{1,0:T(8,128)(2,1)S(1)} %convert_element_type.35), channel_id=1, source_target_pairs={{0,4},{4,0},{8,12},{12,8},{16,20},{20,16},{24,28},{28,24},{1,5},{5... | collective-permute-start | bytes 245768 | tf_op jit(solution)/shard_map/ppermute | solution.py:405
  42.3 5.2 %all-to-all-done = f32[32,1,128]{2,1,0:T(1,128)S(1)} async-done(((f32[32,1,128]{2,1,0:T(1,128)}), f32[32,1,128]{2,1,0:T(1,128)S(1)}, u32[]{:S(2)}, u32[]{:S(2)}) %all-to-all-start) | async-done | bytes 16416 | tf_op jit(solution)/shard_map/all_to_all | solution.py:525
  47.6 0.1 slice_reduce_fusion
  47.6 0.5 %negate_multiply_fusion = f32[2]{0:T(128)} fusion(f32[2]{0:T(128)S(1)} %slice_reduce_fusion), kind=kLoop, calls=%fused_computation.1 | loop fusion | flops 4 | bytes 16 | tf_op jit(solution)/shard_map/div | solution.py:531
  48.1 0.0 collective-permute-done.11
  48.1 1.6 %shard_map.108 = f32[2,128,512]{2,1,0:T(8,128)} custom-call(s32[4]{0:T(128)S(1)} %reshape.7.sh_ref, f32[72,512]{1,0:T(8,128)S(1)} %get-tuple-element.43.keep_ref, f32[80,512]{1,0:T(8,128)S(1)} %convert_element_type.36.got_ref, f32[2,128,512]{2,1,0:T(8,128)S(1)} %get-tuple-element.36.loc_ref), custom_call_target="tpu_custom_call" | custom-call | bytes 1572864 | tf_op jit(solution)/shard_map/pallas_call | solution.py:527
  (9 shorter events, 0.1 us)
Async XLA Ops:
  0.6 12.8 %copy-start = (s32[128,512]{1,0:T(8,128)S(1)}, s32[128,512]{1,0:T(8,128)}, u32[]{:S(2)}) copy-start(s32[128,512]{1,0:T(8,128)} %refs_8_.1) | copy-start | bytes 786436
  0.6 4.8 %copy-start.2 = (bf16[2,2,64,256]{3,2,1,0:T(8,128)(2,1)S(1)}, bf16[2,2,64,256]{3,2,1,0:T(8,128)(2,1)}, u32[]{:S(2)}) copy-start(bf16[2,2,64,256]{3,2,1,0:T(8,128)(2,1)} %refs_4_.1) | copy-start | bytes 393220
  2.4 9.7 %copy-start.3 = (s32[2,2]{1,0:T(2,128)S(1)}, s32[2,2]{1,0:T(2,128)}, u32[]{:S(2)}) copy-start(s32[2,2]{1,0:T(2,128)} %param.11) | copy-start | bytes 52
  2.4 7.7 %collective-permute-start.1 = (bf16[288,256]{1,0:T(8,128)(2,1)S(1)}, bf16[288,256]{1,0:T(8,128)(2,1)S(1)}, u32[]{:S(2)}, u32[]{:S(2)}) collective-permute-start(bf16[288,256]{1,0:T(8,128)(2,1)S(1)} %get-tuple-element.24.refs_0_), channel_id=1, source_target_pairs={{0,2},{1,3},{2,0},{3,1},{4,6},{5,7},{6,4},{7,5},{8,10},{9,11},{10,... | collective-permute-start | bytes 442376 | tf_op jit(solution)/shard_map/ppermute | solution.py:388
  5.4 6.7 %collective-permute-start.4 = (bf16[2,2,64,256]{3,2,1,0:T(8,128)(2,1)S(1)}, bf16[2,2,64,256]{3,2,1,0:T(8,128)(2,1)S(1)}, u32[]{:S(2)}, u32[]{:S(2)}) collective-permute-start(bf16[2,2,64,256]{3,2,1,0:T(8,128)(2,1)S(1)} %copy-done.2), channel_id=1, source_target_pairs={{0,2},{1,3},{2,0},{3,1},{4,6},{5,7},{6,4},{7,5},{8,10},{9,11},{10,... | collective-permute-start | bytes 393224 | tf_op jit(solution)/shard_map/ppermute | solution.py:388
  5.5 6.7 %collective-permute-start = (bf16[288,256]{1,0:T(8,128)(2,1)S(1)}, bf16[288,256]{1,0:T(8,128)(2,1)S(1)}, u32[]{:S(2)}, u32[]{:S(2)}) collective-permute-start(bf16[288,256]{1,0:T(8,128)(2,1)S(1)} %get-tuple-element.24.refs_0_), channel_id=1, source_target_pairs={{0,1},{1,0},{2,3},{3,2},{4,5},{5,4},{6,7},{7,6},{8,9},{9,8},{10,11... | collective-permute-start | bytes 442376 | tf_op jit(solution)/shard_map/ppermute | solution.py:388
  10.1 3.3 %collective-permute-start.2 = (bf16[288,256]{1,0:T(8,128)(2,1)S(1)}, bf16[288,256]{1,0:T(8,128)(2,1)S(1)}, u32[]{:S(2)}, u32[]{:S(2)}) collective-permute-start(bf16[288,256]{1,0:T(8,128)(2,1)S(1)} %collective-permute-done.1.refs_2_), channel_id=1, source_target_pairs={{0,1},{1,0},{2,3},{3,2},{4,5},{5,4},{6,7},{7,6},{8,9},{9,8},{10,11... | collective-permute-start | bytes 442376 | tf_op jit(solution)/shard_map/ppermute | solution.py:388
  10.1 2.0 %collective-permute-start.3 = (bf16[2,2,64,256]{3,2,1,0:T(8,128)(2,1)S(1)}, bf16[2,2,64,256]{3,2,1,0:T(8,128)(2,1)S(1)}, u32[]{:S(2)}, u32[]{:S(2)}) collective-permute-start(bf16[2,2,64,256]{3,2,1,0:T(8,128)(2,1)S(1)} %copy-done.2), channel_id=1, source_target_pairs={{0,1},{1,0},{2,3},{3,2},{4,5},{5,4},{6,7},{7,6},{8,9},{9,8},{10,11... | collective-permute-start | bytes 393224 | tf_op jit(solution)/shard_map/ppermute | solution.py:388
  12.1 1.3 %collective-permute-start.5 = (bf16[2,2,64,256]{3,2,1,0:T(8,128)(2,1)S(1)}, bf16[2,2,64,256]{3,2,1,0:T(8,128)(2,1)S(1)}, u32[]{:S(2)}, u32[]{:S(2)}) collective-permute-start(bf16[2,2,64,256]{3,2,1,0:T(8,128)(2,1)S(1)} %collective-permute-done.4.refs_6_), channel_id=1, source_target_pairs={{0,1},{1,0},{2,3},{3,2},{4,5},{5,4},{6,7},{7,6},{8,9},{9,8},{10,11... | collective-permute-start | bytes 393224 | tf_op jit(solution)/shard_map/ppermute | solution.py:388
  15.9 4.8 %collective-permute-start.6 = (f16[80,512]{1,0:T(8,128)(2,1)S(1)}, f16[80,512]{1,0:T(8,128)(2,1)S(1)}, u32[]{:S(2)}, u32[]{:S(2)}) collective-permute-start(f16[80,512]{1,0:T(8,128)(2,1)S(1)} %convert_element_type.28), channel_id=1, source_target_pairs={{0,4},{4,0},{8,12},{12,8},{16,20},{20,16},{24,28},{28,24},{1,5},{5... | collective-permute-start | bytes 245768 | tf_op jit(solution)/shard_map/ppermute | solution.py:405
  17.8 6.4 %collective-permute-start.7 = (f16[80,512]{1,0:T(8,128)(2,1)S(1)}, f16[80,512]{1,0:T(8,128)(2,1)S(1)}, u32[]{:S(2)}, u32[]{:S(2)}) collective-permute-start(f16[80,512]{1,0:T(8,128)(2,1)S(1)} %convert_element_type.30), channel_id=1, source_target_pairs={{8,0},{12,4},{16,8},{20,12},{24,16},{28,20},{9,1},{13,5},{17,9},{2... | collective-permute-start | bytes 245768 | tf_op jit(solution)/shard_map/ppermute | solution.py:405
  19.1 7.2 %collective-permute-start.8 = (f16[80,512]{1,0:T(8,128)(2,1)S(1)}, f16[80,512]{1,0:T(8,128)(2,1)S(1)}, u32[]{:S(2)}, u32[]{:S(2)}) collective-permute-start(f16[80,512]{1,0:T(8,128)(2,1)S(1)} %convert_element_type.28), channel_id=1, source_target_pairs={{8,4},{12,0},{16,12},{20,8},{24,20},{28,16},{9,5},{13,1},{17,13},{... | collective-permute-start | bytes 245768 | tf_op jit(solution)/shard_map/ppermute | solution.py:405
  20.4 8.6 %collective-permute-start.9 = (bf16[2,72,512]{2,1,0:T(8,128)(2,1)S(1)}, bf16[2,72,512]{2,1,0:T(8,128)(2,1)S(1)}, u32[]{:S(2)}, u32[]{:S(2)}) collective-permute-start(bf16[2,72,512]{2,1,0:T(8,128)(2,1)S(1)} %get-tuple-element.35), channel_id=1, source_target_pairs={{0,4},{4,0},{8,12},{12,8},{16,20},{20,16},{24,28},{28,24},{1,5},{5... | collective-permute-start | bytes 442376 | tf_op jit(solution)/shard_map/ppermute | solution.py:388
  26.3 2.6 %copy-start.1 = (bf16[2,128,512]{2,1,0:T(8,128)(2,1)S(1)}, bf16[2,128,512]{2,1,0:T(8,128)(2,1)}, u32[]{:S(2)}) copy-start(bf16[2,128,512]{2,1,0:T(8,128)(2,1)} %phases_ref.1) | copy-start | bytes 786436
  27.6 7.8 %collective-permute-start.10 = (f16[80,512]{1,0:T(8,128)(2,1)S(1)}, f16[80,512]{1,0:T(8,128)(2,1)S(1)}, u32[]{:S(2)}, u32[]{:S(2)}) collective-permute-start(f16[80,512]{1,0:T(8,128)(2,1)S(1)} %convert_element_type.33), channel_id=1, source_target_pairs={{16,0},{20,4},{24,8},{28,12},{17,1},{21,5},{25,9},{29,13},{18,2},{... | collective-permute-start | bytes 245768 | tf_op jit(solution)/shard_map/ppermute | solution.py:405
  37.0 10.5 %all-to-all-start = ((f32[32,1,128]{2,1,0:T(1,128)}), f32[32,1,128]{2,1,0:T(1,128)S(1)}, u32[]{:S(2)}, u32[]{:S(2)}) async-start(f32[32,1,128]{2,1,0:T(1,128)} %get-tuple-element.45), calls=%async_computation | async-start | bytes 32768 | tf_op jit(solution)/shard_map/all_to_all | solution.py:525
  40.5 7.7 %collective-permute-start.11 = (f16[80,512]{1,0:T(8,128)(2,1)S(1)}, f16[80,512]{1,0:T(8,128)(2,1)S(1)}, u32[]{:S(2)}, u32[]{:S(2)}) collective-permute-start(f16[80,512]{1,0:T(8,128)(2,1)S(1)} %convert_element_type.35), channel_id=1, source_target_pairs={{0,4},{4,0},{8,12},{12,8},{16,20},{20,16},{24,28},{28,24},{1,5},{5... | collective-permute-start | bytes 245768 | tf_op jit(solution)/shard_map/ppermute | solution.py:405
